TPU v7x, 256 devices: a whole 4x4x8 slice. The times are simulated.
256 devices in a mesh: dp: 32 (over z, x_lo, core), chan: 8 (over y, x_hi).
Axes of the slice: x: 4 (x_hi: 2, x_lo: 2; x = x_hi * 2 + x_lo), y: 4, z: 8, core: 2. Of those that a mesh axis runs over, the one named last changes fastest.
Arguments:
- inputs: bfloat16 [32, 2048, 1152], P('dp', 'chan'), may hold values from -6 to 6
- weight: bfloat16 [2048, 9, 256], P('chan'), may hold values from -0.046875 to 0.046875
- cotangent: bfloat16 [32, 256, 1152], P('dp', 'chan'), may hold values from -6 to 6
Outputs:
- result: bfloat16 [32, 256, 1152], P('dp', 'chan')
- input_grad: bfloat16 [32, 2048, 1152], P('dp', 'chan')
- weight_grad: float32 [2048, 9, 256], P('chan')
All inputs are finite; a program needn't handle non-finite values.
Results may differ from a plain program's by a relative error of at most 0.001.
Values may be sent and summed in bfloat16 or wider, within the bound.
A program may use at most 64 MiB of HBM per device.

v0:
```python
import jax
import jax.numpy as jnp
from jax import lax
from jax.sharding import PartitionSpec as P

DILATION_RATE = 12
MAP_HEIGHT = 16
MAP_WIDTH = 72


def translated_input(receptive_field, row_shift, column_shift, reach):
    height, width = (receptive_field.shape[1], receptive_field.shape[2])
    bordered_input = jnp.pad(receptive_field, ((0, 0), (reach, reach), (reach, reach)))
    return bordered_input[
        :,
        reach + row_shift : reach + row_shift + height,
        reach + column_shift : reach + column_shift + width,
    ]


def on_device(inputs, weight, cotangent):
    input_channels_local = inputs.shape[1]
    cout_local = cotangent.shape[1]
    tap_locations = MAP_HEIGHT * MAP_WIDTH
    feature_map = inputs[0].reshape(input_channels_local, MAP_HEIGHT, MAP_WIDTH)
    tap_list = weight.shape[1]
    output_channels_total = weight.shape[2]
    tap_shifts = [
        (DILATION_RATE * (tap_index // 3 - 1), DILATION_RATE * (tap_index % 3 - 1))
        for tap_index in range(tap_list)
    ]
    displaced_input = [
        translated_input(feature_map, first_operand, second_operand, DILATION_RATE).reshape(
            input_channels_local, tap_locations
        )
        for first_operand, second_operand in tap_shifts
    ]
    contract_rows = (((0,), (0,)), ((), ()))
    total = jnp.zeros((cout_local * lax.axis_size("chan"), tap_locations), jnp.float32)
    for tap_index in range(tap_list):
        columns = weight[:, tap_index, :]
        total = total + lax.dot_general(
            columns, displaced_input[tap_index], contract_rows, preferred_element_type=jnp.float32
        )
    owned = lax.psum_scatter(total, "chan", scatter_dimension=0, tiled=True)
    result = owned.astype(jnp.bfloat16).reshape(1, cout_local, tap_locations)
    flat_grads = lax.all_gather(cotangent[0], "chan", axis=0, tiled=True)
    collected_input = flat_grads.reshape(output_channels_total, MAP_HEIGHT, MAP_WIDTH)
    back_sum = jnp.zeros((input_channels_local, tap_locations), jnp.float32)
    for tap_index in range(tap_list):
        row_shift, column_shift = tap_shifts[tap_index]
        displaced_gradient = translated_input(
            collected_input, -row_shift, -column_shift, DILATION_RATE
        ).reshape(output_channels_total, tap_locations)
        back_sum = back_sum + jnp.dot(
            weight[:, tap_index, :], displaced_gradient, preferred_element_type=jnp.float32
        )
    input_grad = back_sum.astype(jnp.bfloat16).reshape(1, input_channels_local, tap_locations)
    contract_cols = (((1,), (1,)), ((), ()))
    local_grad = jnp.stack(
        [
            lax.dot_general(
                displaced_input[tap_index],
                flat_grads,
                contract_cols,
                preferred_element_type=jnp.float32,
            )
            for tap_index in range(tap_list)
        ],
        axis=1,
    )
    summed_grad = lax.psum(local_grad, "dp")
    weight_grad = summed_grad / jnp.float32(lax.axis_size("dp"))
    return (result, input_grad, weight_grad)


def solution(mesh):
    placed = (P("dp", "chan", None), P("chan", None, None), P("dp", "chan", None))
    return jax.shard_map(
        on_device,
        mesh=mesh,
        in_specs=placed,
        out_specs=(P("dp", "chan", None), P("dp", "chan", None), P("chan", None, None)),
        check_vma=False,
    )
```

profile of v0, /device:TPU:1, one launch (start us, length us, event | category | flops | bytes accessed | tf_op | source)
XLA Modules:
  0.0 312.3 jit_solution(14533653808641432408)
XLA Ops:
  8.0 1.3 copy.16
  9.4 0.7 pad_slice_fusion.12
  13.2 0.7 copy-done.5
  13.9 1.5 fusion.3
  15.4 2.7 copy.24
  18.2 32.7 %all-gather = bf16[1,256,1152]{2,1,0:T(8,128)(2,1)S(1)} all-gather(bf16[1,32,1152]{2,1,0:T(8,128)(2,1)} %param.5), channel_id=2, replica_groups=mesh['dp'=32,'chan'=8] {'chan'}, dimensions={1}, use_global_device_ids=true | all-gather | bytes 663552 | tf_op jit(solution)/shard_map/all_gather | solution.py:47
  50.8 2.2 fusion.20
  53.0 1.1 fusion.19
  54.1 1.1 fusion.18
  55.2 1.1 fusion.17
  56.3 1.1 fusion.16
  57.4 1.1 fusion.15
  58.5 1.1 fusion.14
  59.6 1.1 fusion.13
  60.7 1.1 fusion.12
  62.0 0.7 pad_slice_fusion.4
  62.8 0.5 copy-done.8
  66.1 0.5 fusion.11
  66.6 1.1 copy.21
  67.7 30.3 %reduce-scatter.4.cloned.1.call-done = f32[32,1152]{1,0:T(8,128)} async-done(((f32[256,1152]{1,0:T(8,128)}), f32[32,1152]{1,0:T(8,128)}) %reduce-scatter.4.cloned.1.call-update) | async-done | bytes 147472
  97.9 1.1 copy.25
  99.0 0.8 copy.20
  99.8 201.7 %all-reduce.4.cloned.1.call-done = f32[256,9,256]{2,0,1:T(8,128)} async-done(((f32[256,9,256]{2,0,1:T(8,128)}), f32[256,9,256]{2,0,1:T(8,128)}) %all-reduce.4.cloned.1.call-update) | async-done | bytes 2359312 | tf_op jit(solution)/shard_map/psum | solution.py:72
  301.6 3.3 %broadcast_multiply_fusion = f32[256,9,256]{2,0,1:T(8,128)} fusion(f32[256,9,256]{2,0,1:T(8,128)} %all-reduce.4.cloned.1.call-done), kind=kLoop, calls=%fused_computation.44 | loop fusion | flops 589824 | bytes 4718592 | tf_op jit(solution)/shard_map/div | solution.py:73
  (37 shorter events, 6.1 us)
Async XLA Ops:
  8.0 89.9 %reduce-scatter.4.cloned.1.call-start = ((), (), s32[]{:S(2)}) async-start(), calls=%async_computation.2 | async-start | bytes 1327104
  9.3 1.3 copy-start.7
  10.1 1.8 copy-start.4
  10.1 2.1 copy-start.2
  10.1 2.4 copy-start
  12.8 1.1 copy-start.5
  18.1 283.5 %all-reduce.4.cloned.1.call-start = ((), (), s32[]{:S(2)}) async-start(), calls=%async_computation.1 | async-start | bytes 4718592 | tf_op jit(solution)/shard_map/psum | solution.py:72
  18.2 34.9 %copy-start.3 = (bf16[256,16,72]{0,2,1:T(8,128)(2,1)S(1)}, bf16[256,16,72]{0,2,1:T(8,128)(2,1)}, u32[]{:S(2)}) copy-start(bf16[256,16,72]{0,2,1:T(8,128)(2,1)} %copy-done.2) | copy-start | bytes 1769476
  50.8 3.3 %copy-start.1 = (bf16[256,16,72]{0,2,1:T(8,128)(2,1)S(1)}, bf16[256,16,72]{0,2,1:T(8,128)(2,1)}, u32[]{:S(2)}) copy-start(bf16[256,16,72]{0,2,1:T(8,128)(2,1)} %copy-done) | copy-start | bytes 1769476
  54.1 2.2 copy-start.6
  62.0 1.3 copy-start.8
Sparse Core Ops, SparseCore 0:
  18.2 79.6 reduce-scatter.3
Sparse Core Ops, SparseCore 1:
  61.9 239.7 all-reduce.3
where the time goes:
time: 313 us; the launch traced here: 312 us
  waiting for transfers between devices  232 us (74%)
  blocking collectives  32.7 us (10%)
  matrix products  18.1 us (6%)
  between operations  15.7 us (5%)
  local copies, waits for them, and re-layouts  10.5 us (3%)
  other arithmetic  3.27 us (1%)
    psum x1, waiting for transfers between devices, on_device(): summed_grad = lax.psum(local_grad, 'dp')  202 us
    all_gather x1, blocking collectives, on_device(): flat_grads = lax.all_gather(cotangent[0], 'chan', axis=0, tiled=True)  32.7 us
    unnamed x3, waiting for transfers between devices  30.3 us
    dot_general x9, matrix products, on_device(): lax.dot_general(displaced_input[tap_index], flat_grads, contract_cols, pr...  10.9 us
    unnamed x23, local copies, waits for them, and re-layouts  8.74 us
  transfers between devices with their start and end apart: 2, of which 2 were waited for; matrix products, arithmetic and copies ran while one was open for 6% of the time, Pallas kernels for 0%

commit v1 on v0

--- a/solution.py
+++ b/solution.py
@@ -1,6 +1,10 @@
+import functools
+
 import jax
 import jax.numpy as jnp
 from jax import lax
+from jax.experimental import pallas as pl
+from jax.experimental.pallas import tpu as pltpu
 from jax.sharding import PartitionSpec as P
 
 DILATION_RATE = 12
@@ -18,7 +22,138 @@
     ]
 
 
-def on_device(inputs, weight, cotangent):
+def _allreduce_kernel(axis_names, nz, a_ref, o_ref, rc, s1, rx, s2, rp, rm, ap, am,
+                      send_sems, recv_sems):
+    rows, cols = a_ref.shape
+    half = rows // 2
+    quarter = half // 2
+    chunk = quarter // nz
+    lanes = cols // 2
+    MESH = pl.DeviceIdType.MESH
+    dp = lax.axis_index("dp")
+    core = dp % 2
+    xl = (dp // 2) % 2
+    z = dp // 4
+    nd = 4 * nz
+    pc = dp + 1 - 2 * core
+    px = dp + 2 - 4 * xl
+    zr = (dp + 4) % nd
+    zl = (dp + nd - 4) % nd
+
+    def dev(p):
+        return tuple(p if n == "dp" else lax.axis_index(n) for n in axis_names)
+
+    barrier = pltpu.get_barrier_semaphore()
+    for peer in (pc, px, zr, zl):
+        pl.semaphore_signal(barrier, inc=1, device_id=dev(peer), device_id_type=MESH)
+    pl.semaphore_wait(barrier, 4)
+
+    sent = []
+    counter = [0]
+
+    def remote(src, dst, peer):
+        k = counter[0]
+        counter[0] += 1
+        c = pltpu.make_async_remote_copy(
+            src_ref=src, dst_ref=dst, send_sem=send_sems.at[k], recv_sem=recv_sems.at[k],
+            device_id=dev(peer), device_id_type=MESH)
+        c.start()
+        sent.append(c)
+        return c
+
+    mine_c = pl.multiple_of(core * half, 8)
+    other_c = pl.multiple_of((1 - core) * half, 8)
+    c = remote(a_ref.at[pl.ds(other_c, half)], rc, pc)
+    c.wait_recv()
+    s1[...] = a_ref[pl.ds(mine_c, half), :] + rc[...]
+
+    mine_x = pl.multiple_of(xl * quarter, 8)
+    other_x = pl.multiple_of((1 - xl) * quarter, 8)
+    c = remote(s1.at[pl.ds(other_x, quarter)], rx, px)
+    c.wait_recv()
+    s2[...] = s1[pl.ds(mine_x, quarter), :] + rx[...]
+
+    def rows_of(j):
+        return pl.ds(pl.multiple_of(j * chunk, 8), chunk)
+
+    lo = pl.ds(0, lanes)
+    hi = pl.ds(lanes, lanes)
+    for s in range(nz - 1):
+        jp = (z + 2 * nz - 1 - s) % nz
+        jm = (z + 1 + s) % nz
+        if s == 0:
+            src_p = s2.at[rows_of(jp), lo]
+            src_m = s2.at[rows_of(jm), hi]
+        else:
+            ap[s] = s2[rows_of(jp), lo] + rp[s - 1]
+            am[s] = s2[rows_of(jm), hi] + rm[s - 1]
+            src_p = ap.at[s]
+            src_m = am.at[s]
+        cp = remote(src_p, rp.at[s], zr)
+        cm = remote(src_m, rm.at[s], zl)
+        cp.wait_recv()
+        cm.wait_recv()
+
+    base = core * half + xl * quarter
+    own = pl.ds(pl.multiple_of(base + z * chunk, 8), chunk)
+    o_ref[own, lo] = s2[rows_of(z), lo] + rp[nz - 2]
+    o_ref[own, hi] = s2[rows_of(z), hi] + rm[nz - 2]
+
+    for s in range(nz - 1):
+        jp = (z + nz - s) % nz
+        jm = (z + s) % nz
+        rp_rows = pl.ds(pl.multiple_of(base + jp * chunk, 8), chunk)
+        rm_rows = pl.ds(pl.multiple_of(base + jm * chunk, 8), chunk)
+        cp = remote(o_ref.at[rp_rows, lo], o_ref.at[rp_rows, lo], zr)
+        cm = remote(o_ref.at[rm_rows, hi], o_ref.at[rm_rows, hi], zl)
+        cp.wait_recv()
+        cm.wait_recv()
+
+    q_rows = pl.ds(pl.multiple_of(base, 8), quarter)
+    c = remote(o_ref.at[q_rows], o_ref.at[q_rows], px)
+    c.wait_recv()
+
+    h_rows = pl.ds(pl.multiple_of(core * half, 8), half)
+    c = remote(o_ref.at[h_rows], o_ref.at[h_rows], pc)
+    c.wait_recv()
+
+    for c in sent:
+        c.wait_send()
+
+
+def dp_allreduce(a, axis_names):
+    rows, cols = a.shape
+    nz = lax.axis_size("dp") // 4
+    half = rows // 2
+    quarter = half // 2
+    chunk = quarter // nz
+    lanes = cols // 2
+    n_copies = 2 + 2 * (nz - 1) * 2 + 2
+    vmem = pltpu.VMEM
+    return pl.pallas_call(
+        functools.partial(_allreduce_kernel, axis_names, nz),
+        out_shape=jax.ShapeDtypeStruct((rows, cols), a.dtype),
+        in_specs=[pl.BlockSpec(memory_space=vmem)],
+        out_specs=pl.BlockSpec(memory_space=vmem),
+        scratch_shapes=[
+            vmem((half, cols), a.dtype),
+            vmem((half, cols), a.dtype),
+            vmem((quarter, cols), a.dtype),
+            vmem((quarter, cols), a.dtype),
+            vmem((nz - 1, chunk, lanes), a.dtype),
+            vmem((nz - 1, chunk, lanes), a.dtype),
+            vmem((nz - 1, chunk, lanes), a.dtype),
+            vmem((nz - 1, chunk, lanes), a.dtype),
+            pltpu.SemaphoreType.DMA((n_copies,)),
+            pltpu.SemaphoreType.DMA((n_copies,)),
+        ],
+        compiler_params=pltpu.CompilerParams(
+            collective_id=0, has_side_effects=True, vmem_limit_bytes=48 * 1024 * 1024
+        ),
+    )(a)
+
+
+def on_device(axis_names, inputs, weight, cotangent):
     input_channels_local = inputs.shape[1]
     cout_local = cotangent.shape[1]
     tap_locations = MAP_HEIGHT * MAP_WIDTH
@@ -35,6 +170,28 @@
         )
         for first_operand, second_operand in tap_shifts
     ]
+    flat_grads = lax.all_gather(cotangent[0], "chan", axis=0, tiled=True)
+    contract_cols = (((1,), (1,)), ((), ()))
+    local_grad = jnp.stack(
+        [
+            lax.dot_general(
+                displaced_input[tap_index],
+                flat_grads,
+                contract_cols,
+                preferred_element_type=jnp.float32,
+            )
+            for tap_index in range(tap_list)
+        ],
+        axis=0,
+    )
+    summed = dp_allreduce(
+        local_grad.reshape(tap_list * input_channels_local, output_channels_total), axis_names
+    )
+    summed_grad = jnp.transpose(
+        summed.reshape(tap_list, input_channels_local, output_channels_total), (1, 0, 2)
+    )
+    weight_grad = summed_grad / jnp.float32(lax.axis_size("dp"))
+
     contract_rows = (((0,), (0,)), ((), ()))
     total = jnp.zeros((cout_local * lax.axis_size("chan"), tap_locations), jnp.float32)
     for tap_index in range(tap_list):
@@ -44,7 +201,6 @@
         )
     owned = lax.psum_scatter(total, "chan", scatter_dimension=0, tiled=True)
     result = owned.astype(jnp.bfloat16).reshape(1, cout_local, tap_locations)
-    flat_grads = lax.all_gather(cotangent[0], "chan", axis=0, tiled=True)
     collected_input = flat_grads.reshape(output_channels_total, MAP_HEIGHT, MAP_WIDTH)
     back_sum = jnp.zeros((input_channels_local, tap_locations), jnp.float32)
     for tap_index in range(tap_list):
@@ -56,28 +212,13 @@
             weight[:, tap_index, :], displaced_gradient, preferred_element_type=jnp.float32
         )
     input_grad = back_sum.astype(jnp.bfloat16).reshape(1, input_channels_local, tap_locations)
-    contract_cols = (((1,), (1,)), ((), ()))
-    local_grad = jnp.stack(
-        [
-            lax.dot_general(
-                displaced_input[tap_index],
-                flat_grads,
-                contract_cols,
-                preferred_element_type=jnp.float32,
-            )
-            for tap_index in range(tap_list)
-        ],
-        axis=1,
-    )
-    summed_grad = lax.psum(local_grad, "dp")
-    weight_grad = summed_grad / jnp.float32(lax.axis_size("dp"))
     return (result, input_grad, weight_grad)
 
 
 def solution(mesh):
     placed = (P("dp", "chan", None), P("chan", None, None), P("dp", "chan", None))
     return jax.shard_map(
-        on_device,
+        functools.partial(on_device, tuple(mesh.axis_names)),
         mesh=mesh,
         in_specs=placed,
         out_specs=(P("dp", "chan", None), P("dp", "chan", None), P("chan", None, None)),

time: 313 us -> 162 us (0.52)
  waiting for transfers between devices: 232 us -> 0.02 us
  Pallas kernels: 0 us -> 89.2 us
  matrix products: 18.1 us -> 11.8 us
    psum x1 -> x0, waiting for transfers between devices: 202 us -> none  [on_device(): summed_grad = lax.psum(local_grad, 'dp')]
    pallas_call x0 -> x1, Pallas kernels: none -> 89.2 us  [dp_allreduce(): pl.pallas_call(functools.partial(_allreduce_kernel, axis_names, nz), out_...]
    unnamed x3 -> x2, waiting for transfers between devices: 30.3 us -> 0.02 us
    dot_general x9, matrix products: 10.9 us -> 4.56 us  [on_device(): lax.dot_general(displaced_input[tap_index], flat_grads, contract_cols, pr...]
    unnamed x23 -> x25, local copies, waits for them, and re-layouts: 8.74 us -> 9.02 us
  transfers between devices with their start and end apart: 2 -> 1, of which waited for: 2 -> 0; matrix products, arithmetic and copies ran while one was open for 6% -> 8% of each run, Pallas kernels for 0% -> 55%
where the time goes in v1:
time: 162 us; the launch traced here: 161 us
  Pallas kernels  89.2 us (55%)
  blocking collectives  32.5 us (20%)
  between operations  14.3 us (9%)
  matrix products  11.8 us (7%)
  local copies, waits for them, and re-layouts  11.6 us (7%)
    pallas_call x1, Pallas kernels, dp_allreduce(): pl.pallas_call(functools.partial(_allreduce_kernel, axis_names, nz), out_...  89.2 us
    all_gather x1, blocking collectives, on_device(): flat_grads = lax.all_gather(cotangent[0], 'chan', axis=0, tiled=True)  32.5 us
    unnamed x25, local copies, waits for them, and re-layouts  9.02 us
    dot_general x9, matrix products, on_device(): lax.dot_general(displaced_input[tap_index], flat_grads, contract_cols, pr...  4.56 us
    dot_general x9, matrix products, on_device(): lax.dot_general(columns, displaced_input[tap_index], contract_rows, prefe...  3.97 us
    dot_general x9, matrix products, on_device(): jnp.dot(weight[:, tap_index, :], displaced_gradient, preferred_element_ty...  3.29 us
  transfers between devices with their start and end apart: 1, of which 0 were waited for; matrix products, arithmetic and copies ran while one was open for 8% of the time, Pallas kernels for 55%

profile of v1, /device:TPU:1, one launch (start us, length us, event | category | flops | bytes accessed | tf_op | source)
XLA Modules:
  0.0 161.0 jit_solution(10140084583761694243)
XLA Ops:
  7.2 1.3 copy.16
  8.5 0.7 pad_slice_fusion.12
  9.3 0.5 copy-done.7
  12.3 0.7 copy-done.5
  13.1 1.5 fusion.3
  14.6 2.7 %copy.24 = f32[256,1152]{1,0:T(8,128)} copy(f32[256,1152]{0,1:T(8,128)} %fusion.3) | data formatting | bytes 2359296
  17.3 32.5 %all-gather = bf16[1,256,1152]{2,1,0:T(8,128)(2,1)S(1)} all-gather(bf16[1,32,1152]{2,1,0:T(8,128)(2,1)} %param.5), channel_id=2, replica_groups=mesh['dp'=32,'chan'=8] {'chan'}, dimensions={1}, use_global_device_ids=true | all-gather | bytes 663552 | tf_op jit(solution)/shard_map/all_gather | solution.py:173
  49.8 1.1 copy.18
  50.8 1.5 fusion.20
  52.4 0.4 fusion.19
  52.8 0.4 fusion.18
  53.2 0.4 fusion.17
  54.3 0.4 fusion.15
  54.6 0.4 fusion.14
  55.0 0.4 fusion.13
  55.4 0.4 fusion.12
  55.8 89.2 %shard_map.58 = f32[2304,256]{1,0:T(8,128)S(1)} custom-call(f32[2304,256]{1,0:T(8,128)S(1)} %bitcast.179), custom_call_target="tpu_custom_call" | custom-call | tf_op jit(solution)/shard_map/pallas_call | solution.py:133
  145.0 0.7 pad_slice_fusion.4
  145.7 0.5 copy-done.8
  149.1 0.5 fusion.11
  149.6 1.1 copy.21
  150.7 1.6 broadcast_multiply_fusion
  152.2 1.1 copy.25
  153.3 0.8 copy.20
  (37 shorter events, 6.0 us)
Async XLA Ops:
  7.2 145.0 %reduce-scatter.4.cloned.1.call-start = ((), (), s32[]{:S(2)}) async-start(), calls=%async_computation.1 | async-start | bytes 1327104
  8.5 1.3 copy-start.7
  9.3 1.8 %copy-start.4 = (bf16[256,16,72]{0,2,1:T(8,128)(2,1)}, bf16[256,16,72]{0,2,1:T(8,128)(2,1)S(1)}, u32[]{:S(2)}) copy-start(bf16[256,16,72]{0,2,1:T(8,128)(2,1)S(1)} %get-tuple-element.27) | copy-start | bytes 1769476
  9.3 2.1 %copy-start.2 = (bf16[256,16,72]{0,2,1:T(8,128)(2,1)}, bf16[256,16,72]{0,2,1:T(8,128)(2,1)S(1)}, u32[]{:S(2)}) copy-start(bf16[256,16,72]{0,2,1:T(8,128)(2,1)S(1)} %get-tuple-element.21) | copy-start | bytes 1769476
  9.3 2.4 %copy-start = (bf16[256,16,72]{0,2,1:T(8,128)(2,1)}, bf16[256,16,72]{0,2,1:T(8,128)(2,1)S(1)}, u32[]{:S(2)}) copy-start(bf16[256,16,72]{0,2,1:T(8,128)(2,1)S(1)} %get-tuple-element.22) | copy-start | bytes 1769476
  12.0 1.1 copy-start.5
  50.8 1.6 copy-start.3
  50.8 1.9 %copy-start.1 = (bf16[256,16,72]{0,2,1:T(8,128)(2,1)S(1)}, bf16[256,16,72]{0,2,1:T(8,128)(2,1)}, u32[]{:S(2)}) copy-start(bf16[256,16,72]{0,2,1:T(8,128)(2,1)} %copy-done) | copy-start | bytes 1769476
  52.8 1.1 copy-start.6
  55.8 89.2 %copy-start.9 = (bf16[1,256,1152]{1,2,0:T(8,128)(2,1)S(1)}, bf16[1,256,1152]{1,2,0:T(8,128)(2,1)}, u32[]{:S(2)}) copy-start(bf16[1,256,1152]{1,2,0:T(8,128)(2,1)} %copy.18) | copy-start | bytes 1769476
  145.0 1.3 copy-start.8
Sparse Core Ops, SparseCore 0:
  17.4 80.2 reduce-scatter.3

commit v2 on v1

--- a/solution.py
+++ b/solution.py
@@ -153,6 +153,53 @@
     )(a)
 
 
+def _allgather_kernel(axis_names, n, x_ref, o_ref, send_sems, recv_sems):
+    rows = x_ref.shape[0]
+    MESH = pl.DeviceIdType.MESH
+    me = lax.axis_index("chan")
+
+    def dev(p):
+        return tuple(p if a == "chan" else lax.axis_index(a) for a in axis_names)
+
+    barrier = pltpu.get_barrier_semaphore()
+    for k in range(1, n):
+        pl.semaphore_signal(barrier, inc=1, device_id=dev((me + k) % n), device_id_type=MESH)
+    pl.semaphore_wait(barrier, n - 1)
+
+    mine = pl.ds(pl.multiple_of(me * rows, 16), rows)
+    copies = []
+    for k in range(1, n):
+        peer = (me + k) % n
+        c = pltpu.make_async_remote_copy(
+            src_ref=x_ref, dst_ref=o_ref.at[mine], send_sem=send_sems.at[k],
+            recv_sem=recv_sems.at[k], device_id=dev(peer), device_id_type=MESH)
+        c.start()
+        copies.append(c)
+    o_ref[mine, :] = x_ref[...]
+    for k in range(1, n):
+        src = (me + n - k) % n
+        theirs = pl.ds(pl.multiple_of(src * rows, 16), rows)
+        pltpu.make_async_remote_copy(
+            src_ref=x_ref, dst_ref=o_ref.at[theirs], send_sem=send_sems.at[k],
+            recv_sem=recv_sems.at[k], device_id=dev(src), device_id_type=MESH).wait_recv()
+    for c in copies:
+        c.wait_send()
+
+
+def chan_allgather(x, axis_names):
+    rows, cols = x.shape
+    n = lax.axis_size("chan")
+    vmem = pltpu.VMEM
+    return pl.pallas_call(
+        functools.partial(_allgather_kernel, axis_names, n),
+        out_shape=jax.ShapeDtypeStruct((rows * n, cols), x.dtype),
+        in_specs=[pl.BlockSpec(memory_space=vmem)],
+        out_specs=pl.BlockSpec(memory_space=vmem),
+        scratch_shapes=[pltpu.SemaphoreType.DMA((n,)), pltpu.SemaphoreType.DMA((n,))],
+        compiler_params=pltpu.CompilerParams(collective_id=1, has_side_effects=True),
+    )(x)
+
+
 def on_device(axis_names, inputs, weight, cotangent):
     input_channels_local = inputs.shape[1]
     cout_local = cotangent.shape[1]
@@ -170,7 +217,7 @@
         )
         for first_operand, second_operand in tap_shifts
     ]
-    flat_grads = lax.all_gather(cotangent[0], "chan", axis=0, tiled=True)
+    flat_grads = chan_allgather(cotangent[0], axis_names)
     contract_cols = (((1,), (1,)), ((), ()))
     local_grad = jnp.stack(
         [

time: 162 us -> 146 us (0.901)
  blocking collectives: 32.5 us -> 0 us
  Pallas kernels: 89.2 us -> 105 us
    all_gather x1 -> x0, blocking collectives: 32.5 us -> none  [on_device(): flat_grads = lax.all_gather(cotangent[0], 'chan', axis=0, tiled=True)]
    pallas_call x0 -> x1, Pallas kernels: none -> 16.7 us  [chan_allgather(): pl.pallas_call(functools.partial(_allgather_kernel, axis_names, n), out_s...]
    pallas_call x0 -> x1, local copies, waits for them, and re-layouts: none -> 2.18 us  [chan_allgather(): pl.pallas_call(functools.partial(_allgather_kernel, axis_names, n), out_s...]
    unnamed x25 -> x27, local copies, waits for them, and re-layouts: 9.02 us -> 9.03 us
  transfers between devices with their start and end apart: 1 -> 1, of which waited for: 0 -> 0; matrix products, arithmetic and copies ran while one was open for 8% -> 9% of each run, Pallas kernels for 55% -> 72%
where the time goes in v2:
time: 146 us; the launch traced here: 145 us
  Pallas kernels  105 us (72%)
  between operations  14.3 us (10%)
  local copies, waits for them, and re-layouts  12.7 us (9%)
  matrix products  11.8 us (8%)
  other arithmetic  1.56 us (1%)
    pallas_call x1, Pallas kernels, dp_allreduce(): pl.pallas_call(functools.partial(_allreduce_kernel, axis_names, nz), out_...  88.2 us
    pallas_call x1, Pallas kernels, chan_allgather(): pl.pallas_call(functools.partial(_allgather_kernel, axis_names, n), out_s...  16.7 us
    unnamed x27, local copies, waits for them, and re-layouts  9.03 us
    dot_general x9, matrix products, on_device(): lax.dot_general(displaced_input[tap_index], flat_grads, contract_cols, pr...  4.56 us
    dot_general x9, matrix products, on_device(): lax.dot_general(columns, displaced_input[tap_index], contract_rows, prefe...  3.97 us
    dot_general x9, matrix products, on_device(): jnp.dot(weight[:, tap_index, :], displaced_gradient, preferred_element_ty...  3.29 us
  transfers between devices with their start and end apart: 1, of which 0 were waited for; matrix products, arithmetic and copies ran while one was open for 9% of the time, Pallas kernels for 72%

profile of v2, /device:TPU:1, one launch (start us, length us, event | category | flops | bytes accessed | tf_op | source)
XLA Modules:
  0.0 145.3 jit_solution(11577339813475355854)
XLA Ops:
  7.2 1.3 copy.16
  8.5 0.7 pad_slice_fusion.12
  9.3 0.5 copy-done.8
  12.3 0.7 copy-done.6
  13.1 1.5 %fusion.3 = f32[256,1152]{0,1:T(8,128)} fusion(f32[256,1152]{0,1:T(8,128)S(1)} %convolution_bitcast_fusion.4, f32[256,1152]{0,1:T(8,128)S(1)} %convolution_bitcast_fusion.5, f32[256,1152]{0,1:T(8,128)S(1)} %convolution_bitcast_fusion.6, f32[256,1152]{0,1:T(8,128)S(1)} %convolution_bitcast_fusion.7, f32[256,1152]{0,1:T(8,128)S(1)} %fusion.8, ...), kind=kOutput, calls=%fused_computation.27 | convolution fusion | flops 152469504 | bytes 7798784 | tf_op jit(solution)/shard_map/dot_general | solution.py:246
  14.6 2.7 %copy.24 = f32[256,1152]{1,0:T(8,128)} copy(f32[256,1152]{0,1:T(8,128)} %fusion.3) | data formatting | bytes 2359296
  17.3 16.7 %shard_map.58 = bf16[256,1152]{1,0:T(8,128)(2,1)} custom-call(bf16[32,1152]{1,0:T(8,128)(2,1)} %bitcast.198), custom_call_target="tpu_custom_call" | custom-call | tf_op jit(solution)/shard_map/pallas_call | solution.py:193
  34.0 2.2 %copy.18 = bf16[256,1152]{0,1:T(8,128)(2,1)} copy(bf16[256,1152]{1,0:T(8,128)(2,1)} %shard_map.58) | data formatting | bytes 1179648 | tf_op jit(solution)/shard_map/pallas_call | solution.py:193
  36.1 1.5 %fusion.20 = f32[9,256,256]{2,1,0:T(8,128)S(1)} fusion(bf16[256,1152]{0,1:T(8,128)(2,1)} %bitcast.185, bf16[256,1152]{1,0:T(8,128)(2,1)S(1)} %copy-done), kind=kOutput, calls=%fused_computation.62 | convolution fusion | flops 150994944 | bytes 1441792 | tf_op jit(solution)/shard_map/dot_general | solution.py:224
  37.7 0.4 fusion.19
  38.1 0.4 fusion.18
  38.5 0.4 fusion.17
  39.5 0.4 fusion.15
  39.9 0.4 fusion.14
  40.3 0.4 fusion.13
  40.7 0.4 fusion.12
  41.1 88.2 %shard_map.59 = f32[2304,256]{1,0:T(8,128)S(1)} custom-call(f32[2304,256]{1,0:T(8,128)S(1)} %bitcast.169), custom_call_target="tpu_custom_call" | custom-call | tf_op jit(solution)/shard_map/pallas_call | solution.py:133
  129.4 0.7 pad_slice_fusion.4
  130.1 0.5 copy-done.9
  133.5 0.5 fusion.11
  134.0 1.1 copy.21
  135.0 1.6 %broadcast_multiply_fusion = f32[2304,256]{1,0:T(8,128)} fusion(f32[2304,256]{1,0:T(8,128)S(1)} %shard_map.59), kind=kLoop, calls=%fused_computation.44 | loop fusion | flops 589824 | bytes 4718592 | tf_op jit(solution)/shard_map/div | solution.py:240
  136.6 1.1 copy.25
  137.7 0.8 copy.20
  (39 shorter events, 6.0 us)
Async XLA Ops:
  7.2 129.4 %reduce-scatter.4.cloned.1.call-start = ((), (), s32[]{:S(2)}) async-start(), calls=%async_computation.1 | async-start | bytes 1327104
  8.5 1.3 copy-start.8
  9.3 1.8 %copy-start.5 = (bf16[256,16,72]{0,2,1:T(8,128)(2,1)}, bf16[256,16,72]{0,2,1:T(8,128)(2,1)S(1)}, u32[]{:S(2)}) copy-start(bf16[256,16,72]{0,2,1:T(8,128)(2,1)S(1)} %get-tuple-element.27) | copy-start | bytes 1769476
  9.3 2.1 %copy-start.3 = (bf16[256,16,72]{0,2,1:T(8,128)(2,1)}, bf16[256,16,72]{0,2,1:T(8,128)(2,1)S(1)}, u32[]{:S(2)}) copy-start(bf16[256,16,72]{0,2,1:T(8,128)(2,1)S(1)} %get-tuple-element.21) | copy-start | bytes 1769476
  9.3 2.4 %copy-start.1 = (bf16[256,16,72]{0,2,1:T(8,128)(2,1)}, bf16[256,16,72]{0,2,1:T(8,128)(2,1)S(1)}, u32[]{:S(2)}) copy-start(bf16[256,16,72]{0,2,1:T(8,128)(2,1)S(1)} %get-tuple-element.22) | copy-start | bytes 1769476
  12.0 1.1 copy-start.6
  33.9 2.2 %copy-start = (bf16[256,1152]{1,0:T(8,128)(2,1)S(1)}, bf16[256,1152]{1,0:T(8,128)(2,1)}, u32[]{:S(2)}) copy-start(bf16[256,1152]{1,0:T(8,128)(2,1)} %shard_map.58) | copy-start | bytes 1769476
  36.1 1.6 %copy-start.4 = (bf16[256,16,72]{0,2,1:T(8,128)(2,1)S(1)}, bf16[256,16,72]{0,2,1:T(8,128)(2,1)}, u32[]{:S(2)}) copy-start(bf16[256,16,72]{0,2,1:T(8,128)(2,1)} %copy-done.3) | copy-start | bytes 1769476
  36.1 1.9 %copy-start.2 = (bf16[256,16,72]{0,2,1:T(8,128)(2,1)S(1)}, bf16[256,16,72]{0,2,1:T(8,128)(2,1)}, u32[]{:S(2)}) copy-start(bf16[256,16,72]{0,2,1:T(8,128)(2,1)} %copy-done.1) | copy-start | bytes 1769476
  38.1 1.1 copy-start.7
  41.1 88.3 %copy-start.10 = (bf16[256,1152]{0,1:T(8,128)(2,1)S(1)}, bf16[256,1152]{0,1:T(8,128)(2,1)}, u32[]{:S(2)}) copy-start(bf16[256,1152]{0,1:T(8,128)(2,1)} %copy.18) | copy-start | bytes 1769476
  129.4 1.3 copy-start.9
Sparse Core Ops, SparseCore 0:
  17.4 80.2 reduce-scatter.3

commit v3 on v2

--- a/solution.py
+++ b/solution.py
@@ -22,12 +22,11 @@
     ]
 
 
-def _allreduce_kernel(axis_names, nz, a_ref, o_ref, rc, s1, rx, s2, rp, rm, ap, am,
+def _allreduce_kernel(axis_names, nz, a_ref, o_ref, rc, s1, f1, rx, rp, rm, ap, am,
                       send_sems, recv_sems):
     rows, cols = a_ref.shape
     half = rows // 2
-    quarter = half // 2
-    chunk = quarter // nz
+    chunk = half // nz
     lanes = cols // 2
     MESH = pl.DeviceIdType.MESH
     dp = lax.axis_index("dp")
@@ -67,12 +66,6 @@
     c.wait_recv()
     s1[...] = a_ref[pl.ds(mine_c, half), :] + rc[...]
 
-    mine_x = pl.multiple_of(xl * quarter, 8)
-    other_x = pl.multiple_of((1 - xl) * quarter, 8)
-    c = remote(s1.at[pl.ds(other_x, quarter)], rx, px)
-    c.wait_recv()
-    s2[...] = s1[pl.ds(mine_x, quarter), :] + rx[...]
-
     def rows_of(j):
         return pl.ds(pl.multiple_of(j * chunk, 8), chunk)
 
@@ -82,37 +75,42 @@
         jp = (z + 2 * nz - 1 - s) % nz
         jm = (z + 1 + s) % nz
         if s == 0:
-            src_p = s2.at[rows_of(jp), lo]
-            src_m = s2.at[rows_of(jm), hi]
+            src_p = s1.at[rows_of(jp), lo]
+            src_m = s1.at[rows_of(jm), hi]
         else:
-            ap[s] = s2[rows_of(jp), lo] + rp[s - 1]
-            am[s] = s2[rows_of(jm), hi] + rm[s - 1]
+            ap[s] = s1[rows_of(jp), lo] + rp[s - 1]
+            am[s] = s1[rows_of(jm), hi] + rm[s - 1]
             src_p = ap.at[s]
             src_m = am.at[s]
         cp = remote(src_p, rp.at[s], zr)
         cm = remote(src_m, rm.at[s], zl)
         cp.wait_recv()
         cm.wait_recv()
-
-    base = core * half + xl * quarter
-    own = pl.ds(pl.multiple_of(base + z * chunk, 8), chunk)
-    o_ref[own, lo] = s2[rows_of(z), lo] + rp[nz - 2]
-    o_ref[own, hi] = s2[rows_of(z), hi] + rm[nz - 2]
+    f1[:, lo] = s1[rows_of(z), lo] + rp[nz - 2]
+    f1[:, hi] = s1[rows_of(z), hi] + rm[nz - 2]
+
+    piece = chunk // 2
+    mine_x = pl.multiple_of(xl * piece, 8)
+    other_x = pl.multiple_of((1 - xl) * piece, 8)
+    c = remote(f1.at[pl.ds(other_x, piece)], rx, px)
+    c.wait_recv()
+    base = core * half + z * chunk
+    own = pl.ds(pl.multiple_of(base + xl * piece, 8), piece)
+    o_ref[own, :] = f1[pl.ds(mine_x, piece), :] + rx[...]
+
+    c = remote(o_ref.at[own], o_ref.at[own], px)
+    c.wait_recv()
 
     for s in range(nz - 1):
         jp = (z + nz - s) % nz
         jm = (z + s) % nz
-        rp_rows = pl.ds(pl.multiple_of(base + jp * chunk, 8), chunk)
-        rm_rows = pl.ds(pl.multiple_of(base + jm * chunk, 8), chunk)
+        rp_rows = pl.ds(pl.multiple_of(core * half + jp * chunk, 8), chunk)
+        rm_rows = pl.ds(pl.multiple_of(core * half + jm * chunk, 8), chunk)
         cp = remote(o_ref.at[rp_rows, lo], o_ref.at[rp_rows, lo], zr)
         cm = remote(o_ref.at[rm_rows, hi], o_ref.at[rm_rows, hi], zl)
         cp.wait_recv()
         cm.wait_recv()
 
-    q_rows = pl.ds(pl.multiple_of(base, 8), quarter)
-    c = remote(o_ref.at[q_rows], o_ref.at[q_rows], px)
-    c.wait_recv()
-
     h_rows = pl.ds(pl.multiple_of(core * half, 8), half)
     c = remote(o_ref.at[h_rows], o_ref.at[h_rows], pc)
     c.wait_recv()
@@ -125,8 +123,7 @@
     rows, cols = a.shape
     nz = lax.axis_size("dp") // 4
     half = rows // 2
-    quarter = half // 2
-    chunk = quarter // nz
+    chunk = half // nz
     lanes = cols // 2
     n_copies = 2 + 2 * (nz - 1) * 2 + 2
     vmem = pltpu.VMEM
@@ -138,8 +135,8 @@
         scratch_shapes=[
             vmem((half, cols), a.dtype),
             vmem((half, cols), a.dtype),
-            vmem((quarter, cols), a.dtype),
-            vmem((quarter, cols), a.dtype),
+            vmem((chunk, cols), a.dtype),
+            vmem((chunk // 2, cols), a.dtype),
             vmem((nz - 1, chunk, lanes), a.dtype),
             vmem((nz - 1, chunk, lanes), a.dtype),
             vmem((nz - 1, chunk, lanes), a.dtype),

time: 146 us -> 134 us (0.918)
  Pallas kernels: 105 us -> 92.9 us
    pallas_call x1, Pallas kernels: 88.2 us -> 76.2 us  [dp_allreduce(): pl.pallas_call(functools.partial(_allreduce_kernel, axis_names, nz), out_...]
  transfers between devices with their start and end apart: 1 -> 1, of which waited for: 0 -> 0; matrix products, arithmetic and copies ran while one was open for 9% -> 10% of each run, Pallas kernels for 72% -> 70%
where the time goes in v3:
time: 134 us; the launch traced here: 133 us
  Pallas kernels  92.9 us (69%)
  between operations  14.3 us (11%)
  local copies, waits for them, and re-layouts  12.7 us (9%)
  matrix products  11.8 us (9%)
  other arithmetic  1.56 us (1%)
    pallas_call x1, Pallas kernels, dp_allreduce(): pl.pallas_call(functools.partial(_allreduce_kernel, axis_names, nz), out_...  76.2 us
    pallas_call x1, Pallas kernels, chan_allgather(): pl.pallas_call(functools.partial(_allgather_kernel, axis_names, n), out_s...  16.7 us
    unnamed x27, local copies, waits for them, and re-layouts  9.03 us
    dot_general x9, matrix products, on_device(): lax.dot_general(displaced_input[tap_index], flat_grads, contract_cols, pr...  4.56 us
    dot_general x9, matrix products, on_device(): lax.dot_general(columns, displaced_input[tap_index], contract_rows, prefe...  3.97 us
    dot_general x9, matrix products, on_device(): jnp.dot(weight[:, tap_index, :], displaced_gradient, preferred_element_ty...  3.29 us
  transfers between devices with their start and end apart: 1, of which 0 were waited for; matrix products, arithmetic and copies ran while one was open for 10% of the time, Pallas kernels for 70%

profile of v3, /device:TPU:1, one launch (start us, length us, event | category | flops | bytes accessed | tf_op | source)
XLA Modules:
  0.0 133.3 jit_solution(12105872873966275393)
XLA Ops:
  7.2 1.3 copy.16
  8.5 0.7 pad_slice_fusion.12
  9.3 0.5 copy-done.8
  12.3 0.7 copy-done.6
  13.1 1.5 %fusion.3 = f32[256,1152]{0,1:T(8,128)} fusion(f32[256,1152]{0,1:T(8,128)S(1)} %convolution_bitcast_fusion.4, f32[256,1152]{0,1:T(8,128)S(1)} %convolution_bitcast_fusion.5, f32[256,1152]{0,1:T(8,128)S(1)} %convolution_bitcast_fusion.6, f32[256,1152]{0,1:T(8,128)S(1)} %convolution_bitcast_fusion.7, f32[256,1152]{0,1:T(8,128)S(1)} %fusion.8, ...), kind=kOutput, calls=%fused_computation.27 | convolution fusion | flops 152469504 | bytes 7798784 | tf_op jit(solution)/shard_map/dot_general | solution.py:243
  14.6 2.7 %copy.24 = f32[256,1152]{1,0:T(8,128)} copy(f32[256,1152]{0,1:T(8,128)} %fusion.3) | data formatting | bytes 2359296
  17.3 16.7 %shard_map.58 = bf16[256,1152]{1,0:T(8,128)(2,1)} custom-call(bf16[32,1152]{1,0:T(8,128)(2,1)} %bitcast.198), custom_call_target="tpu_custom_call" | custom-call | tf_op jit(solution)/shard_map/pallas_call | solution.py:190
  34.0 2.2 %copy.18 = bf16[256,1152]{0,1:T(8,128)(2,1)} copy(bf16[256,1152]{1,0:T(8,128)(2,1)} %shard_map.58) | data formatting | bytes 1179648 | tf_op jit(solution)/shard_map/pallas_call | solution.py:190
  36.1 1.5 %fusion.20 = f32[9,256,256]{2,1,0:T(8,128)S(1)} fusion(bf16[256,1152]{0,1:T(8,128)(2,1)} %bitcast.185, bf16[256,1152]{1,0:T(8,128)(2,1)S(1)} %copy-done), kind=kOutput, calls=%fused_computation.62 | convolution fusion | flops 150994944 | bytes 1441792 | tf_op jit(solution)/shard_map/dot_general | solution.py:221
  37.7 0.4 fusion.19
  38.1 0.4 fusion.18
  38.5 0.4 fusion.17
  39.5 0.4 fusion.15
  39.9 0.4 fusion.14
  40.3 0.4 fusion.13
  40.7 0.4 fusion.12
  41.1 76.2 %shard_map.59 = f32[2304,256]{1,0:T(8,128)S(1)} custom-call(f32[2304,256]{1,0:T(8,128)S(1)} %bitcast.169), custom_call_target="tpu_custom_call" | custom-call | tf_op jit(solution)/shard_map/pallas_call | solution.py:130
  117.3 0.7 pad_slice_fusion.4
  118.1 0.5 copy-done.9
  121.4 0.5 fusion.11
  121.9 1.1 copy.21
  123.0 1.6 %broadcast_multiply_fusion = f32[2304,256]{1,0:T(8,128)} fusion(f32[2304,256]{1,0:T(8,128)S(1)} %shard_map.59), kind=kLoop, calls=%fused_computation.44 | loop fusion | flops 589824 | bytes 4718592 | tf_op jit(solution)/shard_map/div | solution.py:237
  124.5 1.1 copy.25
  125.7 0.8 copy.20
  (39 shorter events, 6.0 us)
Async XLA Ops:
  7.2 117.4 %reduce-scatter.4.cloned.1.call-start = ((), (), s32[]{:S(2)}) async-start(), calls=%async_computation.1 | async-start | bytes 1327104
  8.5 1.3 copy-start.8
  9.3 1.8 %copy-start.5 = (bf16[256,16,72]{0,2,1:T(8,128)(2,1)}, bf16[256,16,72]{0,2,1:T(8,128)(2,1)S(1)}, u32[]{:S(2)}) copy-start(bf16[256,16,72]{0,2,1:T(8,128)(2,1)S(1)} %get-tuple-element.27) | copy-start | bytes 1769476
  9.3 2.1 %copy-start.3 = (bf16[256,16,72]{0,2,1:T(8,128)(2,1)}, bf16[256,16,72]{0,2,1:T(8,128)(2,1)S(1)}, u32[]{:S(2)}) copy-start(bf16[256,16,72]{0,2,1:T(8,128)(2,1)S(1)} %get-tuple-element.21) | copy-start | bytes 1769476
  9.3 2.4 %copy-start.1 = (bf16[256,16,72]{0,2,1:T(8,128)(2,1)}, bf16[256,16,72]{0,2,1:T(8,128)(2,1)S(1)}, u32[]{:S(2)}) copy-start(bf16[256,16,72]{0,2,1:T(8,128)(2,1)S(1)} %get-tuple-element.22) | copy-start | bytes 1769476
  12.0 1.1 copy-start.6
  33.9 2.2 %copy-start = (bf16[256,1152]{1,0:T(8,128)(2,1)S(1)}, bf16[256,1152]{1,0:T(8,128)(2,1)}, u32[]{:S(2)}) copy-start(bf16[256,1152]{1,0:T(8,128)(2,1)} %shard_map.58) | copy-start | bytes 1769476
  36.1 1.6 %copy-start.4 = (bf16[256,16,72]{0,2,1:T(8,128)(2,1)S(1)}, bf16[256,16,72]{0,2,1:T(8,128)(2,1)}, u32[]{:S(2)}) copy-start(bf16[256,16,72]{0,2,1:T(8,128)(2,1)} %copy-done.3) | copy-start | bytes 1769476
  36.1 1.9 %copy-start.2 = (bf16[256,16,72]{0,2,1:T(8,128)(2,1)S(1)}, bf16[256,16,72]{0,2,1:T(8,128)(2,1)}, u32[]{:S(2)}) copy-start(bf16[256,16,72]{0,2,1:T(8,128)(2,1)} %copy-done.1) | copy-start | bytes 1769476
  38.1 1.1 copy-start.7
  41.1 76.2 %copy-start.10 = (bf16[256,1152]{0,1:T(8,128)(2,1)S(1)}, bf16[256,1152]{0,1:T(8,128)(2,1)}, u32[]{:S(2)}) copy-start(bf16[256,1152]{0,1:T(8,128)(2,1)} %copy.18) | copy-start | bytes 1769476
  117.3 1.3 copy-start.9
Sparse Core Ops, SparseCore 0:
  17.4 79.5 reduce-scatter.3

commit v4 on v3

--- a/solution.py
+++ b/solution.py
@@ -22,8 +22,8 @@
     ]
 
 
-def _allreduce_kernel(axis_names, nz, a_ref, o_ref, rc, s1, f1, rx, rp, rm, ap, am,
-                      send_sems, recv_sems):
+def _allreduce_kernel(axis_names, nz, nc, a_ref, t_ref, o_ref, res_ref, rc, s1, f1, rx, rp, rm,
+                      ap, am, rs_buf, send_sems, recv_sems, rs_send, rs_recv):
     rows, cols = a_ref.shape
     half = rows // 2
     chunk = half // nz
@@ -39,13 +39,31 @@
     zr = (dp + 4) % nd
     zl = (dp + nd - 4) % nd
 
+    me = lax.axis_index("chan")
+
     def dev(p):
         return tuple(p if n == "dp" else lax.axis_index(n) for n in axis_names)
+
+    def cdev(p):
+        return tuple(p if n == "chan" else lax.axis_index(n) for n in axis_names)
 
     barrier = pltpu.get_barrier_semaphore()
     for peer in (pc, px, zr, zl):
         pl.semaphore_signal(barrier, inc=1, device_id=dev(peer), device_id_type=MESH)
-    pl.semaphore_wait(barrier, 4)
+    for k in range(1, nc):
+        pl.semaphore_signal(barrier, inc=1, device_id=cdev((me + k) % nc), device_id_type=MESH)
+    pl.semaphore_wait(barrier, 4 + nc - 1)
+
+    owned = res_ref.shape[0]
+    rs_copies = []
+    for k in range(1, nc):
+        peer = (me + k) % nc
+        c = pltpu.make_async_remote_copy(
+            src_ref=t_ref.at[pl.ds(pl.multiple_of(peer * owned, 8), owned)],
+            dst_ref=rs_buf.at[k], send_sem=rs_send.at[k], recv_sem=rs_recv.at[k],
+            device_id=cdev(peer), device_id_type=MESH)
+        c.start()
+        rs_copies.append(c)
 
     sent = []
     counter = [0]
@@ -115,12 +133,21 @@
     c = remote(o_ref.at[h_rows], o_ref.at[h_rows], pc)
     c.wait_recv()
 
-    for c in sent:
+    for c in rs_copies:
+        c.wait_recv()
+    acc = t_ref[pl.ds(pl.multiple_of(me * owned, 8), owned), :]
+    for k in range(1, nc):
+        acc = acc + rs_buf[k]
+    res_ref[...] = acc.astype(res_ref.dtype)
+
+    for c in sent + rs_copies:
         c.wait_send()
 
 
-def dp_allreduce(a, axis_names):
+def dp_allreduce(a, t, axis_names):
     rows, cols = a.shape
+    nc = lax.axis_size("chan")
+    owned = t.shape[0] // nc
     nz = lax.axis_size("dp") // 4
     half = rows // 2
     chunk = half // nz
@@ -128,10 +155,13 @@
     n_copies = 2 + 2 * (nz - 1) * 2 + 2
     vmem = pltpu.VMEM
     return pl.pallas_call(
-        functools.partial(_allreduce_kernel, axis_names, nz),
-        out_shape=jax.ShapeDtypeStruct((rows, cols), a.dtype),
-        in_specs=[pl.BlockSpec(memory_space=vmem)],
-        out_specs=pl.BlockSpec(memory_space=vmem),
+        functools.partial(_allreduce_kernel, axis_names, nz, nc),
+        out_shape=(
+            jax.ShapeDtypeStruct((rows, cols), a.dtype),
+            jax.ShapeDtypeStruct((owned, t.shape[1]), jnp.bfloat16),
+        ),
+        in_specs=[pl.BlockSpec(memory_space=vmem)] * 2,
+        out_specs=(pl.BlockSpec(memory_space=vmem), pl.BlockSpec(memory_space=vmem)),
         scratch_shapes=[
             vmem((half, cols), a.dtype),
             vmem((half, cols), a.dtype),
@@ -141,13 +171,16 @@
             vmem((nz - 1, chunk, lanes), a.dtype),
             vmem((nz - 1, chunk, lanes), a.dtype),
             vmem((nz - 1, chunk, lanes), a.dtype),
+            vmem((nc, owned, t.shape[1]), t.dtype),
             pltpu.SemaphoreType.DMA((n_copies,)),
             pltpu.SemaphoreType.DMA((n_copies,)),
+            pltpu.SemaphoreType.DMA((nc,)),
+            pltpu.SemaphoreType.DMA((nc,)),
         ],
         compiler_params=pltpu.CompilerParams(
             collective_id=0, has_side_effects=True, vmem_limit_bytes=48 * 1024 * 1024
         ),
-    )(a)
+    )(a, t)
 
 
 def _allgather_kernel(axis_names, n, x_ref, o_ref, send_sems, recv_sems):
@@ -228,14 +261,6 @@
         ],
         axis=0,
     )
-    summed = dp_allreduce(
-        local_grad.reshape(tap_list * input_channels_local, output_channels_total), axis_names
-    )
-    summed_grad = jnp.transpose(
-        summed.reshape(tap_list, input_channels_local, output_channels_total), (1, 0, 2)
-    )
-    weight_grad = summed_grad / jnp.float32(lax.axis_size("dp"))
-
     contract_rows = (((0,), (0,)), ((), ()))
     total = jnp.zeros((cout_local * lax.axis_size("chan"), tap_locations), jnp.float32)
     for tap_index in range(tap_list):
@@ -243,8 +268,15 @@
         total = total + lax.dot_general(
             columns, displaced_input[tap_index], contract_rows, preferred_element_type=jnp.float32
         )
-    owned = lax.psum_scatter(total, "chan", scatter_dimension=0, tiled=True)
-    result = owned.astype(jnp.bfloat16).reshape(1, cout_local, tap_locations)
+    summed, owned = dp_allreduce(
+        local_grad.reshape(tap_list * input_channels_local, output_channels_total), total, axis_names
+    )
+    result = owned.reshape(1, cout_local, tap_locations)
+    summed_grad = jnp.transpose(
+        summed.reshape(tap_list, input_channels_local, output_channels_total), (1, 0, 2)
+    )
+    weight_grad = summed_grad / jnp.float32(lax.axis_size("dp"))
+
     collected_input = flat_grads.reshape(output_channels_total, MAP_HEIGHT, MAP_WIDTH)
     back_sum = jnp.zeros((input_channels_local, tap_locations), jnp.float32)
     for tap_index in range(tap_list):

time: 134 us -> 112 us (0.84)
  between operations: 14.3 us -> 0.86 us
  local copies, waits for them, and re-layouts: 12.7 us -> 5.96 us
  matrix products: 11.8 us -> 10.2 us
    unnamed x27 -> x9, local copies, waits for them, and re-layouts: 9.03 us -> 3.18 us
  transfers between devices with their start and end apart: 1 -> 0, of which waited for: 0 -> 0; matrix products, arithmetic and copies ran while one was open for 10% -> 0% of each run, Pallas kernels for 70% -> 0%
where the time goes in v4:
time: 112 us
  Pallas kernels  93.6 us (84%)
  matrix products  10.2 us (9%)
  local copies, waits for them, and re-layouts  5.96 us (5%)
  other arithmetic  1.56 us (1%)
    pallas_call x1, Pallas kernels, dp_allreduce(): pl.pallas_call(functools.partial(_allreduce_kernel, axis_names, nz, nc),...  77 us
    pallas_call x1, Pallas kernels, chan_allgather(): pl.pallas_call(functools.partial(_allgather_kernel, axis_names, n), out_s...  16.7 us
    dot_general x9, matrix products, on_device(): lax.dot_general(columns, displaced_input[tap_index], contract_rows, prefe...  3.53 us
    dot_general x9, matrix products, on_device(): lax.dot_general(displaced_input[tap_index], flat_grads, contract_cols, pr...  3.39 us
    dot_general x9, matrix products, on_device(): jnp.dot(weight[:, tap_index, :], displaced_gradient, preferred_element_ty...  3.25 us
    unnamed x9, local copies, waits for them, and re-layouts  3.18 us

profile of v4, /device:TPU:1, one launch (start us, length us, event | category | flops | bytes accessed | tf_op | source)
XLA Modules:
  0.0 112.2 jit_solution(10790781852450024449)
XLA Ops:
  0.6 16.7 %shard_map.58 = bf16[256,1152]{1,0:T(8,128)(2,1)} custom-call(bf16[32,1152]{1,0:T(8,128)(2,1)} %bitcast.195), custom_call_target="tpu_custom_call" | custom-call | tf_op jit(solution)/shard_map/pallas_call | solution.py:223
  17.3 1.3 %copy.25 = bf16[256,1152]{0,1:T(8,128)(2,1)S(1)} copy(bf16[256,1152]{1,0:T(8,128)(2,1)} %shard_map.58) | data formatting | bytes 1179648 | tf_op jit(solution)/shard_map/pallas_call | solution.py:223
  18.6 0.7 pad_slice_fusion.4
  19.4 0.5 copy-done.2
  22.7 0.7 copy-done
  23.4 0.5 fusion.11
  23.9 1.1 copy.27
  25.2 0.7 pad_slice_fusion.8
  26.0 0.4 fusion.20
  26.4 0.4 fusion.19
  26.7 0.4 fusion.18
  27.1 0.4 fusion.17
  27.9 0.4 fusion.15
  28.3 0.4 fusion.14
  28.7 0.4 fusion.13
  29.1 0.4 fusion.12
  29.8 0.4 convolution_add_fusion.7
  30.2 0.4 convolution_add_fusion.6
  30.6 0.4 fusion.8
  31.3 0.4 convolution_bitcast_fusion.5
  32.5 0.5 fusion.3.t_ref
  33.0 77.0 %shard_map.59 = (f32[2304,256]{1,0:T(8,128)S(1)}, bf16[32,1152]{1,0:T(8,128)(2,1)S(1)}) custom-call(f32[2304,256]{1,0:T(8,128)S(1)} %bitcast.166, f32[256,1152]{1,0:T(8,128)S(1)} %fusion.3.t_ref), custom_call_target="tpu_custom_call" | custom-call | tf_op jit(solution)/shard_map/pallas_call | solution.py:157
  110.0 1.6 %broadcast_multiply_fusion = f32[2304,256]{1,0:T(8,128)} fusion(f32[2304,256]{1,0:T(8,128)S(1)} %get-tuple-element.6), kind=kLoop, calls=%fused_computation.44 | loop fusion | flops 589824 | bytes 4718592 | tf_op jit(solution)/shard_map/div | solution.py:278
  111.5 0.6 copy.46
  (18 shorter events, 4.9 us)
Async XLA Ops:
  18.6 1.3 %copy-start.2 = (bf16[256,9,256]{2,0,1:T(8,128)(2,1)S(1)}, bf16[256,9,256]{2,0,1:T(8,128)(2,1)}, u32[]{:S(2)}) copy-start(bf16[256,9,256]{2,0,1:T(8,128)(2,1)} %param.4) | copy-start | bytes 3538948
  22.3 1.1 copy-start
  23.9 1.1 copy-start.1

commit v5 on v4

--- a/solution.py
+++ b/solution.py
@@ -78,20 +78,41 @@
         sent.append(c)
         return c
 
-    mine_c = pl.multiple_of(core * half, 8)
-    other_c = pl.multiple_of((1 - core) * half, 8)
-    c = remote(a_ref.at[pl.ds(other_c, half)], rc, pc)
-    c.wait_recv()
-    s1[...] = a_ref[pl.ds(mine_c, half), :] + rc[...]
-
     def rows_of(j):
         return pl.ds(pl.multiple_of(j * chunk, 8), chunk)
+
+    mine_c = core * half
+    other_c = (1 - core) * half
+    order = []
+    for d in range(1, nz // 2 + 1):
+        order.append((z + nz - d) % nz)
+        if 2 * d != nz:
+            order.append((z + d) % nz)
+    order.append(z)
+    core_in = []
+    for j in order:
+        src_rows = pl.ds(pl.multiple_of(other_c + j * chunk, 8), chunk)
+        core_in.append((j, remote(a_ref.at[src_rows], rc.at[rows_of(j)], pc)))
+    ready = [0]
+
+    def ready_upto(n):
+        while ready[0] < n:
+            j, c = core_in[ready[0]]
+            c.wait_recv()
+            own_rows = pl.ds(pl.multiple_of(mine_c + j * chunk, 8), chunk)
+            s1[rows_of(j), :] = a_ref[own_rows, :] + rc[rows_of(j), :]
+            ready[0] += 1
+
+    def needed(d):
+        return min(len(order) - 1, 2 * d - (1 if 2 * d == nz else 0))
 
     lo = pl.ds(0, lanes)
     hi = pl.ds(lanes, lanes)
     for s in range(nz - 1):
         jp = (z + 2 * nz - 1 - s) % nz
         jm = (z + 1 + s) % nz
+        if s + 1 <= nz // 2:
+            ready_upto(needed(s + 1))
         if s == 0:
             src_p = s1.at[rows_of(jp), lo]
             src_m = s1.at[rows_of(jm), hi]
@@ -104,6 +125,7 @@
         cm = remote(src_m, rm.at[s], zl)
         cp.wait_recv()
         cm.wait_recv()
+    ready_upto(len(order))
     f1[:, lo] = s1[rows_of(z), lo] + rp[nz - 2]
     f1[:, hi] = s1[rows_of(z), hi] + rm[nz - 2]
 
@@ -119,6 +141,8 @@
     c = remote(o_ref.at[own], o_ref.at[own], px)
     c.wait_recv()
 
+    own_chunk = pl.ds(pl.multiple_of(core * half + z * chunk, 8), chunk)
+    to_core = [remote(o_ref.at[own_chunk], o_ref.at[own_chunk], pc)]
     for s in range(nz - 1):
         jp = (z + nz - s) % nz
         jm = (z + s) % nz
@@ -128,10 +152,12 @@
         cm = remote(o_ref.at[rm_rows, hi], o_ref.at[rm_rows, hi], zl)
         cp.wait_recv()
         cm.wait_recv()
-
-    h_rows = pl.ds(pl.multiple_of(core * half, 8), half)
-    c = remote(o_ref.at[h_rows], o_ref.at[h_rows], pc)
-    c.wait_recv()
+        gp = pl.ds(pl.multiple_of(core * half + ((jp + nz - 1) % nz) * chunk, 8), chunk)
+        gm = pl.ds(pl.multiple_of(core * half + ((jm + 1) % nz) * chunk, 8), chunk)
+        to_core.append(remote(o_ref.at[gp, lo], o_ref.at[gp, lo], pc))
+        to_core.append(remote(o_ref.at[gm, hi], o_ref.at[gm, hi], pc))
+    for c in to_core:
+        c.wait_recv()
 
     for c in rs_copies:
         c.wait_recv()
@@ -152,7 +178,7 @@
     half = rows // 2
     chunk = half // nz
     lanes = cols // 2
-    n_copies = 2 + 2 * (nz - 1) * 2 + 2
+    n_copies = nz + 6 * (nz - 1) + 3
     vmem = pltpu.VMEM
     return pl.pallas_call(
         functools.partial(_allreduce_kernel, axis_names, nz, nc),

time: 112 us -> 110 us (0.982)
  Pallas kernels: 93.6 us -> 91.6 us
    pallas_call x1, Pallas kernels: 77 us -> 74.9 us  [dp_allreduce(): pl.pallas_call(functools.partial(_allreduce_kernel, axis_names, nz, nc),...]
where the time goes in v5:
time: 110 us
  Pallas kernels  91.6 us (83%)
  matrix products  10.2 us (9%)
  local copies, waits for them, and re-layouts  5.96 us (5%)
  other arithmetic  1.56 us (1%)
    pallas_call x1, Pallas kernels, dp_allreduce(): pl.pallas_call(functools.partial(_allreduce_kernel, axis_names, nz, nc),...  74.9 us
    pallas_call x1, Pallas kernels, chan_allgather(): pl.pallas_call(functools.partial(_allgather_kernel, axis_names, n), out_s...  16.7 us
    dot_general x9, matrix products, on_device(): lax.dot_general(columns, displaced_input[tap_index], contract_rows, prefe...  3.53 us
    dot_general x9, matrix products, on_device(): lax.dot_general(displaced_input[tap_index], flat_grads, contract_cols, pr...  3.39 us
    dot_general x9, matrix products, on_device(): jnp.dot(weight[:, tap_index, :], displaced_gradient, preferred_element_ty...  3.25 us
    unnamed x9, local copies, waits for them, and re-layouts  3.18 us

profile of v5, /device:TPU:1, one launch (start us, length us, event | category | flops | bytes accessed | tf_op | source)
XLA Modules:
  0.0 110.1 jit_solution(7758897675407614018)
XLA Ops:
  0.6 16.7 %shard_map.58 = bf16[256,1152]{1,0:T(8,128)(2,1)} custom-call(bf16[32,1152]{1,0:T(8,128)(2,1)} %bitcast.195), custom_call_target="tpu_custom_call" | custom-call | tf_op jit(solution)/shard_map/pallas_call | solution.py:249
  17.3 1.3 %copy.25 = bf16[256,1152]{0,1:T(8,128)(2,1)S(1)} copy(bf16[256,1152]{1,0:T(8,128)(2,1)} %shard_map.58) | data formatting | bytes 1179648 | tf_op jit(solution)/shard_map/pallas_call | solution.py:249
  18.6 0.7 pad_slice_fusion.4
  19.4 0.5 copy-done.2
  22.7 0.7 copy-done
  23.4 0.5 fusion.11
  23.9 1.1 copy.27
  25.2 0.7 pad_slice_fusion.8
  26.0 0.4 fusion.20
  26.4 0.4 fusion.19
  26.7 0.4 fusion.18
  27.1 0.4 fusion.17
  27.9 0.4 fusion.15
  28.3 0.4 fusion.14
  28.7 0.4 fusion.13
  29.1 0.4 fusion.12
  29.8 0.4 convolution_add_fusion.7
  30.2 0.4 convolution_add_fusion.6
  30.6 0.4 fusion.8
  31.3 0.4 convolution_bitcast_fusion.5
  32.5 0.5 fusion.3.t_ref
  33.0 74.9 %shard_map.59 = (f32[2304,256]{1,0:T(8,128)S(1)}, bf16[32,1152]{1,0:T(8,128)(2,1)S(1)}) custom-call(f32[2304,256]{1,0:T(8,128)S(1)} %bitcast.166, f32[256,1152]{1,0:T(8,128)S(1)} %fusion.3.t_ref), custom_call_target="tpu_custom_call" | custom-call | tf_op jit(solution)/shard_map/pallas_call | solution.py:183
  107.9 1.6 %broadcast_multiply_fusion = f32[2304,256]{1,0:T(8,128)} fusion(f32[2304,256]{1,0:T(8,128)S(1)} %get-tuple-element.6), kind=kLoop, calls=%fused_computation.44 | loop fusion | flops 589824 | bytes 4718592 | tf_op jit(solution)/shard_map/div | solution.py:304
  109.5 0.6 copy.46
  (18 shorter events, 4.9 us)
Async XLA Ops:
  18.6 1.3 %copy-start.2 = (bf16[256,9,256]{2,0,1:T(8,128)(2,1)S(1)}, bf16[256,9,256]{2,0,1:T(8,128)(2,1)}, u32[]{:S(2)}) copy-start(bf16[256,9,256]{2,0,1:T(8,128)(2,1)} %param.4) | copy-start | bytes 3538948
  22.3 1.1 copy-start
  23.9 1.1 copy-start.1

commit v6 on v5

--- a/solution.py
+++ b/solution.py
@@ -10,6 +10,7 @@
 DILATION_RATE = 12
 MAP_HEIGHT = 16
 MAP_WIDTH = 72
+STREAMS = 2
 
 
 def translated_input(receptive_field, row_shift, column_shift, reach):
@@ -22,7 +23,7 @@
     ]
 
 
-def _allreduce_kernel(axis_names, nz, nc, a_ref, t_ref, o_ref, res_ref, rc, s1, f1, rx, rp, rm,
+def _allreduce_kernel(axis_names, nz, nc, streams, a_ref, t_ref, o_ref, res_ref, rc, s1, f1, rx, rp, rm,
                       ap, am, rs_buf, send_sems, recv_sems, rs_send, rs_recv):
     rows, cols = a_ref.shape
     half = rows // 2
@@ -108,23 +109,33 @@
 
     lo = pl.ds(0, lanes)
     hi = pl.ds(lanes, lanes)
+    sub = chunk // streams
+
+    def srows(j, q):
+        return pl.ds(pl.multiple_of(j * chunk + q * sub, 8), sub)
+
+    blk = [pl.ds(q * sub, sub) for q in range(streams)]
+    pending = [None] * streams
     for s in range(nz - 1):
         jp = (z + 2 * nz - 1 - s) % nz
         jm = (z + 1 + s) % nz
         if s + 1 <= nz // 2:
             ready_upto(needed(s + 1))
-        if s == 0:
-            src_p = s1.at[rows_of(jp), lo]
-            src_m = s1.at[rows_of(jm), hi]
-        else:
-            ap[s] = s1[rows_of(jp), lo] + rp[s - 1]
-            am[s] = s1[rows_of(jm), hi] + rm[s - 1]
-            src_p = ap.at[s]
-            src_m = am.at[s]
-        cp = remote(src_p, rp.at[s], zr)
-        cm = remote(src_m, rm.at[s], zl)
-        cp.wait_recv()
-        cm.wait_recv()
+        for q in range(streams):
+            if s == 0:
+                src_p = s1.at[srows(jp, q), lo]
+                src_m = s1.at[srows(jm, q), hi]
+            else:
+                pending[q][0].wait_recv()
+                pending[q][1].wait_recv()
+                ap[s, blk[q], :] = s1[srows(jp, q), lo] + rp[s - 1, blk[q], :]
+                am[s, blk[q], :] = s1[srows(jm, q), hi] + rm[s - 1, blk[q], :]
+                src_p = ap.at[s, blk[q]]
+                src_m = am.at[s, blk[q]]
+            pending[q] = (remote(src_p, rp.at[s, blk[q]], zr), remote(src_m, rm.at[s, blk[q]], zl))
+    for q in range(streams):
+        pending[q][0].wait_recv()
+        pending[q][1].wait_recv()
     ready_upto(len(order))
     f1[:, lo] = s1[rows_of(z), lo] + rp[nz - 2]
     f1[:, hi] = s1[rows_of(z), hi] + rm[nz - 2]
@@ -143,19 +154,30 @@
 
     own_chunk = pl.ds(pl.multiple_of(core * half + z * chunk, 8), chunk)
     to_core = [remote(o_ref.at[own_chunk], o_ref.at[own_chunk], pc)]
+
+    def grows(j, q):
+        return pl.ds(pl.multiple_of(core * half + j * chunk + q * sub, 8), sub)
+
+    def arrived(q, jp, jm):
+        pending[q][0].wait_recv()
+        pending[q][1].wait_recv()
+        gp = grows((jp + nz - 1) % nz, q)
+        gm = grows((jm + 1) % nz, q)
+        to_core.append(remote(o_ref.at[gp, lo], o_ref.at[gp, lo], pc))
+        to_core.append(remote(o_ref.at[gm, hi], o_ref.at[gm, hi], pc))
+
     for s in range(nz - 1):
         jp = (z + nz - s) % nz
         jm = (z + s) % nz
-        rp_rows = pl.ds(pl.multiple_of(core * half + jp * chunk, 8), chunk)
-        rm_rows = pl.ds(pl.multiple_of(core * half + jm * chunk, 8), chunk)
-        cp = remote(o_ref.at[rp_rows, lo], o_ref.at[rp_rows, lo], zr)
-        cm = remote(o_ref.at[rm_rows, hi], o_ref.at[rm_rows, hi], zl)
-        cp.wait_recv()
-        cm.wait_recv()
-        gp = pl.ds(pl.multiple_of(core * half + ((jp + nz - 1) % nz) * chunk, 8), chunk)
-        gm = pl.ds(pl.multiple_of(core * half + ((jm + 1) % nz) * chunk, 8), chunk)
-        to_core.append(remote(o_ref.at[gp, lo], o_ref.at[gp, lo], pc))
-        to_core.append(remote(o_ref.at[gm, hi], o_ref.at[gm, hi], pc))
+        for q in range(streams):
+            if s > 0:
+                arrived(q, (jp + 1) % nz, (jm + nz - 1) % nz)
+            gp = grows(jp, q)
+            gm = grows(jm, q)
+            pending[q] = (remote(o_ref.at[gp, lo], o_ref.at[gp, lo], zr),
+                          remote(o_ref.at[gm, hi], o_ref.at[gm, hi], zl))
+    for q in range(streams):
+        arrived(q, (z + 2) % nz, (z + nz - 2) % nz)
     for c in to_core:
         c.wait_recv()
 
@@ -178,10 +200,10 @@
     half = rows // 2
     chunk = half // nz
     lanes = cols // 2
-    n_copies = nz + 6 * (nz - 1) + 3
+    n_copies = nz + 3 + 6 * (nz - 1) * STREAMS
     vmem = pltpu.VMEM
     return pl.pallas_call(
-        functools.partial(_allreduce_kernel, axis_names, nz, nc),
+        functools.partial(_allreduce_kernel, axis_names, nz, nc, STREAMS),
         out_shape=(
             jax.ShapeDtypeStruct((rows, cols), a.dtype),
             jax.ShapeDtypeStruct((owned, t.shape[1]), jnp.bfloat16),

time: 110 us -> 106 us (0.964)
  Pallas kernels: 91.6 us -> 87.4 us
    pallas_call x1, Pallas kernels: 74.9 us -> 70.7 us  [dp_allreduce(): pl.pallas_call(functools.partial(_allreduce_kernel, axis_names, nz, nc, S...]
where the time goes in v6:
time: 106 us
  Pallas kernels  87.4 us (82%)
  matrix products  10.2 us (10%)
  local copies, waits for them, and re-layouts  5.96 us (6%)
  other arithmetic  1.56 us (1%)
    pallas_call x1, Pallas kernels, dp_allreduce(): pl.pallas_call(functools.partial(_allreduce_kernel, axis_names, nz, nc, S...  70.7 us
    pallas_call x1, Pallas kernels, chan_allgather(): pl.pallas_call(functools.partial(_allgather_kernel, axis_names, n), out_s...  16.7 us
    dot_general x9, matrix products, on_device(): lax.dot_general(columns, displaced_input[tap_index], contract_rows, prefe...  3.53 us
    dot_general x9, matrix products, on_device(): lax.dot_general(displaced_input[tap_index], flat_grads, contract_cols, pr...  3.39 us
    dot_general x9, matrix products, on_device(): jnp.dot(weight[:, tap_index, :], displaced_gradient, preferred_element_ty...  3.25 us
    unnamed x9, local copies, waits for them, and re-layouts  3.18 us

profile of v6, /device:TPU:1, one launch (start us, length us, event | category | flops | bytes accessed | tf_op | source)
XLA Modules:
  0.0 106.0 jit_solution(12632570318146274058)
XLA Ops:
  0.6 16.7 %shard_map.58 = bf16[256,1152]{1,0:T(8,128)(2,1)} custom-call(bf16[32,1152]{1,0:T(8,128)(2,1)} %bitcast.195), custom_call_target="tpu_custom_call" | custom-call | tf_op jit(solution)/shard_map/pallas_call | solution.py:271
  17.3 1.3 %copy.25 = bf16[256,1152]{0,1:T(8,128)(2,1)S(1)} copy(bf16[256,1152]{1,0:T(8,128)(2,1)} %shard_map.58) | data formatting | bytes 1179648 | tf_op jit(solution)/shard_map/pallas_call | solution.py:271
  18.6 0.7 pad_slice_fusion.4
  19.4 0.5 copy-done.2
  22.7 0.7 copy-done
  23.4 0.5 fusion.11
  23.9 1.1 copy.27
  25.2 0.7 pad_slice_fusion.8
  26.0 0.4 fusion.20
  26.4 0.4 fusion.19
  26.7 0.4 fusion.18
  27.1 0.4 fusion.17
  27.9 0.4 fusion.15
  28.3 0.4 fusion.14
  28.7 0.4 fusion.13
  29.1 0.4 fusion.12
  29.8 0.4 convolution_add_fusion.7
  30.2 0.4 convolution_add_fusion.6
  30.6 0.4 fusion.8
  31.3 0.4 convolution_bitcast_fusion.5
  32.5 0.5 fusion.3.t_ref
  33.0 70.7 %shard_map.59 = (f32[2304,256]{1,0:T(8,128)S(1)}, bf16[32,1152]{1,0:T(8,128)(2,1)S(1)}) custom-call(f32[2304,256]{1,0:T(8,128)S(1)} %bitcast.166, f32[256,1152]{1,0:T(8,128)S(1)} %fusion.3.t_ref), custom_call_target="tpu_custom_call" | custom-call | tf_op jit(solution)/shard_map/pallas_call | solution.py:205
  103.8 1.6 %broadcast_multiply_fusion = f32[2304,256]{1,0:T(8,128)} fusion(f32[2304,256]{1,0:T(8,128)S(1)} %get-tuple-element.6), kind=kLoop, calls=%fused_computation.44 | loop fusion | flops 589824 | bytes 4718592 | tf_op jit(solution)/shard_map/div | solution.py:326
  105.3 0.6 copy.46
  (18 shorter events, 4.9 us)
Async XLA Ops:
  18.6 1.3 %copy-start.2 = (bf16[256,9,256]{2,0,1:T(8,128)(2,1)S(1)}, bf16[256,9,256]{2,0,1:T(8,128)(2,1)}, u32[]{:S(2)}) copy-start(bf16[256,9,256]{2,0,1:T(8,128)(2,1)} %param.4) | copy-start | bytes 3538948
  22.3 1.1 %copy-start = (bf16[256,1152]{1,0:T(8,128)(2,1)S(1)}, bf16[256,1152]{1,0:T(8,128)(2,1)}, u32[]{:S(2)}) copy-start(bf16[256,1152]{1,0:T(8,128)(2,1)} %shard_map.58) | copy-start | bytes 1769476
  23.9 1.1 %copy-start.1 = (bf16[1,256,1152]{2,1,0:T(8,128)(2,1)S(1)}, bf16[1,256,1152]{2,1,0:T(8,128)(2,1)}, u32[]{:S(2)}) copy-start(bf16[1,256,1152]{2,1,0:T(8,128)(2,1)} %param.3) | copy-start | bytes 1769476

commit v7 on v6

--- a/solution.py
+++ b/solution.py
@@ -10,7 +10,7 @@
 DILATION_RATE = 12
 MAP_HEIGHT = 16
 MAP_WIDTH = 72
-STREAMS = 2
+STREAMS = 3
 
 
 def translated_input(receptive_field, row_shift, column_shift, reach):
@@ -140,19 +140,11 @@
     f1[:, lo] = s1[rows_of(z), lo] + rp[nz - 2]
     f1[:, hi] = s1[rows_of(z), hi] + rm[nz - 2]
 
-    piece = chunk // 2
-    mine_x = pl.multiple_of(xl * piece, 8)
-    other_x = pl.multiple_of((1 - xl) * piece, 8)
-    c = remote(f1.at[pl.ds(other_x, piece)], rx, px)
+    c = remote(f1, rx, px)
     c.wait_recv()
-    base = core * half + z * chunk
-    own = pl.ds(pl.multiple_of(base + xl * piece, 8), piece)
-    o_ref[own, :] = f1[pl.ds(mine_x, piece), :] + rx[...]
-
-    c = remote(o_ref.at[own], o_ref.at[own], px)
-    c.wait_recv()
-
     own_chunk = pl.ds(pl.multiple_of(core * half + z * chunk, 8), chunk)
+    o_ref[own_chunk, :] = f1[...] + rx[...]
+
     to_core = [remote(o_ref.at[own_chunk], o_ref.at[own_chunk], pc)]
 
     def grows(j, q):
@@ -214,7 +206,7 @@
             vmem((half, cols), a.dtype),
             vmem((half, cols), a.dtype),
             vmem((chunk, cols), a.dtype),
-            vmem((chunk // 2, cols), a.dtype),
+            vmem((chunk, cols), a.dtype),
             vmem((nz - 1, chunk, lanes), a.dtype),
             vmem((nz - 1, chunk, lanes), a.dtype),
             vmem((nz - 1, chunk, lanes), a.dtype),

time: 106 us -> 102 us (0.962)
  Pallas kernels: 87.4 us -> 83.6 us
    pallas_call x1, Pallas kernels: 70.7 us -> 66.9 us  [dp_allreduce(): pl.pallas_call(functools.partial(_allreduce_kernel, axis_names, nz, nc, S...]
where the time goes in v7:
time: 102 us
  Pallas kernels  83.6 us (82%)
  matrix products  10.2 us (10%)
  local copies, waits for them, and re-layouts  5.96 us (6%)
  other arithmetic  1.56 us (2%)
    pallas_call x1, Pallas kernels, dp_allreduce(): pl.pallas_call(functools.partial(_allreduce_kernel, axis_names, nz, nc, S...  66.9 us
    pallas_call x1, Pallas kernels, chan_allgather(): pl.pallas_call(functools.partial(_allgather_kernel, axis_names, n), out_s...  16.7 us
    dot_general x9, matrix products, on_device(): lax.dot_general(columns, displaced_input[tap_index], contract_rows, prefe...  3.53 us
    dot_general x9, matrix products, on_device(): lax.dot_general(displaced_input[tap_index], flat_grads, contract_cols, pr...  3.39 us
    dot_general x9, matrix products, on_device(): jnp.dot(weight[:, tap_index, :], displaced_gradient, preferred_element_ty...  3.25 us
    unnamed x9, local copies, waits for them, and re-layouts  3.18 us

profile of v7, /device:TPU:1, one launch (start us, length us, event | category | flops | bytes accessed | tf_op | source)
XLA Modules:
  0.0 102.1 jit_solution(10529127315980562718)
XLA Ops:
  0.6 16.7 %shard_map.58 = bf16[256,1152]{1,0:T(8,128)(2,1)} custom-call(bf16[32,1152]{1,0:T(8,128)(2,1)} %bitcast.195), custom_call_target="tpu_custom_call" | custom-call | tf_op jit(solution)/shard_map/pallas_call | solution.py:263
  17.3 1.3 %copy.25 = bf16[256,1152]{0,1:T(8,128)(2,1)S(1)} copy(bf16[256,1152]{1,0:T(8,128)(2,1)} %shard_map.58) | data formatting | bytes 1179648 | tf_op jit(solution)/shard_map/pallas_call | solution.py:263
  18.6 0.7 pad_slice_fusion.4
  19.4 0.5 copy-done.2
  22.7 0.7 copy-done
  23.4 0.5 fusion.11
  23.9 1.1 %copy.27 = bf16[1,256,1152]{2,1,0:T(8,128)(2,1)} copy(bf16[1,256,1152]{1,2,0:T(8,128)(2,1)S(1)} %fusion.11) | data formatting | bytes 1179648
  25.2 0.7 pad_slice_fusion.8
  26.0 0.4 fusion.20
  26.4 0.4 fusion.19
  26.7 0.4 fusion.18
  27.1 0.4 fusion.17
  27.9 0.4 fusion.15
  28.3 0.4 fusion.14
  28.7 0.4 fusion.13
  29.1 0.4 fusion.12
  29.8 0.4 convolution_add_fusion.7
  30.2 0.4 convolution_add_fusion.6
  30.6 0.4 fusion.8
  31.3 0.4 convolution_bitcast_fusion.5
  32.5 0.5 fusion.3.t_ref
  33.0 66.9 %shard_map.59 = (f32[2304,256]{1,0:T(8,128)S(1)}, bf16[32,1152]{1,0:T(8,128)(2,1)S(1)}) custom-call(f32[2304,256]{1,0:T(8,128)S(1)} %bitcast.166, f32[256,1152]{1,0:T(8,128)S(1)} %fusion.3.t_ref), custom_call_target="tpu_custom_call" | custom-call | tf_op jit(solution)/shard_map/pallas_call | solution.py:197
  99.9 1.6 %broadcast_multiply_fusion = f32[2304,256]{1,0:T(8,128)} fusion(f32[2304,256]{1,0:T(8,128)S(1)} %get-tuple-element.6), kind=kLoop, calls=%fused_computation.44 | loop fusion | flops 589824 | bytes 4718592 | tf_op jit(solution)/shard_map/div | solution.py:318
  101.5 0.6 copy.46
  (18 shorter events, 4.9 us)
Async XLA Ops:
  18.6 1.3 %copy-start.2 = (bf16[256,9,256]{2,0,1:T(8,128)(2,1)S(1)}, bf16[256,9,256]{2,0,1:T(8,128)(2,1)}, u32[]{:S(2)}) copy-start(bf16[256,9,256]{2,0,1:T(8,128)(2,1)} %param.4) | copy-start | bytes 3538948
  22.3 1.1 %copy-start = (bf16[256,1152]{1,0:T(8,128)(2,1)S(1)}, bf16[256,1152]{1,0:T(8,128)(2,1)}, u32[]{:S(2)}) copy-start(bf16[256,1152]{1,0:T(8,128)(2,1)} %shard_map.58) | copy-start | bytes 1769476
  23.9 1.1 %copy-start.1 = (bf16[1,256,1152]{2,1,0:T(8,128)(2,1)S(1)}, bf16[1,256,1152]{2,1,0:T(8,128)(2,1)}, u32[]{:S(2)}) copy-start(bf16[1,256,1152]{2,1,0:T(8,128)(2,1)} %param.3) | copy-start | bytes 1769476

commit v8 on v7

--- a/solution.py
+++ b/solution.py
@@ -10,7 +10,7 @@
 DILATION_RATE = 12
 MAP_HEIGHT = 16
 MAP_WIDTH = 72
-STREAMS = 3
+STREAMS = 6
 
 
 def translated_input(receptive_field, row_shift, column_shift, reach):

time: 102 us -> 103 us (level)
  no operation moved by 1% of the time
where the time goes in v8:
time: 103 us
  Pallas kernels  84.1 us (82%)
  matrix products  10.2 us (10%)
  local copies, waits for them, and re-layouts  5.96 us (6%)
  other arithmetic  1.56 us (2%)
    pallas_call x1, Pallas kernels, dp_allreduce(): pl.pallas_call(functools.partial(_allreduce_kernel, axis_names, nz, nc, S...  67.4 us
    pallas_call x1, Pallas kernels, chan_allgather(): pl.pallas_call(functools.partial(_allgather_kernel, axis_names, n), out_s...  16.7 us
    dot_general x9, matrix products, on_device(): lax.dot_general(columns, displaced_input[tap_index], contract_rows, prefe...  3.53 us
    dot_general x9, matrix products, on_device(): lax.dot_general(displaced_input[tap_index], flat_grads, contract_cols, pr...  3.39 us
    dot_general x9, matrix products, on_device(): jnp.dot(weight[:, tap_index, :], displaced_gradient, preferred_element_ty...  3.25 us
    unnamed x9, local copies, waits for them, and re-layouts  3.18 us

profile of v8, /device:TPU:1, one launch (start us, length us, event | category | flops | bytes accessed | tf_op | source)
XLA Modules:
  0.0 102.7 jit_solution(9555775425585648362)
XLA Ops:
  0.6 16.7 %shard_map.58 = bf16[256,1152]{1,0:T(8,128)(2,1)} custom-call(bf16[32,1152]{1,0:T(8,128)(2,1)} %bitcast.195), custom_call_target="tpu_custom_call" | custom-call | tf_op jit(solution)/shard_map/pallas_call | solution.py:263
  17.3 1.3 %copy.25 = bf16[256,1152]{0,1:T(8,128)(2,1)S(1)} copy(bf16[256,1152]{1,0:T(8,128)(2,1)} %shard_map.58) | data formatting | bytes 1179648 | tf_op jit(solution)/shard_map/pallas_call | solution.py:263
  18.6 0.7 pad_slice_fusion.4
  19.4 0.5 copy-done.2
  22.7 0.7 copy-done
  23.4 0.5 fusion.11
  23.9 1.1 %copy.27 = bf16[1,256,1152]{2,1,0:T(8,128)(2,1)} copy(bf16[1,256,1152]{1,2,0:T(8,128)(2,1)S(1)} %fusion.11) | data formatting | bytes 1179648
  25.2 0.7 pad_slice_fusion.8
  26.0 0.4 fusion.20
  26.4 0.4 fusion.19
  26.7 0.4 fusion.18
  27.1 0.4 fusion.17
  27.9 0.4 fusion.15
  28.3 0.4 fusion.14
  28.7 0.4 fusion.13
  29.1 0.4 fusion.12
  29.8 0.4 convolution_add_fusion.7
  30.2 0.4 convolution_add_fusion.6
  30.6 0.4 fusion.8
  31.3 0.4 convolution_bitcast_fusion.5
  32.5 0.5 fusion.3.t_ref
  33.0 67.4 %shard_map.59 = (f32[2304,256]{1,0:T(8,128)S(1)}, bf16[32,1152]{1,0:T(8,128)(2,1)S(1)}) custom-call(f32[2304,256]{1,0:T(8,128)S(1)} %bitcast.166, f32[256,1152]{1,0:T(8,128)S(1)} %fusion.3.t_ref), custom_call_target="tpu_custom_call" | custom-call | tf_op jit(solution)/shard_map/pallas_call | solution.py:197
  100.5 1.6 %broadcast_multiply_fusion = f32[2304,256]{1,0:T(8,128)} fusion(f32[2304,256]{1,0:T(8,128)S(1)} %get-tuple-element.6), kind=kLoop, calls=%fused_computation.44 | loop fusion | flops 589824 | bytes 4718592 | tf_op jit(solution)/shard_map/div | solution.py:318
  102.0 0.6 copy.46
  (18 shorter events, 4.9 us)
Async XLA Ops:
  18.6 1.3 %copy-start.2 = (bf16[256,9,256]{2,0,1:T(8,128)(2,1)S(1)}, bf16[256,9,256]{2,0,1:T(8,128)(2,1)}, u32[]{:S(2)}) copy-start(bf16[256,9,256]{2,0,1:T(8,128)(2,1)} %param.4) | copy-start | bytes 3538948
  22.3 1.1 %copy-start = (bf16[256,1152]{1,0:T(8,128)(2,1)S(1)}, bf16[256,1152]{1,0:T(8,128)(2,1)}, u32[]{:S(2)}) copy-start(bf16[256,1152]{1,0:T(8,128)(2,1)} %shard_map.58) | copy-start | bytes 1769476
  23.9 1.1 %copy-start.1 = (bf16[1,256,1152]{2,1,0:T(8,128)(2,1)S(1)}, bf16[1,256,1152]{2,1,0:T(8,128)(2,1)}, u32[]{:S(2)}) copy-start(bf16[1,256,1152]{2,1,0:T(8,128)(2,1)} %param.3) | copy-start | bytes 1769476

commit v9 on v7

--- a/solution.py
+++ b/solution.py
@@ -270,6 +270,18 @@
     )(x)
 
 
+def permute_allgather(x):
+    n = lax.axis_size("chan")
+    me = lax.axis_index("chan")
+    rows = x.shape[0]
+    out = jnp.zeros((n * rows,) + x.shape[1:], x.dtype)
+    out = lax.dynamic_update_slice_in_dim(out, x, me * rows, axis=0)
+    for k in range(1, n):
+        got = lax.ppermute(x, "chan", [(j, (j + k) % n) for j in range(n)])
+        out = lax.dynamic_update_slice_in_dim(out, got, ((me + n - k) % n) * rows, axis=0)
+    return out
+
+
 def on_device(axis_names, inputs, weight, cotangent):
     input_channels_local = inputs.shape[1]
     cout_local = cotangent.shape[1]
@@ -287,7 +299,7 @@
         )
         for first_operand, second_operand in tap_shifts
     ]
-    flat_grads = chan_allgather(cotangent[0], axis_names)
+    flat_grads = permute_allgather(cotangent[0])
     contract_cols = (((1,), (1,)), ((), ()))
     local_grad = jnp.stack(
         [

time: 102 us -> 167 us (1.64); the launches traced: 102 us -> 165 us
  local copies, waits for them, and re-layouts: 5.96 us -> 45.8 us
  starting transfers between devices: 0 us -> 14.1 us
  matrix products: 10.2 us -> 22.2 us
  Pallas kernels: 83.6 us -> 73.9 us
  waiting for transfers between devices: 0 us -> 6.42 us
    dynamic_update_slice x0 -> x8, local copies, waits for them, and re-layouts: none -> 35.7 us  [the longest x7 31.4 us: permute_allgather(): lax.dynamic_update_slice_in_dim(out, got, (me + n - k) % n * rows, axis=0)]
    pallas_call x1 -> x0, Pallas kernels: 16.7 us -> none  [chan_allgather(): pl.pallas_call(functools.partial(_allgather_kernel, axis_names, n), out_s...]
    ppermute x0 -> x7, starting transfers between devices: none -> 14.1 us  [permute_allgather(): got = lax.ppermute(x, 'chan', [(j, (j + k) % n) for j in range(n)])]
    dot_general x9, matrix products: 3.39 us -> 13.7 us  [on_device(): lax.dot_general(displaced_input[tap_index], flat_grads, contract_cols, pr...]
    pallas_call x1, Pallas kernels: 66.9 us -> 73.9 us  [dp_allreduce(): pl.pallas_call(functools.partial(_allreduce_kernel, axis_names, nz, nc, S...]
    ppermute x0 -> x7, waiting for transfers between devices: none -> 6.42 us  [permute_allgather(): got = lax.ppermute(x, 'chan', [(j, (j + k) % n) for j in range(n)])]
    unnamed x9 -> x40, local copies, waits for them, and re-layouts: 3.18 us -> 5.66 us
    slice x2, local copies, waits for them, and re-layouts: 1.48 us -> 3.56 us  [translated_input(): bordered_input[:, reach + row_shift:reach + row_shift + height, reach + c...]
  transfers between devices with their start and end apart: 0 -> 7, of which waited for: 0 -> 1; matrix products, arithmetic and copies ran while one was open for 0% -> 22% of each run, Pallas kernels for 0% -> 0%
where the time goes in v9:
time: 167 us; the launch traced here: 165 us
  Pallas kernels  73.9 us (44%)
  local copies, waits for them, and re-layouts  45.8 us (27%)
  matrix products  22.2 us (13%)
  starting transfers between devices  14.1 us (8%)
  waiting for transfers between devices  6.42 us (4%)
    pallas_call x1, Pallas kernels, dp_allreduce(): pl.pallas_call(functools.partial(_allreduce_kernel, axis_names, nz, nc, S...  73.9 us
    dynamic_update_slice x7, local copies, waits for them, and re-layouts, permute_allgather(): lax.dynamic_update_slice_in_dim(out, got, (me + n - k) % n * rows, axis=0)  31.4 us
    ppermute x7, starting transfers between devices, permute_allgather(): got = lax.ppermute(x, 'chan', [(j, (j + k) % n) for j in range(n)])  14.1 us
    dot_general x9, matrix products, on_device(): lax.dot_general(displaced_input[tap_index], flat_grads, contract_cols, pr...  13.7 us
    ppermute x7, waiting for transfers between devices, permute_allgather(): got = lax.ppermute(x, 'chan', [(j, (j + k) % n) for j in range(n)])  6.42 us
    unnamed x40, local copies, waits for them, and re-layouts  5.66 us
    dot_general x9, matrix products, on_device(): jnp.dot(weight[:, tap_index, :], displaced_gradient, preferred_element_ty...  5 us
    dynamic_update_slice x1, local copies, waits for them, and re-layouts, permute_allgather(): out = lax.dynamic_update_slice_in_dim(out, x, me * rows, axis=0)  4.29 us
  transfers between devices with their start and end apart: 7, of which 1 were waited for; matrix products, arithmetic and copies ran while one was open for 22% of the time, Pallas kernels for 0%

profile of v9, /device:TPU:1, one launch (start us, length us, event | category | flops | bytes accessed | tf_op | source)
XLA Modules:
  0.0 165.2 jit_solution(5054054147127561047)
XLA Ops:
  1.7 3.6 %collective-permute-start = (bf16[32,1152]{0,1:T(8,128)(2,1)S(1)}, bf16[32,1152]{0,1:T(8,128)(2,1)S(1)}, u32[]{:S(2)}, u32[]{:S(2)}) collective-permute-start(bf16[32,1152]{0,1:T(8,128)(2,1)S(1)} %bitcast.188), channel_id=1, source_target_pairs={{0,1},{1,2},{2,3},{3,4},{4,5},{5,6},{6,7},{7,0},{8,9},{9,10},{10,1... | collective-permute-start | bytes 221192 | tf_op jit(solution)/shard_map/ppermute | solution.py:280
  6.7 2.0 %collective-permute-start.2 = (bf16[32,1152]{0,1:T(8,128)(2,1)S(1)}, bf16[32,1152]{0,1:T(8,128)(2,1)S(1)}, u32[]{:S(2)}, u32[]{:S(2)}) collective-permute-start(bf16[32,1152]{0,1:T(8,128)(2,1)S(1)} %bitcast.190), channel_id=1, source_target_pairs={{0,3},{1,4},{2,5},{3,6},{4,7},{5,0},{6,1},{7,2},{8,11},{9,12},{10,... | collective-permute-start | bytes 221192 | tf_op jit(solution)/shard_map/ppermute | solution.py:280
  8.6 1.6 collective-permute-start.3
  10.2 4.5 %collective-permute-start.4 = (bf16[32,1152]{0,1:T(8,128)(2,1)S(1)}, bf16[32,1152]{0,1:T(8,128)(2,1)S(1)}, u32[]{:S(2)}, u32[]{:S(2)}) collective-permute-start(bf16[32,1152]{0,1:T(8,128)(2,1)S(1)} %bitcast.192), channel_id=1, source_target_pairs={{0,5},{1,6},{2,7},{3,0},{4,1},{5,2},{6,3},{7,4},{8,13},{9,14},{10,... | collective-permute-start | bytes 221192 | tf_op jit(solution)/shard_map/ppermute | solution.py:280
  21.5 6.4 %collective-permute-done.1 = bf16[32,1152]{0,1:T(8,128)(2,1)S(1)} collective-permute-done((bf16[32,1152]{0,1:T(8,128)(2,1)S(1)}, bf16[32,1152]{0,1:T(8,128)(2,1)S(1)}, u32[]{:S(2)}, u32[]{:S(2)}) %collective-permute-start.1) | collective-permute-done | bytes 73760 | tf_op jit(solution)/shard_map/ppermute | solution.py:280
  29.4 4.3 %dynamic_update_slice.24 = bf16[256,1152]{0,1:T(8,128)(2,1)} dynamic-update-slice(bf16[256,1152]{0,1:T(8,128)(2,1)} %broadcast_in_dim.3, bf16[32,1152]{0,1:T(8,128)(2,1)S(1)} %bitcast.195, s32[]{:T(128)S(6)} %select_n.55, s32[]{:T(128)} %constant.68.clone.1) | dynamic-update-slice | bytes 147460 | tf_op jit(solution)/shard_map/dynamic_update_slice | solution.py:278
  33.7 4.3 %dynamic_update_slice.25 = bf16[256,1152]{0,1:T(8,128)(2,1)} dynamic-update-slice(bf16[256,1152]{0,1:T(8,128)(2,1)} %dynamic_update_slice.24, bf16[32,1152]{0,1:T(8,128)(2,1)S(1)} %collective-permute-done, s32[]{:T(128)S(6)} %select_n.57, s32[]{:T(128)} %constant.68.clone.1) | dynamic-update-slice | bytes 147460 | tf_op jit(solution)/shard_map/dynamic_update_slice | solution.py:281
  38.0 4.3 %dynamic_update_slice.26 = bf16[256,1152]{0,1:T(8,128)(2,1)} dynamic-update-slice(bf16[256,1152]{0,1:T(8,128)(2,1)} %dynamic_update_slice.25, bf16[32,1152]{0,1:T(8,128)(2,1)S(1)} %collective-permute-done.1, s32[]{:T(128)S(6)} %select_n.59, s32[]{:T(128)} %constant.68.clone.1) | dynamic-update-slice | bytes 147460 | tf_op jit(solution)/shard_map/dynamic_update_slice | solution.py:281
  42.3 4.3 %dynamic_update_slice.27 = bf16[256,1152]{0,1:T(8,128)(2,1)} dynamic-update-slice(bf16[256,1152]{0,1:T(8,128)(2,1)} %dynamic_update_slice.26, bf16[32,1152]{0,1:T(8,128)(2,1)S(1)} %collective-permute-done.2, s32[]{:T(128)S(6)} %select_n.61, s32[]{:T(128)} %constant.68.clone.1) | dynamic-update-slice | bytes 147460 | tf_op jit(solution)/shard_map/dynamic_update_slice | solution.py:281
  46.6 3.7 %dynamic_update_slice.28 = bf16[256,1152]{0,1:T(8,128)(2,1)} dynamic-update-slice(bf16[256,1152]{0,1:T(8,128)(2,1)} %dynamic_update_slice.27, bf16[32,1152]{0,1:T(8,128)(2,1)S(1)} %collective-permute-done.3, s32[]{:T(128)S(6)} %select_n.63, s32[]{:T(128)} %constant.68.clone.1) | dynamic-update-slice | bytes 147460 | tf_op jit(solution)/shard_map/dynamic_update_slice | solution.py:281
  50.3 4.9 %dynamic_update_slice.29 = bf16[256,1152]{0,1:T(8,128)(2,1)} dynamic-update-slice(bf16[256,1152]{0,1:T(8,128)(2,1)} %dynamic_update_slice.28, bf16[32,1152]{0,1:T(8,128)(2,1)S(1)} %collective-permute-done.4, s32[]{:T(128)S(6)} %select_n.65, s32[]{:T(128)} %constant.68.clone.1) | dynamic-update-slice | bytes 147460 | tf_op jit(solution)/shard_map/dynamic_update_slice | solution.py:281
  55.2 4.9 %dynamic_update_slice.30 = bf16[256,1152]{0,1:T(8,128)(2,1)} dynamic-update-slice(bf16[256,1152]{0,1:T(8,128)(2,1)} %dynamic_update_slice.29, bf16[32,1152]{0,1:T(8,128)(2,1)S(1)} %collective-permute-done.5, s32[]{:T(128)S(6)} %select_n.67, s32[]{:T(128)} %constant.68.clone.1) | dynamic-update-slice | bytes 147460 | tf_op jit(solution)/shard_map/dynamic_update_slice | solution.py:281
  60.2 4.9 %dynamic_update_slice.31 = bf16[256,1152]{0,1:T(8,128)(2,1)} dynamic-update-slice(bf16[256,1152]{0,1:T(8,128)(2,1)} %dynamic_update_slice.30, bf16[32,1152]{0,1:T(8,128)(2,1)S(1)} %collective-permute-done.6, s32[]{:T(128)S(6)} %select_n.69, s32[]{:T(128)} %constant.68.clone.1) | dynamic-update-slice | bytes 147460 | tf_op jit(solution)/shard_map/dynamic_update_slice | solution.py:281
  65.1 1.6 fusion.16
  66.7 2.8 %pad_slice_fusion = (bf16[256,16,72]{0,2,1:T(8,128)(2,1)S(1)}, bf16[256,16,72]{0,2,1:T(8,128)(2,1)S(1)}, bf16[256,16,72]{0,2,1:T(8,128)(2,1)S(1)}, bf16[256,16,7...) fusion(bf16[256,16,72]{0,2,1:T(8,128)(2,1)} %bitcast.37), kind=kLoop, calls=%fused_computation | loop fusion | bytes 5308416 | tf_op jit(solution)/shard_map/slice | solution.py:19
  74.6 2.1 %copy.25 = bf16[1,256,1152]{2,1,0:T(8,128)(2,1)} copy(bf16[1,256,1152]{1,2,0:T(8,128)(2,1)} %fusion.7) | data formatting | bytes 1179648
  76.7 1.7 %fusion.15 = f32[9,256,256]{2,1,0:T(8,128)S(1)} fusion(f32[9,256,256]{2,1,0:T(8,128)S(1)} %fusion.16, bf16[256,1152]{0,1:T(8,128)(2,1)} %bitcast.178, bf16[256,1152]{0,1:T(8,128)(2,1)} %dynamic_update_slice.31), kind=kOutput, calls=%fused_computation.55 | convolution fusion | flops 150994944 | bytes 1441792 | tf_op jit(solution)/shard_map/dot_general | solution.py:306
  78.5 1.5 fusion.14
  80.0 1.5 fusion.13
  81.5 1.5 fusion.8
  83.0 1.5 fusion.12
  84.6 1.5 fusion.11
  89.0 73.9 %shard_map.58 = (f32[2304,256]{1,0:T(8,128)S(1)}, bf16[32,1152]{1,0:T(8,128)(2,1)S(1)}) custom-call(f32[2304,256]{1,0:T(8,128)S(1)} %bitcast.160, f32[256,1152]{1,0:T(8,128)S(1)} %fusion.3.t_ref), custom_call_target="tpu_custom_call" | custom-call | tf_op jit(solution)/shard_map/pallas_call | solution.py:197
  163.0 1.6 broadcast_multiply_fusion
  (70 shorter events, 18.9 us)
Async XLA Ops:
  1.7 18.7 %collective-permute-start = (bf16[32,1152]{0,1:T(8,128)(2,1)S(1)}, bf16[32,1152]{0,1:T(8,128)(2,1)S(1)}, u32[]{:S(2)}, u32[]{:S(2)}) collective-permute-start(bf16[32,1152]{0,1:T(8,128)(2,1)S(1)} %bitcast.188), channel_id=1, source_target_pairs={{0,1},{1,2},{2,3},{3,4},{4,5},{5,6},{6,7},{7,0},{8,9},{9,10},{10,1... | collective-permute-start | bytes 221192 | tf_op jit(solution)/shard_map/ppermute | solution.py:280
  5.4 22.6 %collective-permute-start.1 = (bf16[32,1152]{0,1:T(8,128)(2,1)S(1)}, bf16[32,1152]{0,1:T(8,128)(2,1)S(1)}, u32[]{:S(2)}, u32[]{:S(2)}) collective-permute-start(bf16[32,1152]{0,1:T(8,128)(2,1)S(1)} %bitcast.189), channel_id=1, source_target_pairs={{0,2},{1,3},{2,4},{3,5},{4,6},{5,7},{6,0},{7,1},{8,10},{9,11},{10,... | collective-permute-start | bytes 221192 | tf_op jit(solution)/shard_map/ppermute | solution.py:280
  6.7 35.6 %collective-permute-start.2 = (bf16[32,1152]{0,1:T(8,128)(2,1)S(1)}, bf16[32,1152]{0,1:T(8,128)(2,1)S(1)}, u32[]{:S(2)}, u32[]{:S(2)}) collective-permute-start(bf16[32,1152]{0,1:T(8,128)(2,1)S(1)} %bitcast.190), channel_id=1, source_target_pairs={{0,3},{1,4},{2,5},{3,6},{4,7},{5,0},{6,1},{7,2},{8,11},{9,12},{10,... | collective-permute-start | bytes 221192 | tf_op jit(solution)/shard_map/ppermute | solution.py:280
  8.6 38.0 %collective-permute-start.3 = (bf16[32,1152]{0,1:T(8,128)(2,1)S(1)}, bf16[32,1152]{0,1:T(8,128)(2,1)S(1)}, u32[]{:S(2)}, u32[]{:S(2)}) collective-permute-start(bf16[32,1152]{0,1:T(8,128)(2,1)S(1)} %bitcast.191), channel_id=1, source_target_pairs={{0,4},{1,5},{2,6},{3,7},{4,0},{5,1},{6,2},{7,3},{8,12},{9,13},{10,... | collective-permute-start | bytes 221192 | tf_op jit(solution)/shard_map/ppermute | solution.py:280
  10.2 40.1 %collective-permute-start.4 = (bf16[32,1152]{0,1:T(8,128)(2,1)S(1)}, bf16[32,1152]{0,1:T(8,128)(2,1)S(1)}, u32[]{:S(2)}, u32[]{:S(2)}) collective-permute-start(bf16[32,1152]{0,1:T(8,128)(2,1)S(1)} %bitcast.192), channel_id=1, source_target_pairs={{0,5},{1,6},{2,7},{3,0},{4,1},{5,2},{6,3},{7,4},{8,13},{9,14},{10,... | collective-permute-start | bytes 221192 | tf_op jit(solution)/shard_map/ppermute | solution.py:280
  16.0 1.3 copy-start.2
  16.7 1.3 copy-start.4
  16.8 1.6 copy-start.8
  16.8 2.0 %copy-start.17 = (bf16[256,16,72]{0,2,1:T(8,128)(2,1)}, bf16[256,16,72]{0,2,1:T(8,128)(2,1)S(1)}, u32[]{:S(2)}) copy-start(bf16[256,16,72]{0,2,1:T(8,128)(2,1)S(1)} %get-tuple-element.28) | copy-start | bytes 1769476
  16.8 2.0 %copy-start.16 = (bf16[256,16,72]{0,2,1:T(8,128)(2,1)}, bf16[256,16,72]{0,2,1:T(8,128)(2,1)S(1)}, u32[]{:S(2)}) copy-start(bf16[256,16,72]{0,2,1:T(8,128)(2,1)S(1)} %get-tuple-element.22) | copy-start | bytes 1769476
  16.8 2.4 %copy-start.14 = (bf16[256,16,72]{0,2,1:T(8,128)(2,1)}, bf16[256,16,72]{0,2,1:T(8,128)(2,1)S(1)}, u32[]{:S(2)}) copy-start(bf16[256,16,72]{0,2,1:T(8,128)(2,1)S(1)} %get-tuple-element.23) | copy-start | bytes 1769476
  16.8 2.8 %copy-start.12 = (bf16[256,16,72]{0,2,1:T(8,128)(2,1)}, bf16[256,16,72]{0,2,1:T(8,128)(2,1)S(1)}, u32[]{:S(2)}) copy-start(bf16[256,16,72]{0,2,1:T(8,128)(2,1)S(1)} %get-tuple-element.24) | copy-start | bytes 1769476
  16.8 3.2 %copy-start.10 = (bf16[256,16,72]{0,2,1:T(8,128)(2,1)}, bf16[256,16,72]{0,2,1:T(8,128)(2,1)S(1)}, u32[]{:S(2)}) copy-start(bf16[256,16,72]{0,2,1:T(8,128)(2,1)S(1)} %get-tuple-element.25) | copy-start | bytes 1769476
  20.0 8.0 %copy-start = (bf16[1,256,1152]{2,1,0:T(8,128)(2,1)S(1)}, bf16[1,256,1152]{2,1,0:T(8,128)(2,1)}, u32[]{:S(2)}) copy-start(bf16[1,256,1152]{2,1,0:T(8,128)(2,1)} %param.3) | copy-start | bytes 1769476
  20.4 34.8 %collective-permute-start.5 = (bf16[32,1152]{0,1:T(8,128)(2,1)S(1)}, bf16[32,1152]{0,1:T(8,128)(2,1)S(1)}, u32[]{:S(2)}, u32[]{:S(2)}) collective-permute-start(bf16[32,1152]{0,1:T(8,128)(2,1)S(1)} %bitcast.193), channel_id=1, source_target_pairs={{0,6},{1,7},{2,0},{3,1},{4,2},{5,3},{6,4},{7,5},{8,14},{9,15},{10,... | collective-permute-start | bytes 221192 | tf_op jit(solution)/shard_map/ppermute | solution.py:280
  27.9 32.2 %collective-permute-start.6 = (bf16[32,1152]{0,1:T(8,128)(2,1)S(1)}, bf16[32,1152]{0,1:T(8,128)(2,1)S(1)}, u32[]{:S(2)}, u32[]{:S(2)}) collective-permute-start(bf16[32,1152]{0,1:T(8,128)(2,1)S(1)} %bitcast.194), channel_id=1, source_target_pairs={{0,7},{1,0},{2,1},{3,2},{4,3},{5,4},{6,5},{7,6},{8,15},{9,8},{10,9... | collective-permute-start | bytes 221192 | tf_op jit(solution)/shard_map/ppermute | solution.py:280
  66.7 2.8 %copy-start.3 = (bf16[256,9,256]{2,0,1:T(8,128)(2,1)S(1)}, bf16[256,9,256]{2,0,1:T(8,128)(2,1)}, u32[]{:S(2)}) copy-start(bf16[256,9,256]{2,0,1:T(8,128)(2,1)} %param.4) | copy-start | bytes 3538948
  76.7 1.7 %copy-start.15 = (bf16[256,16,72]{0,2,1:T(8,128)(2,1)S(1)}, bf16[256,16,72]{0,2,1:T(8,128)(2,1)}, u32[]{:S(2)}) copy-start(bf16[256,16,72]{0,2,1:T(8,128)(2,1)} %copy-done.14) | copy-start | bytes 1769476
  76.7 3.3 %copy-start.13 = (bf16[256,16,72]{0,2,1:T(8,128)(2,1)S(1)}, bf16[256,16,72]{0,2,1:T(8,128)(2,1)}, u32[]{:S(2)}) copy-start(bf16[256,16,72]{0,2,1:T(8,128)(2,1)} %copy-done.12) | copy-start | bytes 1769476
  78.5 3.1 %copy-start.1 = (bf16[1,256,1152]{2,1,0:T(8,128)(2,1)S(1)}, bf16[1,256,1152]{2,1,0:T(8,128)(2,1)}, u32[]{:S(2)}) copy-start(bf16[1,256,1152]{2,1,0:T(8,128)(2,1)} %param.3) | copy-start | bytes 1769476
  80.0 3.0 %copy-start.11 = (bf16[256,16,72]{0,2,1:T(8,128)(2,1)S(1)}, bf16[256,16,72]{0,2,1:T(8,128)(2,1)}, u32[]{:S(2)}) copy-start(bf16[256,16,72]{0,2,1:T(8,128)(2,1)} %copy-done.10) | copy-start | bytes 1769476
  81.5 3.0 %copy-start.9 = (bf16[256,16,72]{0,2,1:T(8,128)(2,1)S(1)}, bf16[256,16,72]{0,2,1:T(8,128)(2,1)}, u32[]{:S(2)}) copy-start(bf16[256,16,72]{0,2,1:T(8,128)(2,1)} %copy-done.8) | copy-start | bytes 1769476
  83.0 3.1 %copy-start.7 = (bf16[256,16,72]{0,2,1:T(8,128)(2,1)S(1)}, bf16[256,16,72]{0,2,1:T(8,128)(2,1)}, u32[]{:S(2)}) copy-start(bf16[256,16,72]{0,2,1:T(8,128)(2,1)} %copy-done.6) | copy-start | bytes 1769476
  84.6 3.0 %copy-start.5 = (bf16[256,16,72]{0,2,1:T(8,128)(2,1)S(1)}, bf16[256,16,72]{0,2,1:T(8,128)(2,1)}, u32[]{:S(2)}) copy-start(bf16[256,16,72]{0,2,1:T(8,128)(2,1)} %copy-done.4) | copy-start | bytes 1769476
  (1 other events, 1.3 us)

commit v10 on v7

--- a/solution.py
+++ b/solution.py
@@ -23,8 +23,9 @@
     ]
 
 
-def _allreduce_kernel(axis_names, nz, nc, streams, a_ref, t_ref, o_ref, res_ref, rc, s1, f1, rx, rp, rm,
-                      ap, am, rs_buf, send_sems, recv_sems, rs_send, rs_recv):
+def _allreduce_kernel(axis_names, nz, nc, streams, a_ref, t_ref, w_ref, g_ref, o_ref, res_ref,
+                      ig_ref, rc, s1, f1, rx, rp, rm, ap, am, rs_buf, ig_acc, send_sems, recv_sems,
+                      rs_send, rs_recv):
     rows, cols = a_ref.shape
     half = rows // 2
     chunk = half // nz
@@ -81,6 +82,19 @@
 
     def rows_of(j):
         return pl.ds(pl.multiple_of(j * chunk, 8), chunk)
+
+    taps = w_ref.shape[0]
+    done_taps = [0]
+
+    def input_grad_tap():
+        t = done_taps[0]
+        if t < taps:
+            term = jnp.dot(w_ref[t], g_ref[t], preferred_element_type=jnp.float32)
+            if t == 0:
+                ig_acc[...] = term
+            else:
+                ig_acc[...] += term
+            done_taps[0] += 1
 
     mine_c = core * half
     other_c = (1 - core) * half
@@ -168,6 +182,10 @@
             gm = grows(jm, q)
             pending[q] = (remote(o_ref.at[gp, lo], o_ref.at[gp, lo], zr),
                           remote(o_ref.at[gm, hi], o_ref.at[gm, hi], zl))
+        input_grad_tap()
+        if s == nz - 2:
+            while done_taps[0] < taps:
+                input_grad_tap()
     for q in range(streams):
         arrived(q, (z + 2) % nz, (z + nz - 2) % nz)
     for c in to_core:
@@ -179,12 +197,13 @@
     for k in range(1, nc):
         acc = acc + rs_buf[k]
     res_ref[...] = acc.astype(res_ref.dtype)
+    ig_ref[...] = ig_acc[...].astype(ig_ref.dtype)
 
     for c in sent + rs_copies:
         c.wait_send()
 
 
-def dp_allreduce(a, t, axis_names):
+def dp_allreduce(a, t, w, g, axis_names):
     rows, cols = a.shape
     nc = lax.axis_size("chan")
     owned = t.shape[0] // nc
@@ -199,9 +218,10 @@
         out_shape=(
             jax.ShapeDtypeStruct((rows, cols), a.dtype),
             jax.ShapeDtypeStruct((owned, t.shape[1]), jnp.bfloat16),
+            jax.ShapeDtypeStruct((w.shape[1], g.shape[2]), jnp.bfloat16),
         ),
-        in_specs=[pl.BlockSpec(memory_space=vmem)] * 2,
-        out_specs=(pl.BlockSpec(memory_space=vmem), pl.BlockSpec(memory_space=vmem)),
+        in_specs=[pl.BlockSpec(memory_space=vmem)] * 4,
+        out_specs=(pl.BlockSpec(memory_space=vmem),) * 3,
         scratch_shapes=[
             vmem((half, cols), a.dtype),
             vmem((half, cols), a.dtype),
@@ -212,6 +232,7 @@
             vmem((nz - 1, chunk, lanes), a.dtype),
             vmem((nz - 1, chunk, lanes), a.dtype),
             vmem((nc, owned, t.shape[1]), t.dtype),
+            vmem((w.shape[1], g.shape[2]), jnp.float32),
             pltpu.SemaphoreType.DMA((n_copies,)),
             pltpu.SemaphoreType.DMA((n_copies,)),
             pltpu.SemaphoreType.DMA((nc,)),
@@ -220,7 +241,7 @@
         compiler_params=pltpu.CompilerParams(
             collective_id=0, has_side_effects=True, vmem_limit_bytes=48 * 1024 * 1024
         ),
-    )(a, t)
+    )(a, t, w, g)
 
 
 def _allgather_kernel(axis_names, n, x_ref, o_ref, send_sems, recv_sems):
@@ -308,26 +329,28 @@
         total = total + lax.dot_general(
             columns, displaced_input[tap_index], contract_rows, preferred_element_type=jnp.float32
         )
-    summed, owned = dp_allreduce(
-        local_grad.reshape(tap_list * input_channels_local, output_channels_total), total, axis_names
+    collected_input = flat_grads.reshape(output_channels_total, MAP_HEIGHT, MAP_WIDTH)
+    displaced_gradient = jnp.stack(
+        [
+            translated_input(collected_input, -row_shift, -column_shift, DILATION_RATE).reshape(
+                output_channels_total, tap_locations
+            )
+            for row_shift, column_shift in tap_shifts
+        ]
+    )
+    summed, owned, back = dp_allreduce(
+        local_grad.reshape(tap_list * input_channels_local, output_channels_total),
+        total,
+        jnp.transpose(weight, (1, 0, 2)),
+        displaced_gradient,
+        axis_names,
     )
     result = owned.reshape(1, cout_local, tap_locations)
     summed_grad = jnp.transpose(
         summed.reshape(tap_list, input_channels_local, output_channels_total), (1, 0, 2)
     )
     weight_grad = summed_grad / jnp.float32(lax.axis_size("dp"))
-
-    collected_input = flat_grads.reshape(output_channels_total, MAP_HEIGHT, MAP_WIDTH)
-    back_sum = jnp.zeros((input_channels_local, tap_locations), jnp.float32)
-    for tap_index in range(tap_list):
-        row_shift, column_shift = tap_shifts[tap_index]
-        displaced_gradient = translated_input(
-            collected_input, -row_shift, -column_shift, DILATION_RATE
-        ).reshape(output_channels_total, tap_locations)
-        back_sum = back_sum + jnp.dot(
-            weight[:, tap_index, :], displaced_gradient, preferred_element_type=jnp.float32
-        )
-    input_grad = back_sum.astype(jnp.bfloat16).reshape(1, input_channels_local, tap_locations)
+    input_grad = back.reshape(1, input_channels_local, tap_locations)
     return (result, input_grad, weight_grad)
 
 

time: 102 us -> 116 us (1.14)
  local copies, waits for them, and re-layouts: 5.96 us -> 19.5 us
  matrix products: 10.2 us -> 6.96 us
  Pallas kernels: 83.6 us -> 86.8 us
    another operation x0 -> x9, local copies, waits for them, and re-layouts: none -> 6.4 us  [on_device(): jnp.stack([translated_input(collected_input, -row_shift, -column_shift, D...]
    unnamed x9 -> x19, local copies, waits for them, and re-layouts: 3.18 us -> 9.34 us
    dot_general x9 -> x0, matrix products: 3.25 us -> none  [on_device(): jnp.dot(weight[:, tap_index, :], displaced_gradient, preferred_element_ty...]
    pallas_call x1, Pallas kernels: 66.9 us -> 70.1 us  [dp_allreduce(): pl.pallas_call(functools.partial(_allreduce_kernel, axis_names, nz, nc, S...]
where the time goes in v10:
time: 116 us
  Pallas kernels  86.8 us (75%)
  local copies, waits for them, and re-layouts  19.5 us (17%)
  matrix products  6.96 us (6%)
  other arithmetic  1.56 us (1%)
    pallas_call x1, Pallas kernels, dp_allreduce(): pl.pallas_call(functools.partial(_allreduce_kernel, axis_names, nz, nc, S...  70.1 us
    pallas_call x1, Pallas kernels, chan_allgather(): pl.pallas_call(functools.partial(_allgather_kernel, axis_names, n), out_s...  16.7 us
    unnamed x19, local copies, waits for them, and re-layouts  9.34 us
    another operation x9, local copies, waits for them, and re-layouts, on_device(): jnp.stack([translated_input(collected_input, -row_shift, -column_shift, D...  6.4 us
    dot_general x9, matrix products, on_device(): lax.dot_general(columns, displaced_input[tap_index], contract_rows, prefe...  3.56 us
    dot_general x9, matrix products, on_device(): lax.dot_general(displaced_input[tap_index], flat_grads, contract_cols, pr...  3.4 us
    slice x2, local copies, waits for them, and re-layouts, translated_input(): bordered_input[:, reach + row_shift:reach + row_shift + height, reach + c...  2.41 us

profile of v10, /device:TPU:1, one launch (start us, length us, event | category | flops | bytes accessed | tf_op | source)
XLA Modules:
  0.0 115.6 jit_solution(1201963423956723813)
XLA Ops:
  0.6 16.7 %shard_map.58 = bf16[256,1152]{1,0:T(8,128)(2,1)} custom-call(bf16[32,1152]{1,0:T(8,128)(2,1)} %bitcast.162), custom_call_target="tpu_custom_call" | custom-call | tf_op jit(solution)/shard_map/pallas_call | solution.py:284
  17.3 1.3 %copy.23 = bf16[256,1152]{0,1:T(8,128)(2,1)S(1)} copy(bf16[256,1152]{1,0:T(8,128)(2,1)} %shard_map.58) | data formatting | bytes 1179648 | tf_op jit(solution)/shard_map/pallas_call | solution.py:284
  18.6 1.7 %pad_slice_fusion = (bf16[256,16,72]{0,2,1:T(8,128)(2,1)S(1)}, bf16[256,16,72]{0,2,1:T(8,128)(2,1)S(1)}, bf16[256,16,72]{0,2,1:T(8,128)(2,1)}, bf16[256,16,72]{0...) fusion(bf16[256,16,72]{0,2,1:T(8,128)(2,1)S(1)} %bitcast.160), kind=kLoop, calls=%fused_computation | loop fusion | bytes 5308416 | tf_op jit(solution)/shard_map/slice | solution.py:19
  20.3 1.4 %copy.24 = bf16[1,256,1152]{2,1,0:T(8,128)(2,1)S(1)} copy(bf16[1,256,1152]{1,2,0:T(8,128)(2,1)} %bitcast.159) | data formatting | bytes 1179648 | tf_op jit(solution)/shard_map/stack;reshape | solution.py:333
  21.7 0.9 constant_dynamic-update-slice_fusion.7
  22.8 0.9 constant_dynamic-update-slice_fusion.6
  23.7 1.4 %copy.26 = bf16[1,256,1152]{2,1,0:T(8,128)(2,1)S(1)} copy(bf16[1,256,1152]{1,2,0:T(8,128)(2,1)} %bitcast.157) | data formatting | bytes 1179648 | tf_op jit(solution)/shard_map/stack;reshape | solution.py:333
  25.1 0.9 constant_dynamic-update-slice_fusion.5
  26.0 1.4 %copy.27 = bf16[1,256,1152]{2,1,0:T(8,128)(2,1)S(1)} copy(bf16[1,256,1152]{1,2,0:T(8,128)(2,1)} %bitcast.156) | data formatting | bytes 1179648 | tf_op jit(solution)/shard_map/stack;reshape | solution.py:333
  27.3 0.9 constant_dynamic-update-slice_fusion.4
  28.2 0.9 bitcast_dynamic-update-slice_fusion
  29.4 0.9 constant_dynamic-update-slice_fusion.3
  30.5 0.9 constant_dynamic-update-slice_fusion.2
  31.7 0.9 constant_dynamic-update-slice_fusion.1
  32.9 0.9 constant_dynamic-update-slice_fusion.g_ref
  34.0 0.7 pad_slice_fusion.8
  37.8 0.4 fusion.5
  38.7 0.4 convolution_add_fusion.3
  39.1 0.5 copy-done.3
  41.9 0.6 fusion.3.t_ref
  42.5 70.1 %shard_map.59 = (f32[2304,256]{1,0:T(8,128)S(1)}, bf16[32,1152]{1,0:T(8,128)(2,1)S(1)}, bf16[256,1152]{1,0:T(8,128)(2,1)S(1)}) custom-call(f32[2304,256]{1,0:T(8,128)} %bitcast.150, f32[256,1152]{1,0:T(8,128)S(1)} %fusion.3.t_ref, bf16[9,256,256]{2,1,0:T(8,128)(2,1)S(1)} %bitcast.131, bf16[9,256,1152]{2,1,0:T(8,128)(2,1)} %constant_dynamic-update-slice_fusion.g_ref), custom_call_target="tpu_custom_call" | custom-call | tf_op jit(solution)/shard_map/pallas_call | solution.py:216
  112.6 1.6 %broadcast_multiply_fusion = f32[2304,256]{1,0:T(8,128)} fusion(f32[2304,256]{1,0:T(8,128)S(1)} %get-tuple-element.8), kind=kLoop, calls=%fused_computation.29 | loop fusion | flops 589824 | bytes 4718592 | tf_op jit(solution)/shard_map/div | solution.py:352
  114.2 0.6 copy.58
  114.8 0.8 copy.59
  (28 shorter events, 7.4 us)
Async XLA Ops:
  25.1 3.2 %copy-start.1 = (bf16[256,1152]{1,0:T(8,128)(2,1)S(1)}, bf16[256,1152]{1,0:T(8,128)(2,1)}, u32[]{:S(2)}) copy-start(bf16[256,1152]{1,0:T(8,128)(2,1)} %shard_map.58) | copy-start | bytes 1769476
  31.7 2.0 %copy-start.2 = (bf16[1,256,1152]{2,1,0:T(8,128)(2,1)S(1)}, bf16[1,256,1152]{2,1,0:T(8,128)(2,1)}, u32[]{:S(2)}) copy-start(bf16[1,256,1152]{2,1,0:T(8,128)(2,1)} %param.3) | copy-start | bytes 1769476
  37.1 1.3 %copy-start = (bf16[256,9,256]{2,0,1:T(8,128)(2,1)S(1)}, bf16[256,9,256]{2,0,1:T(8,128)(2,1)}, u32[]{:S(2)}) copy-start(bf16[256,9,256]{2,0,1:T(8,128)(2,1)} %param.4) | copy-start | bytes 3538948
  38.2 1.4 %copy-start.3 = (f32[9,256,256]{2,1,0:T(8,128)}, f32[9,256,256]{2,1,0:T(8,128)S(1)}, u32[]{:S(2)}) copy-start(f32[9,256,256]{2,1,0:T(8,128)S(1)} %fusion.5) | copy-start | bytes 7077892

commit v11 on v7

--- a/solution.py
+++ b/solution.py
@@ -2,6 +2,7 @@
 
 import jax
 import jax.numpy as jnp
+import numpy as np
 from jax import lax
 from jax.experimental import pallas as pl
 from jax.experimental.pallas import tpu as pltpu
@@ -223,7 +224,8 @@
     )(a, t)
 
 
-def _allgather_kernel(axis_names, n, x_ref, o_ref, send_sems, recv_sems):
+def _allgather_kernel(axis_names, n, shifts, x_ref, w_ref, f_ref, m_ref, o_ref, t_ref,
+                      send_sems, recv_sems):
     rows = x_ref.shape[0]
     MESH = pl.DeviceIdType.MESH
     me = lax.axis_index("chan")
@@ -246,6 +248,16 @@
         c.start()
         copies.append(c)
     o_ref[mine, :] = x_ref[...]
+    size = f_ref.shape[1]
+    for t, shift in enumerate(shifts):
+        y = jnp.dot(w_ref[t], f_ref[...], preferred_element_type=jnp.float32)
+        if shift % size:
+            y = pltpu.roll(y, (-shift) % size, 1)
+        y = y * m_ref[pl.ds(t, 1), :]
+        if t == 0:
+            t_ref[...] = y
+        else:
+            t_ref[...] += y
     for k in range(1, n):
         src = (me + n - k) % n
         theirs = pl.ds(pl.multiple_of(src * rows, 16), rows)
@@ -256,18 +268,23 @@
         c.wait_send()
 
 
-def chan_allgather(x, axis_names):
+def chan_allgather(x, axis_names, w, f, masks, shifts):
     rows, cols = x.shape
     n = lax.axis_size("chan")
     vmem = pltpu.VMEM
     return pl.pallas_call(
-        functools.partial(_allgather_kernel, axis_names, n),
-        out_shape=jax.ShapeDtypeStruct((rows * n, cols), x.dtype),
-        in_specs=[pl.BlockSpec(memory_space=vmem)],
-        out_specs=pl.BlockSpec(memory_space=vmem),
+        functools.partial(_allgather_kernel, axis_names, n, shifts),
+        out_shape=(
+            jax.ShapeDtypeStruct((rows * n, cols), x.dtype),
+            jax.ShapeDtypeStruct((w.shape[1], f.shape[1]), jnp.float32),
+        ),
+        in_specs=[pl.BlockSpec(memory_space=vmem)] * 4,
+        out_specs=(pl.BlockSpec(memory_space=vmem),) * 2,
         scratch_shapes=[pltpu.SemaphoreType.DMA((n,)), pltpu.SemaphoreType.DMA((n,))],
-        compiler_params=pltpu.CompilerParams(collective_id=1, has_side_effects=True),
-    )(x)
+        compiler_params=pltpu.CompilerParams(
+            collective_id=1, has_side_effects=True, vmem_limit_bytes=48 * 1024 * 1024
+        ),
+    )(x, w, f, masks)
 
 
 def on_device(axis_names, inputs, weight, cotangent):
@@ -287,7 +304,22 @@
         )
         for first_operand, second_operand in tap_shifts
     ]
-    flat_grads = chan_allgather(cotangent[0], axis_names)
+    rows_idx = np.arange(tap_locations) // MAP_WIDTH
+    cols_idx = np.arange(tap_locations) % MAP_WIDTH
+    masks = np.stack(
+        [
+            ((rows_idx + a >= 0) & (rows_idx + a < MAP_HEIGHT) & (cols_idx + b >= 0) & (cols_idx + b < MAP_WIDTH))
+            for a, b in tap_shifts
+        ]
+    ).astype(np.float32)
+    flat_grads, total = chan_allgather(
+        cotangent[0],
+        axis_names,
+        jnp.transpose(weight, (1, 2, 0)),
+        inputs[0],
+        jnp.asarray(masks),
+        tuple(a * MAP_WIDTH + b for a, b in tap_shifts),
+    )
     contract_cols = (((1,), (1,)), ((), ()))
     local_grad = jnp.stack(
         [
@@ -301,13 +333,6 @@
         ],
         axis=0,
     )
-    contract_rows = (((0,), (0,)), ((), ()))
-    total = jnp.zeros((cout_local * lax.axis_size("chan"), tap_locations), jnp.float32)
-    for tap_index in range(tap_list):
-        columns = weight[:, tap_index, :]
-        total = total + lax.dot_general(
-            columns, displaced_input[tap_index], contract_rows, preferred_element_type=jnp.float32
-        )
     summed, owned = dp_allreduce(
         local_grad.reshape(tap_list * input_channels_local, output_channels_total), total, axis_names
     )

time: 102 us -> 103 us (level)
  local copies, waits for them, and re-layouts: 5.96 us -> 12.2 us
  matrix products: 10.2 us -> 6.55 us
  Pallas kernels: 83.6 us -> 81.9 us
    dot_general x9 -> x0, matrix products: 3.53 us -> none  [on_device(): lax.dot_general(columns, displaced_input[tap_index], contract_rows, prefe...]
    slice x2, local copies, waits for them, and re-layouts: 1.48 us -> 4.87 us  [translated_input(): bordered_input[:, reach + row_shift:reach + row_shift + height, reach + c...]
    unnamed x9 -> x26, local copies, waits for them, and re-layouts: 3.18 us -> 6.24 us
    pallas_call x1, Pallas kernels: 16.7 us -> 15 us  [chan_allgather(): pl.pallas_call(functools.partial(_allgather_kernel, axis_names, n, shifts...]
where the time goes in v11:
time: 103 us
  Pallas kernels  81.9 us (80%)
  local copies, waits for them, and re-layouts  12.2 us (12%)
  matrix products  6.55 us (6%)
  other arithmetic  1.56 us (2%)
    pallas_call x1, Pallas kernels, dp_allreduce(): pl.pallas_call(functools.partial(_allreduce_kernel, axis_names, nz, nc, S...  66.9 us
    pallas_call x1, Pallas kernels, chan_allgather(): pl.pallas_call(functools.partial(_allgather_kernel, axis_names, n, shifts...  15 us
    unnamed x26, local copies, waits for them, and re-layouts  6.24 us
    slice x2, local copies, waits for them, and re-layouts, translated_input(): bordered_input[:, reach + row_shift:reach + row_shift + height, reach + c...  4.87 us
    dot_general x9, matrix products, on_device(): lax.dot_general(displaced_input[tap_index], flat_grads, contract_cols, pr...  3.42 us
    dot_general x9, matrix products, on_device(): jnp.dot(weight[:, tap_index, :], displaced_gradient, preferred_element_ty...  3.13 us

profile of v11, /device:TPU:1, one launch (start us, length us, event | category | flops | bytes accessed | tf_op | source)
XLA Modules:
  0.0 103.1 jit_solution(14565239237871647373)
XLA Ops:
  0.6 1.3 %copy.9 = bf16[1,256,1152]{1,2,0:T(8,128)(2,1)S(1)} copy(bf16[1,256,1152]{2,1,0:T(8,128)(2,1)} %param.4) | data formatting | bytes 1179648 | tf_op args[0]
  1.9 2.2 %pad_slice_fusion.8 = (bf16[256,16,72]{0,2,1:T(8,128)(2,1)S(1)}, bf16[256,16,72]{0,2,1:T(8,128)(2,1)}, bf16[256,16,72]{0,2,1:T(8,128)(2,1)}, bf16[256,16,72]{0,2...) fusion(bf16[256,16,72]{0,2,1:T(8,128)(2,1)S(1)} %bitcast.138), kind=kLoop, calls=%fused_computation.8 | loop fusion | bytes 5308416 | tf_op jit(solution)/shard_map/slice | solution.py:20
  4.1 1.6 %copy.10 = bf16[256,9,256]{0,2,1:T(8,128)(2,1)S(1)} copy(bf16[256,9,256]{2,0,1:T(8,128)(2,1)} %param.5) | data formatting | bytes 2359296 | tf_op args[1]
  5.8 15.0 %shard_map.67 = (bf16[256,1152]{1,0:T(8,128)(2,1)S(1)}, f32[256,1152]{1,0:T(8,128)S(1)}) custom-call(bf16[32,1152]{1,0:T(8,128)(2,1)S(1)} %bitcast.127, bf16[9,256,256]{2,1,0:T(8,128)(2,1)S(1)} %bitcast.124, bf16[256,1152]{1,0:T(8,128)(2,1)S(1)} %bitcast.123, f32[9,1152]{1,0:T(8,128)S(1)} %copy-done.2), custom_call_target="tpu_custom_call" | custom-call | tf_op jit(solution)/shard_map/pallas_call | solution.py:275
  20.9 0.4 fusion.10
  21.3 0.6 copy-done.9
  21.9 0.4 fusion.9
  22.3 0.4 fusion.8
  23.0 0.4 fusion.7
  23.4 0.4 fusion.6
  24.1 0.4 fusion.5
  24.5 0.4 fusion.4
  25.2 0.4 fusion.3
  25.6 0.4 fusion.2
  26.0 66.9 %shard_map.68 = (f32[2304,256]{1,0:T(8,128)S(1)}, bf16[32,1152]{1,0:T(8,128)(2,1)S(1)}) custom-call(f32[2304,256]{1,0:T(8,128)S(1)} %bitcast.125, f32[256,1152]{1,0:T(8,128)S(1)} %get-tuple-element.8.t_ref), custom_call_target="tpu_custom_call" | custom-call | tf_op jit(solution)/shard_map/pallas_call | solution.py:198
  92.9 1.1 %copy.11 = bf16[256,1152]{0,1:T(8,128)(2,1)} copy(bf16[256,1152]{1,0:T(8,128)(2,1)S(1)} %get-tuple-element.7) | data formatting | bytes 1179648 | tf_op jit(solution)/shard_map/pallas_call | solution.py:275
  94.0 2.7 %pad_slice_fusion = (bf16[256,16,72]{0,2,1:T(8,128)(2,1)S(1)}, bf16[256,16,72]{0,2,1:T(8,128)(2,1)S(1)}, bf16[256,16,72]{0,2,1:T(8,128)(2,1)S(1)}, bf16[256,16,7...) fusion(bf16[256,16,72]{0,2,1:T(8,128)(2,1)} %bitcast.139), kind=kLoop, calls=%fused_computation | loop fusion | bytes 5308416 | tf_op jit(solution)/shard_map/slice | solution.py:20
  96.6 0.3 fusion.19
  97.0 0.4 convolution_add_fusion.7
  98.1 0.4 convolution_add_fusion.4
  99.5 0.3 fusion.1
  99.8 1.1 %copy.12 = bf16[1,256,1152]{2,1,0:T(8,128)(2,1)} copy(bf16[1,256,1152]{1,2,0:T(8,128)(2,1)S(1)} %fusion.1) | data formatting | bytes 1179648
  100.9 1.6 %broadcast_multiply_fusion = f32[2304,256]{1,0:T(8,128)} fusion(f32[2304,256]{1,0:T(8,128)S(1)} %get-tuple-element.10), kind=kLoop, calls=%fused_computation.26 | loop fusion | flops 589824 | bytes 4718592 | tf_op jit(solution)/shard_map/div | solution.py:343
  102.4 0.6 copy.22
  (26 shorter events, 2.7 us)
Async XLA Ops:
  4.1 1.7 %copy-start = (bf16[1,256,1152]{2,1,0:T(8,128)(2,1)S(1)}, bf16[1,256,1152]{2,1,0:T(8,128)(2,1)}, u32[]{:S(2)}) copy-start(bf16[1,256,1152]{2,1,0:T(8,128)(2,1)} %param.4) | copy-start | bytes 1769476
  4.1 1.7 %copy-start.1 = (bf16[1,32,1152]{2,1,0:T(8,128)(2,1)S(1)}, bf16[1,32,1152]{2,1,0:T(8,128)(2,1)}, u32[]{:S(2)}) copy-start(bf16[1,32,1152]{2,1,0:T(8,128)(2,1)} %param.6) | copy-start | bytes 221188
  4.1 1.7 %copy-start.2 = (f32[9,1152]{1,0:T(8,128)S(1)}, f32[9,1152]{1,0:T(8,128)}, u32[]{:S(2)}) copy-start(f32[9,1152]{1,0:T(8,128)} %constant.8.clone.m_ref) | copy-start | bytes 124420
  5.8 15.1 %copy-start.10 = (bf16[256,16,72]{0,2,1:T(8,128)(2,1)S(1)}, bf16[256,16,72]{0,2,1:T(8,128)(2,1)}, u32[]{:S(2)}) copy-start(bf16[256,16,72]{0,2,1:T(8,128)(2,1)} %get-tuple-element.32) | copy-start | bytes 1769476
  20.8 1.1 %copy-start.9 = (bf16[256,16,72]{0,2,1:T(8,128)(2,1)S(1)}, bf16[256,16,72]{0,2,1:T(8,128)(2,1)}, u32[]{:S(2)}) copy-start(bf16[256,16,72]{0,2,1:T(8,128)(2,1)} %get-tuple-element.26) | copy-start | bytes 1769476
  20.9 1.4 %copy-start.8 = (bf16[256,16,72]{0,2,1:T(8,128)(2,1)S(1)}, bf16[256,16,72]{0,2,1:T(8,128)(2,1)}, u32[]{:S(2)}) copy-start(bf16[256,16,72]{0,2,1:T(8,128)(2,1)} %get-tuple-element.27) | copy-start | bytes 1769476
  21.9 1.1 %copy-start.7 = (bf16[256,16,72]{0,2,1:T(8,128)(2,1)S(1)}, bf16[256,16,72]{0,2,1:T(8,128)(2,1)}, u32[]{:S(2)}) copy-start(bf16[256,16,72]{0,2,1:T(8,128)(2,1)} %get-tuple-element.28) | copy-start | bytes 1769476
  23.0 1.1 %copy-start.6 = (bf16[256,16,72]{0,2,1:T(8,128)(2,1)S(1)}, bf16[256,16,72]{0,2,1:T(8,128)(2,1)}, u32[]{:S(2)}) copy-start(bf16[256,16,72]{0,2,1:T(8,128)(2,1)} %get-tuple-element.29) | copy-start | bytes 1769476
  23.4 1.1 %copy-start.5 = (bf16[256,16,72]{0,2,1:T(8,128)(2,1)S(1)}, bf16[256,16,72]{0,2,1:T(8,128)(2,1)}, u32[]{:S(2)}) copy-start(bf16[256,16,72]{0,2,1:T(8,128)(2,1)} %get-tuple-element.30) | copy-start | bytes 1769476
  24.1 1.1 %copy-start.4 = (bf16[256,16,72]{0,2,1:T(8,128)(2,1)S(1)}, bf16[256,16,72]{0,2,1:T(8,128)(2,1)}, u32[]{:S(2)}) copy-start(bf16[256,16,72]{0,2,1:T(8,128)(2,1)} %get-tuple-element.31) | copy-start | bytes 1769476
  94.0 2.7 %copy-start.3 = (bf16[256,9,256]{2,0,1:T(8,128)(2,1)S(1)}, bf16[256,9,256]{2,0,1:T(8,128)(2,1)}, u32[]{:S(2)}) copy-start(bf16[256,9,256]{2,0,1:T(8,128)(2,1)} %param.5) | copy-start | bytes 3538948

commit v12 on v11

--- a/solution.py
+++ b/solution.py
@@ -24,8 +24,9 @@
     ]
 
 
-def _allreduce_kernel(axis_names, nz, nc, streams, a_ref, t_ref, o_ref, res_ref, rc, s1, f1, rx, rp, rm,
-                      ap, am, rs_buf, send_sems, recv_sems, rs_send, rs_recv):
+def _allreduce_kernel(axis_names, nz, nc, streams, shifts, a_ref, t_ref, w_ref, g_ref, m_ref,
+                      o_ref, res_ref, ig_ref, rc, s1, f1, rx, rp, rm, ap, am, rs_buf, ig_acc,
+                      send_sems, recv_sems, rs_send, rs_recv):
     rows, cols = a_ref.shape
     half = rows // 2
     chunk = half // nz
@@ -82,6 +83,22 @@
 
     def rows_of(j):
         return pl.ds(pl.multiple_of(j * chunk, 8), chunk)
+
+    done_taps = [0]
+    size = g_ref.shape[1]
+
+    def input_grad_tap():
+        t = done_taps[0]
+        if t < len(shifts):
+            y = jnp.dot(w_ref[t], g_ref[...], preferred_element_type=jnp.float32)
+            if shifts[t] % size:
+                y = pltpu.roll(y, shifts[t] % size, 1)
+            y = y * m_ref[pl.ds(t, 1), :]
+            if t == 0:
+                ig_acc[...] = y
+            else:
+                ig_acc[...] += y
+            done_taps[0] += 1
 
     mine_c = core * half
     other_c = (1 - core) * half
@@ -169,6 +186,10 @@
             gm = grows(jm, q)
             pending[q] = (remote(o_ref.at[gp, lo], o_ref.at[gp, lo], zr),
                           remote(o_ref.at[gm, hi], o_ref.at[gm, hi], zl))
+        input_grad_tap()
+        if s == nz - 2:
+            while done_taps[0] < len(shifts):
+                input_grad_tap()
     for q in range(streams):
         arrived(q, (z + 2) % nz, (z + nz - 2) % nz)
     for c in to_core:
@@ -180,12 +201,13 @@
     for k in range(1, nc):
         acc = acc + rs_buf[k]
     res_ref[...] = acc.astype(res_ref.dtype)
+    ig_ref[...] = ig_acc[...].astype(ig_ref.dtype)
 
     for c in sent + rs_copies:
         c.wait_send()
 
 
-def dp_allreduce(a, t, axis_names):
+def dp_allreduce(a, t, w, g, masks, shifts, axis_names):
     rows, cols = a.shape
     nc = lax.axis_size("chan")
     owned = t.shape[0] // nc
@@ -196,13 +218,14 @@
     n_copies = nz + 3 + 6 * (nz - 1) * STREAMS
     vmem = pltpu.VMEM
     return pl.pallas_call(
-        functools.partial(_allreduce_kernel, axis_names, nz, nc, STREAMS),
+        functools.partial(_allreduce_kernel, axis_names, nz, nc, STREAMS, shifts),
         out_shape=(
             jax.ShapeDtypeStruct((rows, cols), a.dtype),
             jax.ShapeDtypeStruct((owned, t.shape[1]), jnp.bfloat16),
+            jax.ShapeDtypeStruct((w.shape[1], g.shape[1]), jnp.bfloat16),
         ),
-        in_specs=[pl.BlockSpec(memory_space=vmem)] * 2,
-        out_specs=(pl.BlockSpec(memory_space=vmem), pl.BlockSpec(memory_space=vmem)),
+        in_specs=[pl.BlockSpec(memory_space=vmem)] * 5,
+        out_specs=(pl.BlockSpec(memory_space=vmem),) * 3,
         scratch_shapes=[
             vmem((half, cols), a.dtype),
             vmem((half, cols), a.dtype),
@@ -213,6 +236,7 @@
             vmem((nz - 1, chunk, lanes), a.dtype),
             vmem((nz - 1, chunk, lanes), a.dtype),
             vmem((nc, owned, t.shape[1]), t.dtype),
+            vmem((w.shape[1], g.shape[1]), jnp.float32),
             pltpu.SemaphoreType.DMA((n_copies,)),
             pltpu.SemaphoreType.DMA((n_copies,)),
             pltpu.SemaphoreType.DMA((nc,)),
@@ -221,7 +245,7 @@
         compiler_params=pltpu.CompilerParams(
             collective_id=0, has_side_effects=True, vmem_limit_bytes=48 * 1024 * 1024
         ),
-    )(a, t)
+    )(a, t, w, g, masks)
 
 
 def _allgather_kernel(axis_names, n, shifts, x_ref, w_ref, f_ref, m_ref, o_ref, t_ref,
@@ -333,26 +357,27 @@
         ],
         axis=0,
     )
-    summed, owned = dp_allreduce(
-        local_grad.reshape(tap_list * input_channels_local, output_channels_total), total, axis_names
+    back_masks = np.stack(
+        [
+            ((rows_idx - a >= 0) & (rows_idx - a < MAP_HEIGHT) & (cols_idx - b >= 0) & (cols_idx - b < MAP_WIDTH))
+            for a, b in tap_shifts
+        ]
+    ).astype(np.float32)
+    summed, owned, back = dp_allreduce(
+        local_grad.reshape(tap_list * input_channels_local, output_channels_total),
+        total,
+        jnp.transpose(weight, (1, 0, 2)),
+        flat_grads,
+        jnp.asarray(back_masks),
+        tuple(a * MAP_WIDTH + b for a, b in tap_shifts),
+        axis_names,
     )
     result = owned.reshape(1, cout_local, tap_locations)
     summed_grad = jnp.transpose(
         summed.reshape(tap_list, input_channels_local, output_channels_total), (1, 0, 2)
     )
     weight_grad = summed_grad / jnp.float32(lax.axis_size("dp"))
-
-    collected_input = flat_grads.reshape(output_channels_total, MAP_HEIGHT, MAP_WIDTH)
-    back_sum = jnp.zeros((input_channels_local, tap_locations), jnp.float32)
-    for tap_index in range(tap_list):
-        row_shift, column_shift = tap_shifts[tap_index]
-        displaced_gradient = translated_input(
-            collected_input, -row_shift, -column_shift, DILATION_RATE
-        ).reshape(output_channels_total, tap_locations)
-        back_sum = back_sum + jnp.dot(
-            weight[:, tap_index, :], displaced_gradient, preferred_element_type=jnp.float32
-        )
-    input_grad = back_sum.astype(jnp.bfloat16).reshape(1, input_channels_local, tap_locations)
+    input_grad = back.reshape(1, input_channels_local, tap_locations)
     return (result, input_grad, weight_grad)
 
 

time: 103 us -> 96 us (0.932)
  local copies, waits for them, and re-layouts: 12.2 us -> 6.56 us
  matrix products: 6.55 us -> 3.47 us
  Pallas kernels: 81.9 us -> 83.5 us
    slice x2 -> x1, local copies, waits for them, and re-layouts: 4.87 us -> 0.74 us  [translated_input(): bordered_input[:, reach + row_shift:reach + row_shift + height, reach + c...]
    dot_general x9 -> x0, matrix products: 3.13 us -> none  [on_device(): jnp.dot(weight[:, tap_index, :], displaced_gradient, preferred_element_ty...]
    pallas_call x1, Pallas kernels: 66.9 us -> 68.4 us  [dp_allreduce(): pl.pallas_call(functools.partial(_allreduce_kernel, axis_names, nz, nc, S...]
    pallas_call x1 -> x0, local copies, waits for them, and re-layouts: 1.06 us -> none  [chan_allgather(): pl.pallas_call(functools.partial(_allgather_kernel, axis_names, n, shifts...]
    unnamed x26 -> x16, local copies, waits for them, and re-layouts: 6.24 us -> 5.81 us
where the time goes in v12:
time: 96 us; the launch traced here: 95.8 us
  Pallas kernels  83.5 us (87%)
  local copies, waits for them, and re-layouts  6.56 us (7%)
  matrix products  3.47 us (4%)
  other arithmetic  1.56 us (2%)
    pallas_call x1, Pallas kernels, dp_allreduce(): pl.pallas_call(functools.partial(_allreduce_kernel, axis_names, nz, nc, S...  68.4 us
    pallas_call x1, Pallas kernels, chan_allgather(): pl.pallas_call(functools.partial(_allgather_kernel, axis_names, n, shifts...  15 us
    unnamed x16, local copies, waits for them, and re-layouts  5.81 us
    dot_general x9, matrix products, on_device(): lax.dot_general(displaced_input[tap_index], flat_grads, contract_cols, pr...  3.47 us

profile of v12, /device:TPU:1, one launch (start us, length us, event | category | flops | bytes accessed | tf_op | source)
XLA Modules:
  0.0 95.8 jit_solution(18323098072754992166)
XLA Ops:
  0.6 0.0 copy-start.4
  0.6 0.0 copy-start
  0.7 1.4 %copy.9 = bf16[1,256,1152]{1,2,0:T(8,128)(2,1)S(1)} copy(bf16[1,256,1152]{2,1,0:T(8,128)(2,1)} %param.5) | data formatting | bytes 1179648 | tf_op args[0]
  2.0 1.6 %copy.10 = bf16[256,9,256]{0,2,1:T(8,128)(2,1)S(1)} copy(bf16[256,9,256]{2,0,1:T(8,128)(2,1)} %param.6) | data formatting | bytes 2359296 | tf_op args[1]
  3.6 15.0 %shard_map.76 = (bf16[256,1152]{1,0:T(8,128)(2,1)S(1)}, f32[256,1152]{1,0:T(8,128)S(1)}) custom-call(bf16[32,1152]{1,0:T(8,128)(2,1)S(1)} %bitcast.81, bf16[9,256,256]{2,1,0:T(8,128)(2,1)S(1)} %bitcast.77, bf16[256,1152]{1,0:T(8,128)(2,1)S(1)} %bitcast.76, f32[9,1152]{1,0:T(8,128)S(1)} %copy-done.4), custom_call_target="tpu_custom_call" | custom-call | tf_op jit(solution)/shard_map/pallas_call | solution.py:299
  18.7 0.7 pad_slice_fusion
  19.4 0.4 fusion.8
  19.8 0.4 fusion.7
  20.2 0.4 fusion.6
  20.6 0.4 fusion.5
  21.0 0.4 fusion.4
  21.4 0.4 fusion.3
  21.8 0.0 copy-start.1
  21.8 0.0 copy-start.3
  21.8 0.4 fusion.2
  22.2 0.4 fusion.1
  22.6 0.4 fusion
  23.0 0.0 copy-start.5
  23.0 1.4 %copy-done.5 = f32[9,256,256]{2,1,0:T(8,128)} copy-done((f32[9,256,256]{2,1,0:T(8,128)}, f32[9,256,256]{2,1,0:T(8,128)S(1)}, u32[]{:S(2)}) %copy-start.5) | copy-done | bytes 2359320
  24.4 0.0 copy-done.3
  24.4 68.4 %shard_map.77 = (f32[2304,256]{1,0:T(8,128)S(1)}, bf16[32,1152]{1,0:T(8,128)(2,1)S(1)}, bf16[256,1152]{1,0:T(8,128)(2,1)S(1)}) custom-call(f32[2304,256]{1,0:T(8,128)} %bitcast.82, f32[256,1152]{1,0:T(8,128)S(1)} %get-tuple-element.9.t_ref, bf16[9,256,256]{2,1,0:T(8,128)(2,1)S(1)} %bitcast.78, bf16[256,1152]{1,0:T(8,128)(2,1)S(1)} %get-tuple-element.8.g_ref, ...), custom_call_target="tpu_custom_call" | custom-call | tf_op jit(solution)/shard_map/pallas_call | solution.py:220
  92.8 1.6 %broadcast_multiply_fusion = f32[2304,256]{1,0:T(8,128)} fusion(f32[2304,256]{1,0:T(8,128)S(1)} %get-tuple-element.12), kind=kLoop, calls=%fused_computation.8 | loop fusion | flops 589824 | bytes 4718592 | tf_op jit(solution)/shard_map/div | solution.py:379
  94.4 0.6 copy.21
  95.0 0.8 copy.22
  (5 shorter events, 0.0 us)
Async XLA Ops:
  0.6 3.0 %copy-start.4 = (f32[9,1152]{1,0:T(8,128)S(1)}, f32[9,1152]{1,0:T(8,128)}, u32[]{:S(2)}) copy-start(f32[9,1152]{1,0:T(8,128)} %constant.10.clone.m_ref) | copy-start | bytes 124420
  0.6 3.0 %copy-start = (bf16[1,256,1152]{2,1,0:T(8,128)(2,1)S(1)}, bf16[1,256,1152]{2,1,0:T(8,128)(2,1)}, u32[]{:S(2)}) copy-start(bf16[1,256,1152]{2,1,0:T(8,128)(2,1)} %param.5) | copy-start | bytes 1769476
  0.7 3.0 %copy-start.2 = (bf16[1,32,1152]{2,1,0:T(8,128)(2,1)S(1)}, bf16[1,32,1152]{2,1,0:T(8,128)(2,1)}, u32[]{:S(2)}) copy-start(bf16[1,32,1152]{2,1,0:T(8,128)(2,1)} %param.7) | copy-start | bytes 221188
  21.8 2.6 %copy-start.1 = (bf16[256,9,256]{2,0,1:T(8,128)(2,1)S(1)}, bf16[256,9,256]{2,0,1:T(8,128)(2,1)}, u32[]{:S(2)}) copy-start(bf16[256,9,256]{2,0,1:T(8,128)(2,1)} %param.6) | copy-start | bytes 3538948
  21.8 2.6 %copy-start.3 = (f32[9,1152]{1,0:T(8,128)S(1)}, f32[9,1152]{1,0:T(8,128)}, u32[]{:S(2)}) copy-start(f32[9,1152]{1,0:T(8,128)} %constant.11.clone.m_ref) | copy-start | bytes 124420
  23.0 1.4 %copy-start.5 = (f32[9,256,256]{2,1,0:T(8,128)}, f32[9,256,256]{2,1,0:T(8,128)S(1)}, u32[]{:S(2)}) copy-start(f32[9,256,256]{2,1,0:T(8,128)S(1)} %fusion) | copy-start | bytes 7077892

commit v13 on v12

--- a/solution.py
+++ b/solution.py
@@ -248,8 +248,8 @@
     )(a, t, w, g, masks)
 
 
-def _allgather_kernel(axis_names, n, shifts, x_ref, w_ref, f_ref, m_ref, o_ref, t_ref,
-                      send_sems, recv_sems):
+def _allgather_kernel(axis_names, n, shifts, x_ref, w_ref, f_ref, m_ref, o_ref, t_ref, wg_ref,
+                      xs, send_sems, recv_sems):
     rows = x_ref.shape[0]
     MESH = pl.DeviceIdType.MESH
     me = lax.axis_index("chan")
@@ -282,12 +282,20 @@
             t_ref[...] = y
         else:
             t_ref[...] += y
+    wide = f_ref[...].astype(jnp.float32)
+    for t, shift in enumerate(shifts):
+        v = pltpu.roll(wide, (-shift) % size, 1) if shift % size else wide
+        xs[t] = (v * m_ref[pl.ds(t, 1), :]).astype(xs.dtype)
     for k in range(1, n):
         src = (me + n - k) % n
         theirs = pl.ds(pl.multiple_of(src * rows, 16), rows)
         pltpu.make_async_remote_copy(
             src_ref=x_ref, dst_ref=o_ref.at[theirs], send_sem=send_sems.at[k],
             recv_sem=recv_sems.at[k], device_id=dev(src), device_id_type=MESH).wait_recv()
+    cin = f_ref.shape[0]
+    for t in range(len(shifts)):
+        wg_ref[pl.ds(t * cin, cin), :] = lax.dot_general(
+            xs[t], o_ref[...], (((1,), (1,)), ((), ())), preferred_element_type=jnp.float32)
     for c in copies:
         c.wait_send()
 
@@ -301,10 +309,15 @@
         out_shape=(
             jax.ShapeDtypeStruct((rows * n, cols), x.dtype),
             jax.ShapeDtypeStruct((w.shape[1], f.shape[1]), jnp.float32),
+            jax.ShapeDtypeStruct((len(shifts) * f.shape[0], rows * n), jnp.float32),
         ),
         in_specs=[pl.BlockSpec(memory_space=vmem)] * 4,
-        out_specs=(pl.BlockSpec(memory_space=vmem),) * 2,
-        scratch_shapes=[pltpu.SemaphoreType.DMA((n,)), pltpu.SemaphoreType.DMA((n,))],
+        out_specs=(pl.BlockSpec(memory_space=vmem),) * 3,
+        scratch_shapes=[
+            vmem((len(shifts),) + f.shape, f.dtype),
+            pltpu.SemaphoreType.DMA((n,)),
+            pltpu.SemaphoreType.DMA((n,)),
+        ],
         compiler_params=pltpu.CompilerParams(
             collective_id=1, has_side_effects=True, vmem_limit_bytes=48 * 1024 * 1024
         ),
@@ -322,12 +335,6 @@
         (DILATION_RATE * (tap_index // 3 - 1), DILATION_RATE * (tap_index % 3 - 1))
         for tap_index in range(tap_list)
     ]
-    displaced_input = [
-        translated_input(feature_map, first_operand, second_operand, DILATION_RATE).reshape(
-            input_channels_local, tap_locations
-        )
-        for first_operand, second_operand in tap_shifts
-    ]
     rows_idx = np.arange(tap_locations) // MAP_WIDTH
     cols_idx = np.arange(tap_locations) % MAP_WIDTH
     masks = np.stack(
@@ -336,26 +343,13 @@
             for a, b in tap_shifts
         ]
     ).astype(np.float32)
-    flat_grads, total = chan_allgather(
+    flat_grads, total, local_grad = chan_allgather(
         cotangent[0],
         axis_names,
         jnp.transpose(weight, (1, 2, 0)),
         inputs[0],
         jnp.asarray(masks),
         tuple(a * MAP_WIDTH + b for a, b in tap_shifts),
-    )
-    contract_cols = (((1,), (1,)), ((), ()))
-    local_grad = jnp.stack(
-        [
-            lax.dot_general(
-                displaced_input[tap_index],
-                flat_grads,
-                contract_cols,
-                preferred_element_type=jnp.float32,
-            )
-            for tap_index in range(tap_list)
-        ],
-        axis=0,
     )
     back_masks = np.stack(
         [
@@ -364,7 +358,7 @@
         ]
     ).astype(np.float32)
     summed, owned, back = dp_allreduce(
-        local_grad.reshape(tap_list * input_channels_local, output_channels_total),
+        local_grad,
         total,
         jnp.transpose(weight, (1, 0, 2)),
         flat_grads,

time: 96 us -> 92.3 us (0.961)
  matrix products: 3.47 us -> 0 us
  local copies, waits for them, and re-layouts: 6.56 us -> 4.58 us
  Pallas kernels: 83.5 us -> 85.3 us
    dot_general x9 -> x0, matrix products: 3.47 us -> none  [on_device(): lax.dot_general(displaced_input[tap_index], flat_grads, contract_cols, pr...]
    pallas_call x1, Pallas kernels: 15 us -> 16.9 us  [chan_allgather(): pl.pallas_call(functools.partial(_allgather_kernel, axis_names, n, shifts...]
    unnamed x16 -> x15, local copies, waits for them, and re-layouts: 5.81 us -> 4.58 us
where the time goes in v13:
time: 92.3 us; the launch traced here: 92.2 us
  Pallas kernels  85.3 us (92%)
  local copies, waits for them, and re-layouts  4.58 us (5%)
  other arithmetic  1.56 us (2%)
    pallas_call x1, Pallas kernels, dp_allreduce(): pl.pallas_call(functools.partial(_allreduce_kernel, axis_names, nz, nc, S...  68.4 us
    pallas_call x1, Pallas kernels, chan_allgather(): pl.pallas_call(functools.partial(_allgather_kernel, axis_names, n, shifts...  16.9 us
    unnamed x15, local copies, waits for them, and re-layouts  4.58 us

profile of v13, /device:TPU:1, one launch (start us, length us, event | category | flops | bytes accessed | tf_op | source)
XLA Modules:
  0.0 92.2 jit_solution(9964164447273249973)
XLA Ops:
  0.6 0.0 copy-start.5
  0.6 0.0 copy-start.4
  0.7 0.0 copy-start
  0.7 0.0 copy-start.3
  0.7 0.0 copy-start.2
  0.7 1.7 %copy.8 = bf16[256,9,256]{0,2,1:T(8,128)(2,1)S(1)} copy(bf16[256,9,256]{2,0,1:T(8,128)(2,1)} %param.6) | data formatting | bytes 2359296 | tf_op args[1]
  2.4 0.0 copy-done.5
  2.4 0.0 copy-done.3
  2.4 0.0 copy-done.2
  2.4 16.9 %shard_map.76 = (bf16[256,1152]{1,0:T(8,128)(2,1)S(1)}, f32[256,1152]{1,0:T(8,128)S(1)}, f32[2304,256]{1,0:T(8,128)S(1)}) custom-call(bf16[32,1152]{1,0:T(8,128)(2,1)S(1)} %bitcast.14, bf16[9,256,256]{2,1,0:T(8,128)(2,1)S(1)} %bitcast.9, bf16[256,1152]{1,0:T(8,128)(2,1)S(1)} %bitcast.12, f32[9,1152]{1,0:T(8,128)S(1)} %copy-done.5), custom_call_target="tpu_custom_call" | custom-call | tf_op jit(solution)/shard_map/pallas_call | solution.py:307
  19.3 0.0 copy-start.1
  19.4 1.4 %copy-done.1 = f32[2304,256]{1,0:T(8,128)} copy-done((f32[2304,256]{1,0:T(8,128)}, f32[2304,256]{1,0:T(8,128)S(1)}, u32[]{:S(2)}) %copy-start.1) | copy-done | bytes 2359320
  20.8 0.0 copy-done.4
  20.8 0.0 copy-done
  20.8 68.4 %shard_map.77 = (f32[2304,256]{1,0:T(8,128)S(1)}, bf16[32,1152]{1,0:T(8,128)(2,1)S(1)}, bf16[256,1152]{1,0:T(8,128)(2,1)S(1)}) custom-call(f32[2304,256]{1,0:T(8,128)} %copy-done.1, f32[256,1152]{1,0:T(8,128)S(1)} %get-tuple-element.10.t_ref, bf16[9,256,256]{2,1,0:T(8,128)(2,1)S(1)} %bitcast.10, bf16[256,1152]{1,0:T(8,128)(2,1)S(1)} %get-tuple-element.11.g_ref, ...), custom_call_target="tpu_custom_call" | custom-call | tf_op jit(solution)/shard_map/pallas_call | solution.py:220
  89.2 1.6 %broadcast_multiply_fusion = f32[2304,256]{1,0:T(8,128)} fusion(f32[2304,256]{1,0:T(8,128)S(1)} %get-tuple-element.14), kind=kLoop, calls=%fused_computation | loop fusion | flops 589824 | bytes 4718592 | tf_op jit(solution)/shard_map/div | solution.py:373
  90.7 0.6 copy.11
  91.4 0.8 copy.12
Async XLA Ops:
  0.6 1.8 %copy-start.5 = (f32[9,1152]{1,0:T(8,128)S(1)}, f32[9,1152]{1,0:T(8,128)}, u32[]{:S(2)}) copy-start(f32[9,1152]{1,0:T(8,128)} %constant.7.clone.m_ref) | copy-start | bytes 124420
  0.6 20.1 %copy-start.4 = (f32[9,1152]{1,0:T(8,128)S(1)}, f32[9,1152]{1,0:T(8,128)}, u32[]{:S(2)}) copy-start(f32[9,1152]{1,0:T(8,128)} %constant.8.clone.m_ref) | copy-start | bytes 124420
  0.7 20.1 %copy-start = (bf16[256,9,256]{2,0,1:T(8,128)(2,1)S(1)}, bf16[256,9,256]{2,0,1:T(8,128)(2,1)}, u32[]{:S(2)}) copy-start(bf16[256,9,256]{2,0,1:T(8,128)(2,1)} %param.6) | copy-start | bytes 3538948
  0.7 1.7 %copy-start.3 = (bf16[1,32,1152]{2,1,0:T(8,128)(2,1)S(1)}, bf16[1,32,1152]{2,1,0:T(8,128)(2,1)}, u32[]{:S(2)}) copy-start(bf16[1,32,1152]{2,1,0:T(8,128)(2,1)} %param.7) | copy-start | bytes 221188
  0.7 1.7 %copy-start.2 = (bf16[1,256,1152]{2,1,0:T(8,128)(2,1)S(1)}, bf16[1,256,1152]{2,1,0:T(8,128)(2,1)}, u32[]{:S(2)}) copy-start(bf16[1,256,1152]{2,1,0:T(8,128)(2,1)} %param.5) | copy-start | bytes 1769476
  19.3 1.4 %copy-start.1 = (f32[2304,256]{1,0:T(8,128)}, f32[2304,256]{1,0:T(8,128)S(1)}, u32[]{:S(2)}) copy-start(f32[2304,256]{1,0:T(8,128)S(1)} %get-tuple-element.9.a_ref) | copy-start | bytes 7077892

commit v14 on v13

--- a/solution.py
+++ b/solution.py
@@ -26,7 +26,7 @@
 
 def _allreduce_kernel(axis_names, nz, nc, streams, shifts, a_ref, t_ref, w_ref, g_ref, m_ref,
                       o_ref, res_ref, ig_ref, rc, s1, f1, rx, rp, rm, ap, am, rs_buf, ig_acc,
-                      send_sems, recv_sems, rs_send, rs_recv):
+                      send_sems, recv_sems, rs_send, rs_recv, entry_barrier=True):
     rows, cols = a_ref.shape
     half = rows // 2
     chunk = half // nz
@@ -50,12 +50,13 @@
     def cdev(p):
         return tuple(p if n == "chan" else lax.axis_index(n) for n in axis_names)
 
-    barrier = pltpu.get_barrier_semaphore()
-    for peer in (pc, px, zr, zl):
-        pl.semaphore_signal(barrier, inc=1, device_id=dev(peer), device_id_type=MESH)
-    for k in range(1, nc):
-        pl.semaphore_signal(barrier, inc=1, device_id=cdev((me + k) % nc), device_id_type=MESH)
-    pl.semaphore_wait(barrier, 4 + nc - 1)
+    if entry_barrier:
+        barrier = pltpu.get_barrier_semaphore()
+        for peer in (pc, px, zr, zl):
+            pl.semaphore_signal(barrier, inc=1, device_id=dev(peer), device_id_type=MESH)
+        for k in range(1, nc):
+            pl.semaphore_signal(barrier, inc=1, device_id=cdev((me + k) % nc), device_id_type=MESH)
+        pl.semaphore_wait(barrier, 4 + nc - 1)
 
     owned = res_ref.shape[0]
     rs_copies = []
@@ -249,7 +250,7 @@
 
 
 def _allgather_kernel(axis_names, n, shifts, x_ref, w_ref, f_ref, m_ref, o_ref, t_ref, wg_ref,
-                      xs, send_sems, recv_sems):
+                      xs, send_sems, recv_sems, entry_barrier=True):
     rows = x_ref.shape[0]
     MESH = pl.DeviceIdType.MESH
     me = lax.axis_index("chan")
@@ -257,10 +258,11 @@
     def dev(p):
         return tuple(p if a == "chan" else lax.axis_index(a) for a in axis_names)
 
-    barrier = pltpu.get_barrier_semaphore()
-    for k in range(1, n):
-        pl.semaphore_signal(barrier, inc=1, device_id=dev((me + k) % n), device_id_type=MESH)
-    pl.semaphore_wait(barrier, n - 1)
+    if entry_barrier:
+        barrier = pltpu.get_barrier_semaphore()
+        for k in range(1, n):
+            pl.semaphore_signal(barrier, inc=1, device_id=dev((me + k) % n), device_id_type=MESH)
+        pl.semaphore_wait(barrier, n - 1)
 
     mine = pl.ds(pl.multiple_of(me * rows, 16), rows)
     copies = []
@@ -324,6 +326,78 @@
     )(x, w, f, masks)
 
 
+def _fused_kernel(axis_names, nz, nc, streams, shifts, x_ref, wf_ref, f_ref, mf_ref, wb_ref, mb_ref,
+                  o_ref, res_ref, ig_ref, g_s, t_s, wg_s, xs, ag_send, ag_recv, *ar_scratch):
+    MESH = pl.DeviceIdType.MESH
+    dp = lax.axis_index("dp")
+    me = lax.axis_index("chan")
+    nd = 4 * nz
+    core = dp % 2
+    xl = (dp // 2) % 2
+    peers = (dp + 1 - 2 * core, dp + 2 - 4 * xl, (dp + 4) % nd, (dp + nd - 4) % nd)
+    barrier = pltpu.get_barrier_semaphore()
+    for peer in peers:
+        pl.semaphore_signal(barrier, inc=1, device_id=tuple(peer if a == "dp" else lax.axis_index(a) for a in axis_names), device_id_type=MESH)
+    for k in range(1, nc):
+        pl.semaphore_signal(barrier, inc=1, device_id=tuple((me + k) % nc if a == "chan" else lax.axis_index(a) for a in axis_names), device_id_type=MESH)
+    pl.semaphore_wait(barrier, 4 + nc - 1)
+    _allgather_kernel(axis_names, nc, shifts, x_ref, wf_ref, f_ref, mf_ref, g_s, t_s, wg_s, xs,
+                      ag_send, ag_recv, entry_barrier=False)
+    _allreduce_kernel(axis_names, nz, nc, streams, shifts, wg_s, t_s, wb_ref, g_s, mb_ref,
+                      o_ref, res_ref, ig_ref, *ar_scratch, entry_barrier=False)
+
+
+def fused_step(x, wf, f, mf, wb, mb, shifts, axis_names):
+    nc = lax.axis_size("chan")
+    nz = lax.axis_size("dp") // 4
+    rows_x, cols = x.shape
+    cin, taps = f.shape[0], len(shifts)
+    cout = rows_x * nc
+    rows, width = taps * cin, cout
+    owned = cout // nc
+    half = rows // 2
+    chunk = half // nz
+    lanes = width // 2
+    n_copies = nz + 3 + 6 * (nz - 1) * STREAMS
+    vmem = pltpu.VMEM
+    f32 = jnp.float32
+    return pl.pallas_call(
+        functools.partial(_fused_kernel, axis_names, nz, nc, STREAMS, shifts),
+        out_shape=(
+            jax.ShapeDtypeStruct((rows, width), f32),
+            jax.ShapeDtypeStruct((owned, cols), jnp.bfloat16),
+            jax.ShapeDtypeStruct((cin, cols), jnp.bfloat16),
+        ),
+        in_specs=[pl.BlockSpec(memory_space=vmem)] * 6,
+        out_specs=(pl.BlockSpec(memory_space=vmem),) * 3,
+        scratch_shapes=[
+            vmem((cout, cols), x.dtype),
+            vmem((cout, cols), f32),
+            vmem((rows, width), f32),
+            vmem((taps,) + f.shape, f.dtype),
+            pltpu.SemaphoreType.DMA((nc,)),
+            pltpu.SemaphoreType.DMA((nc,)),
+            vmem((half, width), f32),
+            vmem((half, width), f32),
+            vmem((chunk, width), f32),
+            vmem((chunk, width), f32),
+            vmem((nz - 1, chunk, lanes), f32),
+            vmem((nz - 1, chunk, lanes), f32),
+            vmem((nz - 1, chunk, lanes), f32),
+            vmem((nz - 1, chunk, lanes), f32),
+            vmem((nc, owned, cols), f32),
+            vmem((cin, cols), f32),
+            pltpu.SemaphoreType.DMA((n_copies,)),
+            pltpu.SemaphoreType.DMA((n_copies,)),
+            pltpu.SemaphoreType.DMA((nc,)),
+            pltpu.SemaphoreType.DMA((nc,)),
+        ],
+        compiler_params=pltpu.CompilerParams(
+            collective_id=0, has_side_effects=True, vmem_limit_bytes=56 * 1024 * 1024
+        ),
+    )(x, wf, f, mf, wb, mb)
+
+
 def on_device(axis_names, inputs, weight, cotangent):
     input_channels_local = inputs.shape[1]
     cout_local = cotangent.shape[1]
@@ -343,25 +417,18 @@
             for a, b in tap_shifts
         ]
     ).astype(np.float32)
-    flat_grads, total, local_grad = chan_allgather(
-        cotangent[0],
-        axis_names,
-        jnp.transpose(weight, (1, 2, 0)),
-        inputs[0],
-        jnp.asarray(masks),
-        tuple(a * MAP_WIDTH + b for a, b in tap_shifts),
-    )
     back_masks = np.stack(
         [
             ((rows_idx - a >= 0) & (rows_idx - a < MAP_HEIGHT) & (cols_idx - b >= 0) & (cols_idx - b < MAP_WIDTH))
             for a, b in tap_shifts
         ]
     ).astype(np.float32)
-    summed, owned, back = dp_allreduce(
-        local_grad,
-        total,
+    summed, owned, back = fused_step(
+        cotangent[0],
+        jnp.transpose(weight, (1, 2, 0)),
+        inputs[0],
+        jnp.asarray(masks),
         jnp.transpose(weight, (1, 0, 2)),
-        flat_grads,
         jnp.asarray(back_masks),
         tuple(a * MAP_WIDTH + b for a, b in tap_shifts),
         axis_names,

time: 92.3 us -> 91 us (0.986)
  Pallas kernels: 85.3 us -> 82.6 us
  other arithmetic: 1.56 us -> 3.29 us
    pallas_call x2 -> x1, Pallas kernels: 85.3 us -> 82.6 us  [fused_step(): pl.pallas_call(functools.partial(_fused_kernel, axis_names, nz, nc, STREA...]
    div x1, other arithmetic: 1.56 us -> 3.29 us  [on_device(): weight_grad = summed_grad / jnp.float32(lax.axis_size('dp'))]
    unnamed x15 -> x7, local copies, waits for them, and re-layouts: 4.58 us -> 3.83 us
where the time goes in v14:
time: 91 us; the launch traced here: 90.4 us
  Pallas kernels  82.6 us (91%)
  local copies, waits for them, and re-layouts  3.83 us (4%)
  other arithmetic  3.29 us (4%)
    pallas_call x1, Pallas kernels, fused_step(): pl.pallas_call(functools.partial(_fused_kernel, axis_names, nz, nc, STREA...  82.6 us
    unnamed x7, local copies, waits for them, and re-layouts  3.83 us
    div x1, other arithmetic, on_device(): weight_grad = summed_grad / jnp.float32(lax.axis_size('dp'))  3.29 us

profile of v14, /device:TPU:1, one launch (start us, length us, event | category | flops | bytes accessed | tf_op | source)
XLA Modules:
  0.0 90.4 jit_solution(16977224765477829713)
XLA Ops:
  0.6 2.4 %copy.8 = bf16[256,9,256]{0,2,1:T(8,128)(2,1)} copy(bf16[256,9,256]{2,0,1:T(8,128)(2,1)} %param.6) | data formatting | bytes 2359296 | tf_op args[1]
  3.0 82.6 %shard_map.76 = (f32[2304,256]{1,0:T(8,128)}, bf16[32,1152]{1,0:T(8,128)(2,1)}, bf16[256,1152]{1,0:T(8,128)(2,1)}) custom-call(bf16[32,1152]{1,0:T(8,128)(2,1)} %bitcast.14, bf16[9,256,256]{2,1,0:T(8,128)(2,1)} %bitcast.10, bf16[256,1152]{1,0:T(8,128)(2,1)} %bitcast.13, f32[9,1152]{1,0:T(8,128)} %constant.7.clone.mf_ref, bf16[9,256,256]{2,1,0:T(8,128)(2,1)} %bitcast.9, ...), custom_call_target="tpu_custom_call" | custom-call | tf_op jit(solution)/shard_map/pallas_call | solution.py:364
  85.6 0.0 copy-start.1
  85.6 0.0 copy-start
  85.6 3.3 %broadcast_multiply_fusion = f32[2304,256]{1,0:T(8,128)} fusion(f32[2304,256]{1,0:T(8,128)} %get-tuple-element.8), kind=kLoop, calls=%fused_computation | loop fusion | flops 589824 | bytes 4718592 | tf_op jit(solution)/shard_map/div | solution.py:440
  88.9 0.0 copy-done.1
  88.9 0.6 copy.11
  89.6 0.0 copy-done
  89.6 0.8 copy.12
Async XLA Ops:
  85.6 3.3 %copy-start.1 = (bf16[32,1152]{1,0:T(8,128)(2,1)S(1)}, bf16[32,1152]{1,0:T(8,128)(2,1)}, u32[]{:S(2)}) copy-start(bf16[32,1152]{1,0:T(8,128)(2,1)} %get-tuple-element.6) | copy-start | bytes 221188
  85.6 3.9 %copy-start = (bf16[256,1152]{1,0:T(8,128)(2,1)S(1)}, bf16[256,1152]{1,0:T(8,128)(2,1)}, u32[]{:S(2)}) copy-start(bf16[256,1152]{1,0:T(8,128)(2,1)} %get-tuple-element.7) | copy-start | bytes 1769476

commit v15 on v14

--- a/solution.py
+++ b/solution.py
@@ -24,9 +24,24 @@
     ]
 
 
+def start_chan_scatter(axis_names, nc, t_ref, rs_buf, rs_send, rs_recv, owned):
+    me = lax.axis_index("chan")
+    copies = []
+    for k in range(1, nc):
+        peer = (me + k) % nc
+        c = pltpu.make_async_remote_copy(
+            src_ref=t_ref.at[pl.ds(pl.multiple_of(peer * owned, 8), owned)],
+            dst_ref=rs_buf.at[k], send_sem=rs_send.at[k], recv_sem=rs_recv.at[k],
+            device_id=tuple(peer if a == "chan" else lax.axis_index(a) for a in axis_names),
+            device_id_type=pl.DeviceIdType.MESH)
+        c.start()
+        copies.append(c)
+    return copies
+
+
 def _allreduce_kernel(axis_names, nz, nc, streams, shifts, a_ref, t_ref, w_ref, g_ref, m_ref,
                       o_ref, res_ref, ig_ref, rc, s1, f1, rx, rp, rm, ap, am, rs_buf, ig_acc,
-                      send_sems, recv_sems, rs_send, rs_recv, entry_barrier=True):
+                      send_sems, recv_sems, rs_send, rs_recv, entry_barrier=True, rs_started=None):
     rows, cols = a_ref.shape
     half = rows // 2
     chunk = half // nz
@@ -59,15 +74,10 @@
         pl.semaphore_wait(barrier, 4 + nc - 1)
 
     owned = res_ref.shape[0]
-    rs_copies = []
-    for k in range(1, nc):
-        peer = (me + k) % nc
-        c = pltpu.make_async_remote_copy(
-            src_ref=t_ref.at[pl.ds(pl.multiple_of(peer * owned, 8), owned)],
-            dst_ref=rs_buf.at[k], send_sem=rs_send.at[k], recv_sem=rs_recv.at[k],
-            device_id=cdev(peer), device_id_type=MESH)
-        c.start()
-        rs_copies.append(c)
+    if rs_started is None:
+        rs_copies = start_chan_scatter(axis_names, nc, t_ref, rs_buf, rs_send, rs_recv, owned)
+    else:
+        rs_copies = rs_started
 
     sent = []
     counter = [0]
@@ -250,7 +260,7 @@
 
 
 def _allgather_kernel(axis_names, n, shifts, x_ref, w_ref, f_ref, m_ref, o_ref, t_ref, wg_ref,
-                      xs, send_sems, recv_sems, entry_barrier=True):
+                      xs, send_sems, recv_sems, entry_barrier=True, before_wgrad=None):
     rows = x_ref.shape[0]
     MESH = pl.DeviceIdType.MESH
     me = lax.axis_index("chan")
@@ -294,12 +304,14 @@
         pltpu.make_async_remote_copy(
             src_ref=x_ref, dst_ref=o_ref.at[theirs], send_sem=send_sems.at[k],
             recv_sem=recv_sems.at[k], device_id=dev(src), device_id_type=MESH).wait_recv()
+    started = before_wgrad() if before_wgrad is not None else None
     cin = f_ref.shape[0]
     for t in range(len(shifts)):
         wg_ref[pl.ds(t * cin, cin), :] = lax.dot_general(
             xs[t], o_ref[...], (((1,), (1,)), ((), ())), preferred_element_type=jnp.float32)
     for c in copies:
         c.wait_send()
+    return started
 
 
 def chan_allgather(x, axis_names, w, f, masks, shifts):
@@ -341,10 +353,17 @@
     for k in range(1, nc):
         pl.semaphore_signal(barrier, inc=1, device_id=tuple((me + k) % nc if a == "chan" else lax.axis_index(a) for a in axis_names), device_id_type=MESH)
     pl.semaphore_wait(barrier, 4 + nc - 1)
-    _allgather_kernel(axis_names, nc, shifts, x_ref, wf_ref, f_ref, mf_ref, g_s, t_s, wg_s, xs,
-                      ag_send, ag_recv, entry_barrier=False)
+    rs_buf, rs_send, rs_recv = ar_scratch[8], ar_scratch[12], ar_scratch[13]
+
+    def scatter():
+        return start_chan_scatter(axis_names, nc, t_s, rs_buf, rs_send, rs_recv, res_ref.shape[0])
+
+    started = _allgather_kernel(axis_names, nc, shifts, x_ref, wf_ref, f_ref, mf_ref, g_s, t_s,
+                                wg_s, xs, ag_send, ag_recv, entry_barrier=False,
+                                before_wgrad=scatter)
     _allreduce_kernel(axis_names, nz, nc, streams, shifts, wg_s, t_s, wb_ref, g_s, mb_ref,
-                      o_ref, res_ref, ig_ref, *ar_scratch, entry_barrier=False)
+                      o_ref, res_ref, ig_ref, *ar_scratch, entry_barrier=False,
+                      rs_started=started)
 
 
 def fused_step(x, wf, f, mf, wb, mb, shifts, axis_names):

time: 91 us -> 91 us (level)
  no operation moved by 1% of the time
where the time goes in v15:
time: 91 us; the launch traced here: 90.3 us
  Pallas kernels  82.6 us (91%)
  local copies, waits for them, and re-layouts  3.83 us (4%)
  other arithmetic  3.29 us (4%)
    pallas_call x1, Pallas kernels, fused_step(): pl.pallas_call(functools.partial(_fused_kernel, axis_names, nz, nc, STREA...  82.6 us
    unnamed x7, local copies, waits for them, and re-layouts  3.83 us
    div x1, other arithmetic, on_device(): weight_grad = summed_grad / jnp.float32(lax.axis_size('dp'))  3.29 us

profile of v15, /device:TPU:1, one launch (start us, length us, event | category | flops | bytes accessed | tf_op | source)
XLA Modules:
  0.0 90.3 jit_solution(6618180043675532213)
XLA Ops:
  0.6 2.4 %copy.8 = bf16[256,9,256]{0,2,1:T(8,128)(2,1)} copy(bf16[256,9,256]{2,0,1:T(8,128)(2,1)} %param.6) | data formatting | bytes 2359296 | tf_op args[1]
  3.0 82.6 %shard_map.76 = (f32[2304,256]{1,0:T(8,128)}, bf16[32,1152]{1,0:T(8,128)(2,1)}, bf16[256,1152]{1,0:T(8,128)(2,1)}) custom-call(bf16[32,1152]{1,0:T(8,128)(2,1)} %bitcast.14, bf16[9,256,256]{2,1,0:T(8,128)(2,1)} %bitcast.10, bf16[256,1152]{1,0:T(8,128)(2,1)} %bitcast.13, f32[9,1152]{1,0:T(8,128)} %constant.7.clone.mf_ref, bf16[9,256,256]{2,1,0:T(8,128)(2,1)} %bitcast.9, ...), custom_call_target="tpu_custom_call" | custom-call | tf_op jit(solution)/shard_map/pallas_call | solution.py:383
  85.6 0.0 copy-start.1
  85.6 0.0 copy-start
  85.6 3.3 %broadcast_multiply_fusion = f32[2304,256]{1,0:T(8,128)} fusion(f32[2304,256]{1,0:T(8,128)} %get-tuple-element.8), kind=kLoop, calls=%fused_computation | loop fusion | flops 589824 | bytes 4718592 | tf_op jit(solution)/shard_map/div | solution.py:459
  88.9 0.0 copy-done.1
  88.9 0.6 copy.11
  89.5 0.0 copy-done
  89.5 0.8 copy.12
Async XLA Ops:
  85.6 3.3 %copy-start.1 = (bf16[32,1152]{1,0:T(8,128)(2,1)S(1)}, bf16[32,1152]{1,0:T(8,128)(2,1)}, u32[]{:S(2)}) copy-start(bf16[32,1152]{1,0:T(8,128)(2,1)} %get-tuple-element.6) | copy-start | bytes 221188
  85.6 3.9 %copy-start = (bf16[256,1152]{1,0:T(8,128)(2,1)S(1)}, bf16[256,1152]{1,0:T(8,128)(2,1)}, u32[]{:S(2)}) copy-start(bf16[256,1152]{1,0:T(8,128)(2,1)} %get-tuple-element.7) | copy-start | bytes 1769476

commit v16 on v14

--- a/solution.py
+++ b/solution.py
@@ -343,8 +343,12 @@
     pl.semaphore_wait(barrier, 4 + nc - 1)
     _allgather_kernel(axis_names, nc, shifts, x_ref, wf_ref, f_ref, mf_ref, g_s, t_s, wg_s, xs,
                       ag_send, ag_recv, entry_barrier=False)
+    o_s = ar_scratch[-1]
     _allreduce_kernel(axis_names, nz, nc, streams, shifts, wg_s, t_s, wb_ref, g_s, mb_ref,
-                      o_ref, res_ref, ig_ref, *ar_scratch, entry_barrier=False)
+                      o_s, res_ref, ig_ref, *ar_scratch[:-1], entry_barrier=False)
+    cin = o_ref.shape[0]
+    for t in range(o_ref.shape[1]):
+        o_ref[:, t, :] = o_s[pl.ds(t * cin, cin), :] * (1.0 / (4 * nz))
 
 
 def fused_step(x, wf, f, mf, wb, mb, shifts, axis_names):
@@ -364,7 +368,7 @@
     return pl.pallas_call(
         functools.partial(_fused_kernel, axis_names, nz, nc, STREAMS, shifts),
         out_shape=(
-            jax.ShapeDtypeStruct((rows, width), f32),
+            jax.ShapeDtypeStruct((cin, taps, width), f32),
             jax.ShapeDtypeStruct((owned, cols), jnp.bfloat16),
             jax.ShapeDtypeStruct((cin, cols), jnp.bfloat16),
         ),
@@ -391,6 +395,7 @@
             pltpu.SemaphoreType.DMA((n_copies,)),
             pltpu.SemaphoreType.DMA((nc,)),
             pltpu.SemaphoreType.DMA((nc,)),
+            vmem((rows, width), f32),
         ],
         compiler_params=pltpu.CompilerParams(
             collective_id=0, has_side_effects=True, vmem_limit_bytes=56 * 1024 * 1024
@@ -434,10 +439,7 @@
         axis_names,
     )
     result = owned.reshape(1, cout_local, tap_locations)
-    summed_grad = jnp.transpose(
-        summed.reshape(tap_list, input_channels_local, output_channels_total), (1, 0, 2)
-    )
-    weight_grad = summed_grad / jnp.float32(lax.axis_size("dp"))
+    weight_grad = summed
     input_grad = back.reshape(1, input_channels_local, tap_locations)
     return (result, input_grad, weight_grad)
 

time: 91 us -> 94.4 us (1.037)
  local copies, waits for them, and re-layouts: 3.83 us -> 8.86 us
  other arithmetic: 3.29 us -> 0 us
  Pallas kernels: 82.6 us -> 84.2 us
    unnamed x7 -> x8, local copies, waits for them, and re-layouts: 3.83 us -> 8.86 us
    div x1 -> x0, other arithmetic: 3.29 us -> none  [on_device(): weight_grad = summed_grad / jnp.float32(lax.axis_size('dp'))]
    pallas_call x1, Pallas kernels: 82.6 us -> 84.2 us  [fused_step(): pl.pallas_call(functools.partial(_fused_kernel, axis_names, nz, nc, STREA...]
where the time goes in v16:
time: 94.4 us; the launch traced here: 93.8 us
  Pallas kernels  84.2 us (89%)
  local copies, waits for them, and re-layouts  8.86 us (9%)
    pallas_call x1, Pallas kernels, fused_step(): pl.pallas_call(functools.partial(_fused_kernel, axis_names, nz, nc, STREA...  84.2 us
    unnamed x8, local copies, waits for them, and re-layouts  8.86 us

profile of v16, /device:TPU:1, one launch (start us, length us, event | category | flops | bytes accessed | tf_op | source)
XLA Modules:
  0.0 93.8 jit_solution(1722549946025319281)
XLA Ops:
  0.6 2.4 %copy.8 = bf16[256,9,256]{0,2,1:T(8,128)(2,1)} copy(bf16[256,9,256]{2,0,1:T(8,128)(2,1)} %param.6) | data formatting | bytes 2359296 | tf_op args[1]
  3.0 84.2 %shard_map.76 = (f32[256,9,256]{2,1,0:T(8,128)}, bf16[32,1152]{1,0:T(8,128)(2,1)}, bf16[256,1152]{1,0:T(8,128)(2,1)}) custom-call(bf16[32,1152]{1,0:T(8,128)(2,1)} %bitcast.10, bf16[9,256,256]{2,1,0:T(8,128)(2,1)} %bitcast.7, bf16[256,1152]{1,0:T(8,128)(2,1)} %bitcast.9, f32[9,1152]{1,0:T(8,128)} %constant.4.clone.mf_ref, bf16[9,256,256]{2,1,0:T(8,128)(2,1)} %bitcast.6, ...), custom_call_target="tpu_custom_call" | custom-call | tf_op jit(solution)/shard_map/pallas_call | solution.py:368
  87.3 0.0 copy-start.1
  87.3 0.0 copy-start
  87.3 5.0 %copy.9 = f32[256,9,256]{2,0,1:T(8,128)} copy(f32[256,9,256]{2,1,0:T(8,128)} %get-tuple-element.11) | data formatting | bytes 4718592
  92.3 0.0 copy-done.1
  92.3 0.6 copy.12
  92.9 0.0 copy-done
  92.9 0.8 copy.13
Async XLA Ops:
  87.3 5.0 %copy-start.1 = (bf16[32,1152]{1,0:T(8,128)(2,1)S(1)}, bf16[32,1152]{1,0:T(8,128)(2,1)}, u32[]{:S(2)}) copy-start(bf16[32,1152]{1,0:T(8,128)(2,1)} %get-tuple-element.6) | copy-start | bytes 221188
  87.3 5.7 %copy-start = (bf16[256,1152]{1,0:T(8,128)(2,1)S(1)}, bf16[256,1152]{1,0:T(8,128)(2,1)}, u32[]{:S(2)}) copy-start(bf16[256,1152]{1,0:T(8,128)(2,1)} %get-tuple-element.7) | copy-start | bytes 1769476

commit v17 on v14

--- a/solution.py
+++ b/solution.py
@@ -152,6 +152,7 @@
                 src_p = ap.at[s, blk[q]]
                 src_m = am.at[s, blk[q]]
             pending[q] = (remote(src_p, rp.at[s, blk[q]], zr), remote(src_m, rm.at[s, blk[q]], zl))
+        input_grad_tap()
     for q in range(streams):
         pending[q][0].wait_recv()
         pending[q][1].wait_recv()

time: 91 us -> 91 us (level)
  no operation moved by 1% of the time
where the time goes in v17:
time: 91 us; the launch traced here: 90.4 us
  Pallas kernels  82.6 us (91%)
  local copies, waits for them, and re-layouts  3.83 us (4%)
  other arithmetic  3.29 us (4%)
    pallas_call x1, Pallas kernels, fused_step(): pl.pallas_call(functools.partial(_fused_kernel, axis_names, nz, nc, STREA...  82.6 us
    unnamed x7, local copies, waits for them, and re-layouts  3.83 us
    div x1, other arithmetic, on_device(): weight_grad = summed_grad / jnp.float32(lax.axis_size('dp'))  3.29 us

profile of v17, /device:TPU:1, one launch (start us, length us, event | category | flops | bytes accessed | tf_op | source)
XLA Modules:
  0.0 90.4 jit_solution(14325888356948700869)
XLA Ops:
  0.6 2.4 %copy.8 = bf16[256,9,256]{0,2,1:T(8,128)(2,1)} copy(bf16[256,9,256]{2,0,1:T(8,128)(2,1)} %param.6) | data formatting | bytes 2359296 | tf_op args[1]
  3.0 82.6 %shard_map.76 = (f32[2304,256]{1,0:T(8,128)}, bf16[32,1152]{1,0:T(8,128)(2,1)}, bf16[256,1152]{1,0:T(8,128)(2,1)}) custom-call(bf16[32,1152]{1,0:T(8,128)(2,1)} %bitcast.14, bf16[9,256,256]{2,1,0:T(8,128)(2,1)} %bitcast.10, bf16[256,1152]{1,0:T(8,128)(2,1)} %bitcast.13, f32[9,1152]{1,0:T(8,128)} %constant.7.clone.mf_ref, bf16[9,256,256]{2,1,0:T(8,128)(2,1)} %bitcast.9, ...), custom_call_target="tpu_custom_call" | custom-call | tf_op jit(solution)/shard_map/pallas_call | solution.py:365
  85.6 0.0 copy-start.1
  85.6 0.0 copy-start
  85.6 3.3 %broadcast_multiply_fusion = f32[2304,256]{1,0:T(8,128)} fusion(f32[2304,256]{1,0:T(8,128)} %get-tuple-element.8), kind=kLoop, calls=%fused_computation | loop fusion | flops 589824 | bytes 4718592 | tf_op jit(solution)/shard_map/div | solution.py:441
  88.9 0.0 copy-done.1
  88.9 0.6 copy.11
  89.6 0.0 copy-done
  89.6 0.8 copy.12
Async XLA Ops:
  85.6 3.3 %copy-start.1 = (bf16[32,1152]{1,0:T(8,128)(2,1)S(1)}, bf16[32,1152]{1,0:T(8,128)(2,1)}, u32[]{:S(2)}) copy-start(bf16[32,1152]{1,0:T(8,128)(2,1)} %get-tuple-element.6) | copy-start | bytes 221188
  85.6 3.9 %copy-start = (bf16[256,1152]{1,0:T(8,128)(2,1)S(1)}, bf16[256,1152]{1,0:T(8,128)(2,1)}, u32[]{:S(2)}) copy-start(bf16[256,1152]{1,0:T(8,128)(2,1)} %get-tuple-element.7) | copy-start | bytes 1769476

commit v18 on v14

--- a/solution.py
+++ b/solution.py
@@ -97,6 +97,8 @@
             y = y * m_ref[pl.ds(t, 1), :]
             if t == 0:
                 ig_acc[...] = y
+            elif t == len(shifts) - 1:
+                ig_ref[...] = (ig_acc[...] + y).astype(ig_ref.dtype)
             else:
                 ig_acc[...] += y
             done_taps[0] += 1
@@ -202,7 +204,6 @@
     for k in range(1, nc):
         acc = acc + rs_buf[k]
     res_ref[...] = acc.astype(res_ref.dtype)
-    ig_ref[...] = ig_acc[...].astype(ig_ref.dtype)
 
     for c in sent + rs_copies:
         c.wait_send()

time: 91 us -> 91 us (level)
  no operation moved by 1% of the time
where the time goes in v18:
time: 91 us; the launch traced here: 90.3 us
  Pallas kernels  82.6 us (91%)
  local copies, waits for them, and re-layouts  3.83 us (4%)
  other arithmetic  3.29 us (4%)
    pallas_call x1, Pallas kernels, fused_step(): pl.pallas_call(functools.partial(_fused_kernel, axis_names, nz, nc, STREA...  82.6 us
    unnamed x7, local copies, waits for them, and re-layouts  3.83 us
    div x1, other arithmetic, on_device(): weight_grad = summed_grad / jnp.float32(lax.axis_size('dp'))  3.29 us

profile of v18, /device:TPU:1, one launch (start us, length us, event | category | flops | bytes accessed | tf_op | source)
XLA Modules:
  0.0 90.3 jit_solution(7097930686366282540)
XLA Ops:
  0.6 2.4 %copy.8 = bf16[256,9,256]{0,2,1:T(8,128)(2,1)} copy(bf16[256,9,256]{2,0,1:T(8,128)(2,1)} %param.6) | data formatting | bytes 2359296 | tf_op args[1]
  3.0 82.6 %shard_map.76 = (f32[2304,256]{1,0:T(8,128)}, bf16[32,1152]{1,0:T(8,128)(2,1)}, bf16[256,1152]{1,0:T(8,128)(2,1)}) custom-call(bf16[32,1152]{1,0:T(8,128)(2,1)} %bitcast.14, bf16[9,256,256]{2,1,0:T(8,128)(2,1)} %bitcast.10, bf16[256,1152]{1,0:T(8,128)(2,1)} %bitcast.13, f32[9,1152]{1,0:T(8,128)} %constant.7.clone.mf_ref, bf16[9,256,256]{2,1,0:T(8,128)(2,1)} %bitcast.9, ...), custom_call_target="tpu_custom_call" | custom-call | tf_op jit(solution)/shard_map/pallas_call | solution.py:365
  85.6 0.0 copy-start.1
  85.6 0.0 copy-start
  85.6 3.3 %broadcast_multiply_fusion = f32[2304,256]{1,0:T(8,128)} fusion(f32[2304,256]{1,0:T(8,128)} %get-tuple-element.8), kind=kLoop, calls=%fused_computation | loop fusion | flops 589824 | bytes 4718592 | tf_op jit(solution)/shard_map/div | solution.py:441
  88.9 0.0 copy-done.1
  88.9 0.6 copy.11
  89.5 0.0 copy-done
  89.5 0.8 copy.12
Async XLA Ops:
  85.6 3.3 %copy-start.1 = (bf16[32,1152]{1,0:T(8,128)(2,1)S(1)}, bf16[32,1152]{1,0:T(8,128)(2,1)}, u32[]{:S(2)}) copy-start(bf16[32,1152]{1,0:T(8,128)(2,1)} %get-tuple-element.6) | copy-start | bytes 221188
  85.6 3.9 %copy-start = (bf16[256,1152]{1,0:T(8,128)(2,1)S(1)}, bf16[256,1152]{1,0:T(8,128)(2,1)}, u32[]{:S(2)}) copy-start(bf16[256,1152]{1,0:T(8,128)(2,1)} %get-tuple-element.7) | copy-start | bytes 1769476

commit v19 on v18

--- a/solution.py
+++ b/solution.py
@@ -190,6 +190,13 @@
             pending[q] = (remote(o_ref.at[gp, lo], o_ref.at[gp, lo], zr),
                           remote(o_ref.at[gm, hi], o_ref.at[gm, hi], zl))
         input_grad_tap()
+        if s == 0:
+            for c in rs_copies:
+                c.wait_recv()
+            acc = t_ref[pl.ds(pl.multiple_of(me * owned, 8), owned), :]
+            for k in range(1, nc):
+                acc = acc + rs_buf[k]
+            res_ref[...] = acc.astype(res_ref.dtype)
         if s == nz - 2:
             while done_taps[0] < len(shifts):
                 input_grad_tap()
@@ -198,12 +205,6 @@
     for c in to_core:
         c.wait_recv()
 
-    for c in rs_copies:
-        c.wait_recv()
-    acc = t_ref[pl.ds(pl.multiple_of(me * owned, 8), owned), :]
-    for k in range(1, nc):
-        acc = acc + rs_buf[k]
-    res_ref[...] = acc.astype(res_ref.dtype)
 
     for c in sent + rs_copies:
         c.wait_send()

time: 91 us -> 90.9 us (level)
  no operation moved by 1% of the time
where the time goes in v19:
time: 90.9 us; the launch traced here: 90.3 us
  Pallas kernels  82.5 us (91%)
  local copies, waits for them, and re-layouts  3.83 us (4%)
  other arithmetic  3.29 us (4%)
    pallas_call x1, Pallas kernels, fused_step(): pl.pallas_call(functools.partial(_fused_kernel, axis_names, nz, nc, STREA...  82.5 us
    unnamed x7, local copies, waits for them, and re-layouts  3.83 us
    div x1, other arithmetic, on_device(): weight_grad = summed_grad / jnp.float32(lax.axis_size('dp'))  3.29 us

profile of v19, /device:TPU:1, one launch (start us, length us, event | category | flops | bytes accessed | tf_op | source)
XLA Modules:
  0.0 90.3 jit_solution(1759979226459881901)
XLA Ops:
  0.6 2.4 %copy.8 = bf16[256,9,256]{0,2,1:T(8,128)(2,1)} copy(bf16[256,9,256]{2,0,1:T(8,128)(2,1)} %param.6) | data formatting | bytes 2359296 | tf_op args[1]
  3.0 82.5 %shard_map.76 = (f32[2304,256]{1,0:T(8,128)}, bf16[32,1152]{1,0:T(8,128)(2,1)}, bf16[256,1152]{1,0:T(8,128)(2,1)}) custom-call(bf16[32,1152]{1,0:T(8,128)(2,1)} %bitcast.14, bf16[9,256,256]{2,1,0:T(8,128)(2,1)} %bitcast.10, bf16[256,1152]{1,0:T(8,128)(2,1)} %bitcast.13, f32[9,1152]{1,0:T(8,128)} %constant.7.clone.mf_ref, bf16[9,256,256]{2,1,0:T(8,128)(2,1)} %bitcast.9, ...), custom_call_target="tpu_custom_call" | custom-call | tf_op jit(solution)/shard_map/pallas_call | solution.py:366
  85.5 0.0 copy-start.1
  85.5 0.0 copy-start
  85.5 3.3 %broadcast_multiply_fusion = f32[2304,256]{1,0:T(8,128)} fusion(f32[2304,256]{1,0:T(8,128)} %get-tuple-element.8), kind=kLoop, calls=%fused_computation | loop fusion | flops 589824 | bytes 4718592 | tf_op jit(solution)/shard_map/div | solution.py:442
  88.8 0.0 copy-done.1
  88.8 0.6 copy.11
  89.5 0.0 copy-done
  89.5 0.8 copy.12
Async XLA Ops:
  85.5 3.3 %copy-start.1 = (bf16[32,1152]{1,0:T(8,128)(2,1)S(1)}, bf16[32,1152]{1,0:T(8,128)(2,1)}, u32[]{:S(2)}) copy-start(bf16[32,1152]{1,0:T(8,128)(2,1)} %get-tuple-element.6) | copy-start | bytes 221188
  85.5 3.9 %copy-start = (bf16[256,1152]{1,0:T(8,128)(2,1)S(1)}, bf16[256,1152]{1,0:T(8,128)(2,1)}, u32[]{:S(2)}) copy-start(bf16[256,1152]{1,0:T(8,128)(2,1)} %get-tuple-element.7) | copy-start | bytes 1769476
